TPU v7x, 128 devices: a whole 4x4x4 slice. The times are simulated.
128 devices in a mesh: rng: 8 (over z_lo, x), az: 16 (over y, z_hi, core).
Axes of the slice: x: 4, y: 4, z: 4 (z_hi: 2, z_lo: 2; z = z_hi * 2 + z_lo), core: 2. Of those that a mesh axis runs over, the one named last changes fastest.
Arguments:
- echoes: bfloat16 [16, 2, 64, 12288], P('az', None, None, 'rng'), may hold values from -6 to 6
- owner_map: int32 [8], replicated, may hold values from 0 to 15, as said below
- band_start: int32 [48, 16, 8], P('rng', 'az'), may hold values from 0 to 1536, as said below
- interp: bfloat16 [8, 16, 6144, 256], P(None, 'az', 'rng'), may hold values from -0.375 to 0.375
- steer_phase: float32 [8, 64, 16384], P(None, None, 'az'), may hold values from -3.140625 to 3.140625
Outputs:
- focused_image: bfloat16 [6144, 2, 16384], P('rng', None, 'az')
Inputs may be any that keep to these rules, and one draw needn't show every extreme that they name: `owner_map`: the pings' slots are distinct. band_start[g, j, p] lies within 128 of (g mod 6) * 256 + 128.
All inputs are finite; a program needn't handle non-finite values.
Results may differ from a plain program's by a relative error of at most 0.01.
The roundings to bfloat16 on the way count: a program that leaves them out, or rounds other values in their place, can miss the bound.
Values may be sent and summed in bfloat16 or wider, within the bound.
No kernel may reach another device: no remote copies, remote signals or barrier semaphores. Data moves between devices by JAX's collectives and lax.ppermute only.
A program may use at most 128 MiB of HBM per device.

v0:
```python
import jax
import jax.numpy as jnp
from jax import lax
from jax.sharding import PartitionSpec as P

GUARD = 128


def padded_2(block, sides, width):
    for axis, dim in sides:
        count = lax.axis_size(axis)
        forward = [(i, i + 1) for i in range(count - 1)]
        backward = [(target, source) for source, target in forward]
        low = lax.ppermute(
            lax.slice_in_dim(block, block.shape[dim] - width, None, axis=dim), axis, forward
        )
        high = lax.ppermute(lax.slice_in_dim(block, 0, width, axis=dim), axis, backward)
        block = jnp.concatenate([low, block, high], axis=dim)
    return block


def spread(value, axis, source):
    kept = jnp.where(lax.axis_index(axis) == source, value, 0).astype(value.dtype)
    return lax.psum(kept, axis)


def apply_phase(real_part, imag_part, phase, axis_of_cells):
    cosine = jnp.cos(phase)
    sine = jnp.sin(phase)
    return jnp.stack(
        [real_part * cosine + imag_part * sine, imag_part * cosine - real_part * sine],
        axis=axis_of_cells,
    ).astype(jnp.bfloat16)


def focus_lines(lines):
    real_part = lines[:, 0].astype(jnp.float32)
    imag_part = lines[:, 1].astype(jnp.float32)
    cross = jnp.sum(
        real_part[:, :-1] * imag_part[:, 1:] - imag_part[:, :-1] * real_part[:, 1:], axis=0
    )
    cross = jnp.concatenate([cross, jnp.zeros((1,), jnp.float32)])
    power = jnp.sum(real_part * real_part + imag_part * imag_part, axis=0)
    cross, power = lax.psum((cross, power), ("rng", "az"))
    slope = cross / (power + 1e-06)
    phase = jnp.cumsum(slope) - slope
    return apply_phase(real_part, imag_part, phase, 1)


def per_device(echoes, owner_map, band_start, interp, steer_phase):
    hydrophones = echoes.shape[2]
    pings = owner_map.shape[0]
    padded = padded_2(echoes, (("rng", 3),), GUARD)
    windows = jnp.stack([spread(padded[0], "az", owner_map[ping]) for ping in range(pings)])
    starts = band_start[:, 0, :]
    blocks = starts.shape[0]
    kernels = interp[:, 0]
    range_cells = kernels.shape[1]
    band = kernels.shape[2]
    kernels = kernels.reshape(pings, blocks, range_cells // blocks, band)

    def cut(window, start):
        return lax.dynamic_slice_in_dim(window, start, band, 2)

    slabs = jax.vmap(jax.vmap(cut, (None, 0)), (0, 1))(windows, starts)
    focused = jnp.einsum("pbik,pbchk->bipch", kernels, slabs, preferred_element_type=jnp.float32)
    focused = focused.astype(jnp.bfloat16).reshape(range_cells, pings * 2 * hydrophones)
    scale = 1.0 / jnp.sqrt(jnp.float32(pings * hydrophones))
    steer_re = (jnp.cos(steer_phase) * scale).astype(jnp.bfloat16)
    steer_im = (jnp.sin(steer_phase) * scale).astype(jnp.bfloat16)
    azimuth_cells = steer_phase.shape[2]
    upper = jnp.stack([steer_re, steer_im], axis=2)
    lower = jnp.stack([-steer_im, steer_re], axis=2)
    steering = jnp.stack([upper, lower], axis=1).reshape(pings * 2 * hydrophones, 2 * azimuth_cells)
    image = jnp.dot(focused, steering, preferred_element_type=jnp.float32).astype(jnp.bfloat16)
    image = image.reshape(range_cells, 2, azimuth_cells)
    lines = lax.all_to_all(image, "az", split_axis=0, concat_axis=2, tiled=True)
    lines = focus_lines(focus_lines(lines))
    return lax.all_to_all(lines, "az", split_axis=2, concat_axis=0, tiled=True)


def solution(mesh):
    in_specs = (
        P("az", None, None, "rng"),
        P(),
        P("rng", "az", None),
        P(None, "az", "rng", None),
        P(None, None, "az"),
    )
    out_specs = P("rng", None, "az")
    return jax.shard_map(
        per_device, mesh=mesh, in_specs=in_specs, out_specs=out_specs, check_vma=False
    )
```

profile of v0, /device:TPU:6, one launch (start us, length us, event | category | flops | bytes accessed | tf_op | source)
XLA Modules:
  0.0 739.3 jit_solution(18338887578274943396)
XLA Ops:
  6.5 3.1 copy.46
  10.6 3.7 collective-permute-start
  14.3 2.1 collective-permute-start.1
  16.4 1.6 fusion.41
  23.1 7.2 broadcast_select_fusion
  30.3 5.8 broadcast_select_fusion.1
  37.0 8.0 %negate_bitcast_fusion = bf16[8,64,1,1024]{3,1,0,2:T(8,128)(2,1)S(1)} fusion(f32[8,64,1024]{2,1,0:T(8,128)} %param.9), kind=kLoop, calls=%fused_computation.54 | loop fusion | flops 2621440 | bytes 3145728 | tf_op jit(solution)/shard_map/stack | solution.py:73
  45.0 7.6 %fusion.28 = (bf16[8,64,1,1024]{3,1,0,2:T(8,128)(2,1)S(1)}, bf16[8,64,1,1024]{3,1,0,2:T(8,128)(2,1)S(1)}) fusion(f32[8,64,1024]{2,1,0:T(8,128)S(1)} %copy-done.4), kind=kLoop, calls=%fused_computation.56 | loop fusion | flops 2097152 | bytes 4194304 | tf_op jit(solution)/shard_map/stack | solution.py:72
  52.9 2.3 pad_maximum_fusion
  55.2 8.6 %copy.53 = bf16[8,2,64,2,1024]{4,3,2,1,0:T(2,128)(2,1)} copy(bf16[8,2,64,2,1024]{4,2,0,3,1:T(8,128)(2,1)} %pad_maximum_fusion) | data formatting | bytes 8388608 | tf_op jit(solution)/shard_map/stack | solution.py:74
  63.8 5.6 copy.74
  69.5 149.8 %all-reduce.12.cloned.1.call-done = (bf16[1,2,64,1792]{2,1,0,3:T(2,128)(2,1)}, bf16[1,2,64,1792]{2,1,0,3:T(2,128)(2,1)}, bf16[1,2,64,1792]{2,1,0,3:T(2,128)(2,1)...) async-done(((bf16[1,2,64,1792]{2,1,0,3:T(2,128)(2,1)}, ...) | async-done | bytes 3670032 | tf_op jit(solution)/shard_map/psum | solution.py:24
  219.3 2.6 constant_dynamic-update-slice_fusion.7
  222.0 2.6 constant_dynamic-update-slice_fusion.6
  230.5 1.7 constant_dynamic-update-slice_fusion.1
  233.7 21.9 %gather_fusion = bf16[48,2,64,256]{2,1,3,0:T(2,128)(2,1)} fusion(bf16[8,2,64,1792]{2,1,0,3:T(2,128)(2,1)} %constant_dynamic-update-slice_fusion, s32[48]{0:T(128)S(1)} %reshape.128), kind=kCustom, calls=%fused_computation | custom fusion | bytes 6292224 | tf_op jit(solution)/shard_map/vmap(vmap())/gather | solution.py:63
  255.6 4.7 fusion.22
  261.6 4.9 convolution_convert_fusion
  266.6 4.8 reshape.111
  271.3 47.2 %all_to_all.36 = bf16[768,2,1024]{2,1,0:T(2,128)(2,1)S(1)} all-to-all(bf16[768,2,1024]{2,1,0:T(2,128)(2,1)S(1)} %reshape.111), channel_id=1, replica_groups=mesh['rng'=8,'az'=16] {'az'}, dimensions={0} | all-to-all | bytes 6291456 | tf_op jit(solution)/shard_map/all_to_all | solution.py:77
  321.9 1.7 fusion.13
  324.4 138.2 %all-reduce.10.cloned.1.call-done = (f32[16384]{0:T(1024)}, f32[16384]{0:T(1024)}) async-done(((f32[16384]{0:T(1024)}, f32[16384]{0:T(1024)}), (f32[16384]{0:T(1024)}, f32[16384]{0:T(1024)})) %all-reduce.10.cloned.1.call-update) | async-done | bytes 131088 | tf_op jit(solution)/shard_map/psum | solution.py:44
  465.4 2.0 add_reduce_fusion
  469.1 1.7 fusion.11
  471.5 140.3 %all-reduce.8.cloned.1.call-done = (f32[16384]{0:T(1024)}, f32[16384]{0:T(1024)}) async-done(((f32[16384]{0:T(1024)}, f32[16384]{0:T(1024)}), (f32[16384]{0:T(1024)}, f32[16384]{0:T(1024)})) %all-reduce.8.cloned.1.call-update) | async-done | bytes 131088 | tf_op jit(solution)/shard_map/psum | solution.py:44
  614.6 2.8 fusion.7
  617.7 13.0 %copy.62 = bf16[48,2,16384]{0,1,2:T(2,128)(2,1)} copy(bf16[48,2,16384]{2,0,1:T(8,128)(2,1)S(1)} %pad_maximum_fusion.1) | data formatting | bytes 6291456 | tf_op jit(solution)/shard_map/stack | solution.py:30
  630.7 15.4 %reshape.142 = bf16[16,2,49152]{2,1,0:T(2,128)(2,1)S(1)} reshape(bf16[16384,2,48]{2,1,0:T(2,128)(2,1)} %bitcast.91) | data formatting | bytes 6291456
  646.0 45.2 %all_to_all.37 = bf16[16,2,49152]{2,1,0:T(2,128)(2,1)} all-to-all(bf16[16,2,49152]{2,1,0:T(2,128)(2,1)S(1)} %reshape.142), channel_id=1, replica_groups=mesh['rng'=8,'az'=16] {'az'}, dimensions={0} | all-to-all | bytes 6291456 | tf_op jit(solution)/shard_map/all_to_all | solution.py:79
  691.3 14.4 %reshape.143 = bf16[16384,2,48]{2,1,0:T(2,128)(2,1)} reshape(bf16[16,2,49152]{2,1,0:T(2,128)(2,1)} %all_to_all.37) | data formatting | bytes 6291456
  705.7 19.9 %copy.70 = bf16[48,2,16,1024]{3,0,2,1:T(8,128)(2,1)} copy(bf16[48,2,16,1024]{0,1,3,2:T(2,128)(2,1)} %bitcast.92) | data formatting | bytes 6291456 | tf_op jit(solution)/shard_map/all_to_all | solution.py:79
  725.6 6.9 copy.65
  (74 shorter events, 23.2 us)
Async XLA Ops:
  6.5 249.1 %copy-start = (bf16[8,1,768,256]{3,2,1,0:T(8,128)(2,1)S(1)}, bf16[8,1,768,256]{3,2,1,0:T(8,128)(2,1)}, u32[]{:S(2)}) copy-start(bf16[8,1,768,256]{3,2,1,0:T(8,128)(2,1)} %param.8) | copy-start | bytes 9437188
  6.5 212.8 %all-reduce.12.cloned.1.call-start = ((), (), s32[]{:S(2)}) async-start(), calls=%async_computation.4 | async-start | bytes 14680064 | tf_op jit(solution)/shard_map/psum | solution.py:24
  10.6 12.5 %collective-permute-start = (bf16[1,2,64,128]{2,1,0,3:T(2,128)(2,1)S(1)}, bf16[1,2,64,128]{2,1,0,3:T(2,128)(2,1)S(1)}, u32[]{:S(2)}, u32[]{:S(2)}) collective-permute-start(bf16[1,2,64,128]{2,1,0,3:T(2,128)(2,1)S(1)} %get-tuple-element.37), channel_id=1, source_target_pairs={{0,16},{16,32},{32,48},{48,64},{64,80},{80,96},{96,112},{1,17},{17... | collective-permute-start | bytes 98312 | tf_op jit(solution)/shard_map/ppermute | solution.py:14
  14.3 8.8 %collective-permute-start.1 = (bf16[1,2,64,128]{2,1,0,3:T(2,128)(2,1)S(1)}, bf16[1,2,64,128]{2,1,0,3:T(2,128)(2,1)S(1)}, u32[]{:S(2)}, u32[]{:S(2)}) collective-permute-start(bf16[1,2,64,128]{2,1,0,3:T(2,128)(2,1)S(1)} %get-tuple-element.38), channel_id=1, source_target_pairs={{16,0},{32,16},{48,32},{64,48},{80,64},{96,80},{112,96},{17,1},{33... | collective-permute-start | bytes 98312 | tf_op jit(solution)/shard_map/ppermute | solution.py:17
  36.1 0.7 copy-start.12
  36.1 426.4 %all-reduce.10.cloned.1.call-start = ((), (), s32[]{:S(2)}) async-start(), calls=%async_computation.3 | async-start | bytes 262144 | tf_op jit(solution)/shard_map/psum | solution.py:44
  37.0 8.0 %copy-start.4 = (f32[8,64,1024]{2,1,0:T(8,128)S(1)}, f32[8,64,1024]{2,1,0:T(8,128)}, u32[]{:S(2)}) copy-start(f32[8,64,1024]{2,1,0:T(8,128)} %param.9) | copy-start | bytes 6291460
  219.3 5.2 copy-start.11
  219.3 6.7 copy-start.10
  222.0 5.6 copy-start.9
  224.5 4.5 copy-start.8
  226.0 4.4 copy-start.7
  227.5 4.6 copy-start.6
  255.6 6.0 copy-start.5
  324.3 287.5 %all-reduce.8.cloned.1.call-start = ((), (), s32[]{:S(2)}) async-start(), calls=%async_computation.2 | async-start | bytes 262144 | tf_op jit(solution)/shard_map/psum | solution.py:44
  467.4 1.2 copy-start.2
  467.4 1.7 copy-start.3
  725.6 6.9 copy-start.1
Sparse Core Ops, SparseCore 0:
  36.2 183.0 all-reduce.11
  324.4 138.0 all-reduce.9
  471.6 140.1 all-reduce.7
where the time goes:
time: 747 us; the launch traced here: 739 us
  waiting for transfers between devices  428 us (57%)
  local copies, waits for them, and re-layouts  136 us (18%)
  blocking collectives  92.4 us (12%)
  other arithmetic  48.3 us (6%)
  between operations  18.6 us (2%)
  matrix products  9.65 us (1%)
    psum x2, waiting for transfers between devices, focus_lines(): cross, power = lax.psum((cross, power), ('rng', 'az'))  278 us
    psum x1, waiting for transfers between devices, spread(): return lax.psum(kept, axis)  150 us
    unnamed x37, local copies, waits for them, and re-layouts  52.9 us
    all_to_all x1, blocking collectives, per_device(): lines = lax.all_to_all(image, 'az', split_axis=0, concat_axis=2, tiled=True)  47.2 us
    all_to_all x1, blocking collectives, per_device(): return lax.all_to_all(lines, 'az', split_axis=2, concat_axis=0, tiled=True)  45.2 us
    all_to_all x2, local copies, waits for them, and re-layouts, per_device(): return lax.all_to_all(lines, 'az', split_axis=2, concat_axis=0, tiled=True)  26.9 us
    gather x3, local copies, waits for them, and re-layouts, cut(): return lax.dynamic_slice_in_dim(window, start, band, 2)  22.1 us
  transfers between devices with their start and end apart: 5, of which 3 were waited for; matrix products, arithmetic and copies ran while one was open for 5% of the time, Pallas kernels for 0%

commit v1 on v0

v1 whole, which is shorter than its diff:
```python
import jax
import jax.numpy as jnp
from jax import lax
from jax.experimental import pallas as pl
from jax.experimental.pallas import tpu as pltpu
from jax.sharding import PartitionSpec as P

GUARD = 128
LANES = 128
N_Y, N_ZH, N_CORE = 4, 2, 2

PIO2_HI = 1.5707964
PIO2_LO = -4.371139e-8


def sine_cosine(x):
    turns = jnp.round(x * 0.63661975)
    r = (x - turns * PIO2_HI) - turns * PIO2_LO
    r2 = r * r
    sine = r + r * r2 * (-1.6666654611e-1 + r2 * (8.3321608736e-3 + r2 * -1.9515295891e-4))
    cosine = 1.0 - 0.5 * r2 + r2 * r2 * (
        4.166664568298827e-2 + r2 * (-1.388731625493765e-3 + r2 * 2.443315711809948e-5)
    )
    quadrant = turns.astype(jnp.int32)
    odd = (quadrant & 1) == 1
    first = jnp.where(odd, cosine, sine)
    second = jnp.where(odd, sine, cosine)
    sine = jnp.where((quadrant & 2) == 2, -first, first)
    cosine = jnp.where(((quadrant + 1) & 2) == 2, -second, second)
    return sine, cosine


def steering_kernel(scale, phase_ref, re_ref, im_ref):
    hydrophones = phase_ref.shape[1]
    sine, cosine = sine_cosine(phase_ref[0])
    steer_re = (cosine * scale).astype(jnp.bfloat16)
    steer_im = (sine * scale).astype(jnp.bfloat16)
    re_ref[:hydrophones] = steer_re
    re_ref[hydrophones:] = -steer_im
    im_ref[:hydrophones] = steer_im
    im_ref[hydrophones:] = steer_re


def steering(phases):
    pings, hydrophones, cells = phases.shape
    scale = float(1.0 / (pings * hydrophones) ** 0.5)
    block = pl.BlockSpec((2 * hydrophones, cells), lambda p: (p, 0))
    out = jax.ShapeDtypeStruct((pings * 2 * hydrophones, cells), jnp.bfloat16)
    return pl.pallas_call(
        lambda *refs: steering_kernel(scale, *refs),
        grid=(pings,),
        in_specs=[pl.BlockSpec((1, hydrophones, cells), lambda p: (p, 0, 0))],
        out_specs=[block, block],
        out_shape=[out, out],
        name="steering",
    )(phases)


def focus_kernel(n_slots, band, rel_ref, start_ref, *refs):
    slots = refs[:n_slots]
    interp_ref, re_ref, im_ref, out_ref, edge_ref, window, sems = refs[n_slots:]
    pings = window.shape[0]
    rows = window.shape[1]
    width = slots[0].shape[1]
    blocks = start_ref.shape[0] // pings
    cells = interp_ref.shape[1] // blocks
    p = pl.program_id(0)

    @pl.when(p == 0)
    def _():
        for ping in range(pings):
            for s in range(n_slots):

                @pl.when(rel_ref[ping] == s)
                def _():
                    pltpu.make_async_copy(
                        slots[s], window.at[ping, :, pl.ds(0, width)], sems.at[ping]
                    ).start()

    pltpu.make_async_copy(slots[0], window.at[p, :, pl.ds(0, width)], sems.at[p]).wait()
    for b in range(blocks):
        start = start_ref[b * pings + p]
        aligned = pl.multiple_of((start // LANES) * LANES, LANES)
        wide = window[p, :, pl.ds(aligned, band + LANES)].astype(jnp.float32)
        shift = (band + LANES) - (start - aligned)
        slab = pltpu.roll(wide, shift, 1)[:, :band].astype(jnp.bfloat16)
        kernel = interp_ref[0, b * cells : (b + 1) * cells, :]
        got = lax.dot_general(
            kernel, slab, (((1,), (1,)), ((), ())), preferred_element_type=jnp.float32
        )
        out_ref[b * cells : (b + 1) * cells, pl.ds(pl.multiple_of(p * rows, LANES), rows)] = (
            got.astype(jnp.bfloat16)
        )

    @pl.when(p == pings - 1)
    def _():
        n = re_ref.shape[1]
        focused = out_ref[...]

        def line(column_ref, low, row):
            part = column_ref[:, low : low + LANES]
            got = lax.dot_general(
                part, focused, (((0,), (1,)), ((), ())), preferred_element_type=jnp.float32
            )
            return got[row : row + 1, :].astype(jnp.bfloat16).astype(jnp.float32)

        edge_ref[0:1, :] = line(re_ref, 0, 0)
        edge_ref[1:2, :] = line(im_ref, 0, 0)
        edge_ref[2:3, :] = line(re_ref, n - LANES, LANES - 1)
        edge_ref[3:4, :] = line(im_ref, n - LANES, LANES - 1)


def focus(slots, rel, starts, interp, steer_re, steer_im):
    pings, range_cells, band = interp.shape
    rows, width = slots[0].shape
    any_spec = pl.BlockSpec(memory_space=pl.ANY)
    whole = pl.BlockSpec(steer_re.shape, lambda p, *_: (0, 0))
    kernel = lambda *refs: focus_kernel(len(slots), band, *refs)
    return pl.pallas_call(
        kernel,
        grid_spec=pltpu.PrefetchScalarGridSpec(
            num_scalar_prefetch=2,
            grid=(pings,),
            in_specs=[any_spec] * len(slots)
            + [pl.BlockSpec((1, range_cells, band), lambda p, *_: (p, 0, 0)), whole, whole],
            out_specs=[
                pl.BlockSpec((range_cells, pings * rows), lambda p, *_: (0, 0)),
                pl.BlockSpec((8, range_cells), lambda p, *_: (0, 0)),
            ],
            scratch_shapes=[
                pltpu.VMEM((pings, rows, width + LANES), jnp.bfloat16),
                pltpu.SemaphoreType.DMA((pings,)),
            ],
        ),
        out_shape=[
            jax.ShapeDtypeStruct((range_cells, pings * rows), jnp.bfloat16),
            jax.ShapeDtypeStruct((8, range_cells), jnp.float32),
        ],
        name="focus",
    )(rel, starts, *slots, interp, steer_re, steer_im)


def image_kernel(focused_ref, re_ref, im_ref, out_re, out_im, stats_ref):
    tile = 256
    rows, cells = out_re.shape
    focused = focused_ref[...]
    for n in range(cells // tile):
        part = slice(n * tile, (n + 1) * tile)
        out_re[:, part] = jnp.dot(
            focused, re_ref[:, part], preferred_element_type=jnp.float32
        ).astype(jnp.bfloat16)
        out_im[:, part] = jnp.dot(
            focused, im_ref[:, part], preferred_element_type=jnp.float32
        ).astype(jnp.bfloat16)
    step = 16
    half = 512

    def fold(x):
        return x[:8] + x[8:]

    stats_ref[...] = jnp.zeros_like(stats_ref)
    for low in range(0, cells, half):
        last = low + half == cells
        span = half if last else half + LANES

        def body(i, carry):
            power, real, imag = carry
            here = pl.ds(pl.multiple_of(i * step, step), step)
            a = out_re[here, low : low + span].astype(jnp.float32)
            b = out_im[here, low : low + span].astype(jnp.float32)
            na = pltpu.roll(a, span - 1, 1)[:, :half]
            nb = pltpu.roll(b, span - 1, 1)[:, :half]
            a, b = a[:, :half], b[:, :half]
            power = power + fold(a * a + b * b)
            real = real + fold(a * na + b * nb)
            imag = imag + fold(a * nb - b * na)
            return power, real, imag

        zero = jnp.zeros((8, half), jnp.float32)
        sums = lax.fori_loop(0, rows // step, body, (zero, zero, zero))
        for k, value in enumerate(sums):
            stats_ref[k : k + 1, low : low + half] = jnp.sum(value, axis=0, keepdims=True)


def image(focused, steer_re, steer_im):
    rows, cells = focused.shape[0], steer_re.shape[1]
    out = jax.ShapeDtypeStruct((rows, cells), jnp.bfloat16)
    return pl.pallas_call(
        image_kernel,
        out_shape=[out, out, jax.ShapeDtypeStruct((8, cells), jnp.float32)],
        name="image",
    )(focused, steer_re, steer_im)


def apply_kernel(re_ref, im_ref, cos_ref, sin_ref, out_ref, scratch):
    rows = re_ref.shape[0]
    tiles = re_ref.shape[1] // LANES
    for t in range(tiles):
        part = slice(t * LANES, (t + 1) * LANES)
        a = re_ref[:, part].astype(jnp.float32)
        b = im_ref[:, part].astype(jnp.float32)
        cosine = cos_ref[:, part]
        sine = sin_ref[:, part]
        scratch[pl.ds(2 * t, rows, stride=2 * tiles), :] = a * cosine + b * sine
        scratch[pl.ds(2 * t + 1, rows, stride=2 * tiles), :] = b * cosine - a * sine
    out_ref[...] = scratch[...].astype(jnp.bfloat16)


def apply(real, imag, cosine, sine):
    rows, cells = real.shape
    tiles = cells // LANES
    step = 64
    block = pl.BlockSpec((step, cells), lambda i: (i, 0))
    table = pl.BlockSpec((1, cells), lambda i: (0, 0))
    out = pl.pallas_call(
        apply_kernel,
        grid=(rows // step,),
        in_specs=[block, block, table, table],
        out_specs=pl.BlockSpec((step * 2 * tiles, LANES), lambda i: (i, 0)),
        out_shape=jax.ShapeDtypeStruct((rows * 2 * tiles, LANES), jnp.bfloat16),
        scratch_shapes=[pltpu.VMEM((step * 2 * tiles, LANES), jnp.float32)],
        name="apply",
    )(real, imag, cosine, sine)
    out = out.reshape(rows, tiles, 2, LANES).transpose(0, 2, 1, 3)
    return out.reshape(rows, 2, cells)


def send(x, axis, move):
    n = lax.axis_size(axis)
    return lax.ppermute(x, axis, [(i, move(i)) for i in range(n)])


def padded(block):
    n = lax.axis_size("rng")
    forward = [(i, i + 1) for i in range(n - 1)]
    backward = [(i + 1, i) for i in range(n - 1)]
    width = block.shape[1]
    low = lax.ppermute(block[:, width - GUARD :], "rng", forward)
    high = lax.ppermute(block[:, :GUARD], "rng", backward)
    return jnp.concatenate([low, block, high], axis=1)


def spread(own):
    up = lambda i: (i + 4) % 16
    down = lambda i: (i - 4) % 16
    across = lambda i: i ^ 2
    other = send(own, "az", across)
    slots = {(0, 0): own, (0, 1): other}
    for z, x in ((0, own), (1, other)):
        slots[3, z] = send(x, "az", up)
        slots[1, z] = send(x, "az", down)
    slots[2, 0] = send(slots[3, 0], "az", up)
    slots[2, 1] = send(slots[1, 1], "az", down)
    out = []
    for y in range(N_Y):
        for z in range(N_ZH):
            out.append(slots[y, z])
            out.append(send(slots[y, z], "az", lambda i: i ^ 1))
    return out


def per_device(echoes, owner_map, band_start, interp, steer_phase):
    hydrophones = echoes.shape[2]
    samples = echoes.shape[3]
    slots = spread(padded(echoes[0].reshape(2 * hydrophones, samples)))
    me = lax.axis_index("az")
    rel = (
        (owner_map // 4 - me // 4) % N_Y * 4
        + ((owner_map // 2) % 2 ^ (me // 2) % 2) * 2
        + (owner_map % 2 ^ me % 2)
    ).astype(jnp.int32)
    steer_re, steer_im = steering(steer_phase)
    focused, edges = focus(
        slots, rel, band_start.reshape(-1), interp[:, 0], steer_re, steer_im
    )
    n_az = lax.axis_size("az")
    halo = lax.ppermute(edges[:2], "az", [(i + 1, i) for i in range(n_az - 1)])
    real, imag, stats = image(focused, steer_re, steer_im)
    last_re, last_im = edges[2], edges[3]
    seam_re = jnp.sum(last_re * halo[0] + last_im * halo[1])
    seam_im = jnp.sum(last_re * halo[1] - last_im * halo[0])
    cells = real.shape[1]
    seam = jnp.stack([jnp.float32(0), seam_re, seam_im])[:, None]
    at_seam = (jnp.arange(cells) == cells - 1)[None, :]
    at_sum = (jnp.arange(3) == 0)[:, None]
    stats = jnp.where(at_seam & ~at_sum, seam, stats[:3])
    for mask in (1, 3, 4):
        stats = stats + send(stats, "rng", lambda i: i ^ mask)
    power, cross_re, cross_im = stats[0] + 1e-06, stats[1], stats[2]
    first = cross_im / power
    second = (cross_im * jnp.cos(first) - cross_re * jnp.sin(first)) / power
    slope = first + second
    summed = jnp.cumsum(slope)
    total = summed[-1:]
    before = jnp.zeros_like(total)
    for mask, bit in ((1, 1), (2, 2), (4, 4), (12, 8)):
        got = send(total, "az", lambda i: i ^ mask)
        before = before + jnp.where((me & bit) != 0, got, 0.0)
        total = total + got
    phase = (before + (summed - slope))[None, :]
    return apply(real, imag, jnp.cos(phase), jnp.sin(phase))


def solution(mesh):
    in_specs = (
        P("az", None, None, "rng"),
        P(),
        P("rng", "az", None),
        P(None, "az", "rng", None),
        P(None, None, "az"),
    )
    out_specs = P("rng", None, "az")
    return jax.shard_map(
        per_device, mesh=mesh, in_specs=in_specs, out_specs=out_specs, check_vma=False
    )
```

time: 747 us -> 144 us (0.19)
  waiting for transfers between devices: 428 us -> 45.1 us
  local copies, waits for them, and re-layouts: 136 us -> 3.87 us
  blocking collectives: 92.4 us -> 0 us
  Pallas kernels: 0 us -> 46.3 us
  other arithmetic: 48.3 us -> 7.65 us
  starting transfers between devices: 6.1 us -> 34.3 us
  between operations: 18.6 us -> 5.46 us
  matrix products: 9.65 us -> 0 us
    psum x3 -> x0, waiting for transfers between devices: 428 us -> none  [the longest x2 278 us: focus_lines(): cross, power = lax.psum((cross, power), ('rng', 'az'))]
    all_to_all x2 -> x0, blocking collectives: 92.4 us -> none  [the longest x1 47.2 us: per_device(): lines = lax.all_to_all(image, 'az', split_axis=0, concat_axis=2, tiled=True)]
    unnamed x37 -> x22, local copies, waits for them, and re-layouts: 52.9 us -> 0.21 us
    pallas_call x0 -> x4, Pallas kernels: none -> 46.3 us  [the longest x1 16.3 us: image(): pl.pallas_call(image_kernel, out_shape=[out, out, jax.ShapeDtypeStruct((8...]
    ppermute x2 -> x25, waiting for transfers between devices: 0.01 us -> 45.1 us  [the longest x22 39.3 us: send(): return lax.ppermute(x, axis, [(i, move(i)) for i in range(n)])]
    ppermute x2 -> x25, starting transfers between devices: 5.84 us -> 34.3 us  [the longest x22 27.2 us: send(): return lax.ppermute(x, axis, [(i, move(i)) for i in range(n)])]
    all_to_all x4 -> x0, local copies, waits for them, and re-layouts: 28.3 us -> none  [the longest x2 26.9 us: per_device(): return lax.all_to_all(lines, 'az', split_axis=2, concat_axis=0, tiled=True)]
    another operation x10 -> x1, local copies, waits for them, and re-layouts: 23.7 us -> 0.12 us  [the longest x1 13 us: apply_phase(): jnp.stack([real_part * cosine + imag_part * sine, imag_part * cosine - re...]
  transfers between devices with their start and end apart: 5 -> 25, of which waited for: 3 -> 11; matrix products, arithmetic and copies ran while one was open for 5% -> 1% of each run, Pallas kernels for 0% -> 17%
where the time goes in v1:
time: 144 us; the launch traced here: 143 us
  Pallas kernels  46.3 us (32%)
  waiting for transfers between devices  45.1 us (31%)
  starting transfers between devices  34.3 us (24%)
  other arithmetic  7.65 us (5%)
  between operations  5.46 us (4%)
  local copies, waits for them, and re-layouts  3.87 us (3%)
    ppermute x22, waiting for transfers between devices, send(): return lax.ppermute(x, axis, [(i, move(i)) for i in range(n)])  39.3 us
    ppermute x22, starting transfers between devices, send(): return lax.ppermute(x, axis, [(i, move(i)) for i in range(n)])  27.2 us
    pallas_call x1, Pallas kernels, image(): pl.pallas_call(image_kernel, out_shape=[out, out, jax.ShapeDtypeStruct((8...  16.3 us
    pallas_call x1, Pallas kernels, focus(): pl.pallas_call(kernel, grid_spec=pltpu.PrefetchScalarGridSpec(num_scalar_...  13.1 us
    pallas_call x1, Pallas kernels, apply(): pl.pallas_call(apply_kernel, grid=(rows // step,), in_specs=[block, block...  9.55 us
    pallas_call x1, Pallas kernels, steering(): pl.pallas_call(lambda *refs: steering_kernel(scale, *refs), grid=(pings,)...  7.35 us
    ppermute x1, waiting for transfers between devices, padded(): high = lax.ppermute(block[:, :GUARD], 'rng', backward)  5.8 us
    ppermute x1, starting transfers between devices, padded(): low = lax.ppermute(block[:, width - GUARD:], 'rng', forward)  3.73 us
  transfers between devices with their start and end apart: 25, of which 11 were waited for; matrix products, arithmetic and copies ran while one was open for 1% of the time, Pallas kernels for 17%

profile of v1, /device:TPU:6, one launch (start us, length us, event | category | flops | bytes accessed | tf_op | source)
XLA Modules:
  0.0 142.7 jit_solution(9515810717136445400)
XLA Ops:
  0.8 3.7 %collective-permute-start = (bf16[128,128]{1,0:T(8,128)(2,1)S(1)}, bf16[128,128]{1,0:T(8,128)(2,1)S(1)}, u32[]{:S(2)}, u32[]{:S(2)}) collective-permute-start(bf16[128,128]{1,0:T(8,128)(2,1)S(1)} %get-tuple-element.23), channel_id=1, source_target_pairs={{0,16},{16,32},{32,48},{48,64},{64,80},{80,96},{96,112},{1,17},{17... | collective-permute-start | bytes 98312 | tf_op jit(solution)/shard_map/ppermute | solution.py:238
  4.5 2.1 %collective-permute-start.1 = (bf16[128,128]{1,0:T(8,128)(2,1)S(1)}, bf16[128,128]{1,0:T(8,128)(2,1)S(1)}, u32[]{:S(2)}, u32[]{:S(2)}) collective-permute-start(bf16[128,128]{1,0:T(8,128)(2,1)S(1)} %get-tuple-element.24), channel_id=1, source_target_pairs={{16,0},{32,16},{48,32},{64,48},{80,64},{96,80},{112,96},{17,1},{33... | collective-permute-start | bytes 98312 | tf_op jit(solution)/shard_map/ppermute | solution.py:239
  6.7 5.8 %collective-permute-done.1 = bf16[128,128]{1,0:T(8,128)(2,1)S(1)} collective-permute-done((bf16[128,128]{1,0:T(8,128)(2,1)S(1)}, bf16[128,128]{1,0:T(8,128)(2,1)S(1)}, u32[]{:S(2)}, u32[]{:S(2)}) %collective-permute-start.1) | collective-permute-done | bytes 32800 | tf_op jit(solution)/shard_map/ppermute | solution.py:239
  12.5 1.0 pad_maximum_fusion.refs_2_
  13.5 3.8 %collective-permute-start.3 = (bf16[128,1792]{1,0:T(8,128)(2,1)S(1)}, bf16[128,1792]{1,0:T(8,128)(2,1)S(1)}, u32[]{:S(2)}, u32[]{:S(2)}) collective-permute-start(bf16[128,1792]{1,0:T(8,128)(2,1)S(1)} %pad_maximum_fusion.refs_2_), channel_id=1, source_target_pairs={{0,2},{1,3},{2,0},{3,1},{4,6},{5,7},{6,4},{7,5},{8,10},{9,11},{10,... | collective-permute-start | bytes 1376264 | tf_op jit(solution)/shard_map/ppermute | solution.py:230
  17.3 1.6 %collective-permute-start.9 = (bf16[128,1792]{1,0:T(8,128)(2,1)S(1)}, bf16[128,1792]{1,0:T(8,128)(2,1)S(1)}, u32[]{:S(2)}, u32[]{:S(2)}) collective-permute-start(bf16[128,1792]{1,0:T(8,128)(2,1)S(1)} %pad_maximum_fusion.refs_2_), channel_id=1, source_target_pairs={{0,4},{1,5},{2,6},{3,7},{4,8},{5,9},{6,10},{7,11},{8,12},{9,13},{1... | collective-permute-start | bytes 1376264 | tf_op jit(solution)/shard_map/ppermute | solution.py:230
  18.9 1.7 %collective-permute-start.5 = (bf16[128,1792]{1,0:T(8,128)(2,1)S(1)}, bf16[128,1792]{1,0:T(8,128)(2,1)S(1)}, u32[]{:S(2)}, u32[]{:S(2)}) collective-permute-start(bf16[128,1792]{1,0:T(8,128)(2,1)S(1)} %pad_maximum_fusion.refs_2_), channel_id=1, source_target_pairs={{0,12},{1,13},{2,14},{3,15},{4,0},{5,1},{6,2},{7,3},{8,4},{9,5},{1... | collective-permute-start | bytes 1376264 | tf_op jit(solution)/shard_map/ppermute | solution.py:230
  20.5 5.7 %collective-permute-done.3.refs_4_ = bf16[128,1792]{1,0:T(8,128)(2,1)S(1)} collective-permute-done((bf16[128,1792]{1,0:T(8,128)(2,1)S(1)}, bf16[128,1792]{1,0:T(8,128)(2,1)S(1)}, u32[]{:S(2)}, u32[]{:S(2)}) %collective-permute-start.3) | collective-permute-done | bytes 458784 | tf_op jit(solution)/shard_map/ppermute | solution.py:230
  26.3 3.0 %collective-permute-start.7 = (bf16[128,1792]{1,0:T(8,128)(2,1)S(1)}, bf16[128,1792]{1,0:T(8,128)(2,1)S(1)}, u32[]{:S(2)}, u32[]{:S(2)}) collective-permute-start(bf16[128,1792]{1,0:T(8,128)(2,1)S(1)} %collective-permute-done.3.refs_4_), channel_id=1, source_target_pairs={{0,12},{1,13},{2,14},{3,15},{4,0},{5,1},{6,2},{7,3},{8,4},{9,5},{1... | collective-permute-start | bytes 1376264 | tf_op jit(solution)/shard_map/ppermute | solution.py:230
  29.9 1.6 %collective-permute-done.5.refs_6_ = bf16[128,1792]{1,0:T(8,128)(2,1)S(1)} collective-permute-done((bf16[128,1792]{1,0:T(8,128)(2,1)S(1)}, bf16[128,1792]{1,0:T(8,128)(2,1)S(1)}, u32[]{:S(2)}, u32[]{:S(2)}) %collective-permute-start.5) | collective-permute-done | bytes 458784 | tf_op jit(solution)/shard_map/ppermute | solution.py:230
  32.0 6.9 %collective-permute-done.7.refs_8_ = bf16[128,1792]{1,0:T(8,128)(2,1)S(1)} collective-permute-done((bf16[128,1792]{1,0:T(8,128)(2,1)S(1)}, bf16[128,1792]{1,0:T(8,128)(2,1)S(1)}, u32[]{:S(2)}, u32[]{:S(2)}) %collective-permute-start.7) | collective-permute-done | bytes 458784 | tf_op jit(solution)/shard_map/ppermute | solution.py:230
  38.9 2.9 %collective-permute-start.12 = (bf16[128,1792]{1,0:T(8,128)(2,1)S(1)}, bf16[128,1792]{1,0:T(8,128)(2,1)}, u32[]{:S(2)}, u32[]{:S(2)}) collective-permute-start(bf16[128,1792]{1,0:T(8,128)(2,1)S(1)} %collective-permute-done.7.refs_8_), channel_id=1, source_target_pairs={{0,12},{1,13},{2,14},{3,15},{4,0},{5,1},{6,2},{7,3},{8,4},{9,5},{1... | collective-permute-start | bytes 1376264 | tf_op jit(solution)/shard_map/ppermute | solution.py:230
  41.8 2.1 %collective-permute-done.15.refs_16_ = bf16[128,1792]{1,0:T(8,128)(2,1)S(1)} collective-permute-done((bf16[128,1792]{1,0:T(8,128)(2,1)S(1)}, bf16[128,1792]{1,0:T(8,128)(2,1)S(1)}, u32[]{:S(2)}, u32[]{:S(2)}) %collective-permute-start.15) | collective-permute-done | bytes 458784 | tf_op jit(solution)/shard_map/ppermute | solution.py:230
  43.9 6.4 %collective-permute-done.10.refs_10_ = bf16[128,1792]{1,0:T(8,128)(2,1)} collective-permute-done((bf16[128,1792]{1,0:T(8,128)(2,1)S(1)}, bf16[128,1792]{1,0:T(8,128)(2,1)}, u32[]{:S(2)}, u32[]{:S(2)}) %collective-permute-start.10) | collective-permute-done | bytes 458784 | tf_op jit(solution)/shard_map/ppermute | solution.py:230
  51.6 7.3 %steering.1 = (bf16[1024,1024]{1,0:T(8,128)(2,1)}, bf16[1024,1024]{1,0:T(8,128)(2,1)}) custom-call(f32[8,64,1024]{2,1,0:T(8,128)} %refs_0_.1), custom_call_target="tpu_custom_call" | custom-call | tf_op jit(solution)/shard_map/steering/pallas_call | solution.py:49
  60.3 13.1 %focus.1 = (bf16[768,1024]{1,0:T(8,128)(2,1)}, f32[8,768]{1,0:T(8,128)}) custom-call(s32[8]{0:T(128)} %fusion.2.refs_0_, s32[48]{0:T(128)} %reshape.70.refs_1_, bf16[128,1792]{1,0:T(8,128)(2,1)} %copy-done, bf16[128,1792]{1,0:T(8,128)(2,1)} %copy-done.4, bf16[128,1792]{1,0:T(8,128)(2,1)} %copy-done.1, bf16[128,1792]{1,0:T(8,128)(2,1)} %copy-done.7, ...), custom_call_target="tpu_custom_call" | custom-call | tf_op jit(solution)/shard_map/focus/pallas_call | solution.py:119
  74.1 1.3 collective-permute-start.17
  75.4 16.3 %image.1 = (bf16[768,1024]{1,0:T(8,128)(2,1)}, bf16[768,1024]{1,0:T(8,128)(2,1)}, f32[8,1024]{1,0:T(8,128)}) custom-call(bf16[768,1024]{1,0:T(8,128)(2,1)} %get-tuple-element.14.focused_ref, bf16[1024,1024]{1,0:T(8,128)(2,1)} %get-tuple-element.12.refs_19_.re_ref, bf16[1024,1024]{1,0:T(8,128)(2,1)} %get-tuple-element.13.refs_20_.im_ref), custom_call_target="tpu_custom_call" | custom-call | tf_op jit(solution)/shard_map/image/pallas_call | solution.py:188
  91.8 1.5 %add_reduce_fusion = (f32[]{:T(128)}, f32[]{:T(128)}) fusion(f32[2,768]{1,0:T(2,128)S(1)} %collective-permute-done.17, f32[8,768]{1,0:T(8,128)} %get-tuple-element.17), kind=kLoop, calls=%fused_computation.8 | loop fusion | flops 6142 | bytes 12296 | tf_op jit(solution)/shard_map/reduce_sum | solution.py:280
  93.3 1.4 pad_maximum_fusion.1
  94.7 0.8 slice_select_fusion
  95.6 3.7 %collective-permute-done.18 = f32[3,1024]{1,0:T(4,128)S(1)} collective-permute-done((f32[3,1024]{1,0:T(4,128)S(1)}, f32[3,1024]{1,0:T(4,128)S(1)}, u32[]{:S(2)}, u32[]{:S(2)}) %collective-permute-start.18) | collective-permute-done | bytes 12320 | tf_op jit(solution)/shard_map/ppermute | solution.py:230
  99.3 0.8 fusion.12
  100.2 4.9 %collective-permute-done.19 = f32[3,1024]{1,0:T(4,128)S(1)} collective-permute-done((f32[3,1024]{1,0:T(4,128)S(1)}, f32[3,1024]{1,0:T(4,128)S(1)}, u32[]{:S(2)}, u32[]{:S(2)}) %collective-permute-start.19) | collective-permute-done | bytes 12320 | tf_op jit(solution)/shard_map/ppermute | solution.py:230
  105.1 3.7 %collective-permute-done.20 = f32[3,1024]{1,0:T(4,128)S(1)} collective-permute-done((f32[3,1024]{1,0:T(4,128)S(1)}, f32[3,1024]{1,0:T(4,128)S(1)}, u32[]{:S(2)}, u32[]{:S(2)}) %collective-permute-start.20) | collective-permute-done | bytes 12320 | tf_op jit(solution)/shard_map/ppermute | solution.py:230
  110.2 1.3 collective-permute-done.21
  112.8 5.3 %collective-permute-start.22 = (f32[1]{0:T(128)}, f32[1]{0:T(128)}, u32[]{:S(2)}, u32[]{:S(2)}) collective-permute-start(f32[1]{0:T(128)} %add.109), channel_id=1, source_target_pairs={{0,2},{1,3},{2,0},{3,1},{4,6},{5,7},{6,4},{7,5},{8,10},{9,11},{10,... | collective-permute-start | bytes 20 | tf_op jit(solution)/shard_map/ppermute | solution.py:230
  119.4 5.4 %collective-permute-start.23 = (f32[1]{0:T(128)}, f32[1]{0:T(128)}, u32[]{:S(2)}, u32[]{:S(2)}) collective-permute-start(f32[1]{0:T(128)} %add.111), channel_id=1, source_target_pairs={{0,4},{1,5},{2,6},{3,7},{4,0},{5,1},{6,2},{7,3},{8,12},{9,13},{10,... | collective-permute-start | bytes 20 | tf_op jit(solution)/shard_map/ppermute | solution.py:230
  126.1 1.4 collective-permute-start.24
  128.1 2.8 %collective-permute-done.24 = f32[1]{0:T(128)} collective-permute-done((f32[1]{0:T(128)}, f32[1]{0:T(128)}, u32[]{:S(2)}, u32[]{:S(2)}) %collective-permute-start.24) | collective-permute-done | bytes 36 | tf_op jit(solution)/shard_map/ppermute | solution.py:230
  131.6 0.9 fusion.8
  133.2 9.6 %apply.1 = bf16[12288,128]{1,0:T(8,128)(2,1)} custom-call(bf16[768,1024]{1,0:T(8,128)(2,1)} %get-tuple-element.15.re_ref, bf16[768,1024]{1,0:T(8,128)(2,1)} %get-tuple-element.16.im_ref, f32[1,1024]{1,0:T(1,128)} %cos.13.cos_ref, f32[1,1024]{1,0:T(1,128)} %get-tuple-element.21.sin_ref), custom_call_target="tpu_custom_call" | custom-call | tf_op jit(solution)/shard_map/apply/pallas_call | solution.py:215
  (69 shorter events, 7.3 us)
Async XLA Ops:
  0.0 59.0 %copy-start.9 = (s32[6,1,8]{2,1,0:T(1,128)S(1)}, s32[6,1,8]{2,1,0:T(1,128)}, u32[]{:S(2)}) copy-start(s32[6,1,8]{2,1,0:T(1,128)} %param.7) | copy-start | bytes 580
  0.0 59.6 %copy-start.10 = (s32[8]{0:T(128)S(1)}, s32[8]{0:T(128)}, u32[]{:S(2)}) copy-start(s32[8]{0:T(128)} %param.6) | copy-start | bytes 100
  0.8 5.8 %collective-permute-start = (bf16[128,128]{1,0:T(8,128)(2,1)S(1)}, bf16[128,128]{1,0:T(8,128)(2,1)S(1)}, u32[]{:S(2)}, u32[]{:S(2)}) collective-permute-start(bf16[128,128]{1,0:T(8,128)(2,1)S(1)} %get-tuple-element.23), channel_id=1, source_target_pairs={{0,16},{16,32},{32,48},{48,64},{64,80},{80,96},{96,112},{1,17},{17... | collective-permute-start | bytes 98312 | tf_op jit(solution)/shard_map/ppermute | solution.py:238
  4.5 7.9 %collective-permute-start.1 = (bf16[128,128]{1,0:T(8,128)(2,1)S(1)}, bf16[128,128]{1,0:T(8,128)(2,1)S(1)}, u32[]{:S(2)}, u32[]{:S(2)}) collective-permute-start(bf16[128,128]{1,0:T(8,128)(2,1)S(1)} %get-tuple-element.24), channel_id=1, source_target_pairs={{16,0},{32,16},{48,32},{64,48},{80,64},{96,80},{112,96},{17,1},{33... | collective-permute-start | bytes 98312 | tf_op jit(solution)/shard_map/ppermute | solution.py:239
  13.5 46.7 %copy-start = (bf16[128,1792]{1,0:T(8,128)(2,1)}, bf16[128,1792]{1,0:T(8,128)(2,1)S(1)}, u32[]{:S(2)}) copy-start(bf16[128,1792]{1,0:T(8,128)(2,1)S(1)} %pad_maximum_fusion.refs_2_) | copy-start | bytes 1376260
  13.5 12.8 %collective-permute-start.3 = (bf16[128,1792]{1,0:T(8,128)(2,1)S(1)}, bf16[128,1792]{1,0:T(8,128)(2,1)S(1)}, u32[]{:S(2)}, u32[]{:S(2)}) collective-permute-start(bf16[128,1792]{1,0:T(8,128)(2,1)S(1)} %pad_maximum_fusion.refs_2_), channel_id=1, source_target_pairs={{0,2},{1,3},{2,0},{3,1},{4,6},{5,7},{6,4},{7,5},{8,10},{9,11},{10,... | collective-permute-start | bytes 1376264 | tf_op jit(solution)/shard_map/ppermute | solution.py:230
  17.3 12.0 %collective-permute-start.9 = (bf16[128,1792]{1,0:T(8,128)(2,1)S(1)}, bf16[128,1792]{1,0:T(8,128)(2,1)S(1)}, u32[]{:S(2)}, u32[]{:S(2)}) collective-permute-start(bf16[128,1792]{1,0:T(8,128)(2,1)S(1)} %pad_maximum_fusion.refs_2_), channel_id=1, source_target_pairs={{0,4},{1,5},{2,6},{3,7},{4,8},{5,9},{6,10},{7,11},{8,12},{9,13},{1... | collective-permute-start | bytes 1376264 | tf_op jit(solution)/shard_map/ppermute | solution.py:230
  18.9 12.6 %collective-permute-start.5 = (bf16[128,1792]{1,0:T(8,128)(2,1)S(1)}, bf16[128,1792]{1,0:T(8,128)(2,1)S(1)}, u32[]{:S(2)}, u32[]{:S(2)}) collective-permute-start(bf16[128,1792]{1,0:T(8,128)(2,1)S(1)} %pad_maximum_fusion.refs_2_), channel_id=1, source_target_pairs={{0,12},{1,13},{2,14},{3,15},{4,0},{5,1},{6,2},{7,3},{8,4},{9,5},{1... | collective-permute-start | bytes 1376264 | tf_op jit(solution)/shard_map/ppermute | solution.py:230
  20.5 10.9 %collective-permute-start.2 = (bf16[128,1792]{1,0:T(8,128)(2,1)S(1)}, bf16[128,1792]{1,0:T(8,128)(2,1)S(1)}, u32[]{:S(2)}, u32[]{:S(2)}) collective-permute-start(bf16[128,1792]{1,0:T(8,128)(2,1)S(1)} %pad_maximum_fusion.refs_2_), channel_id=1, source_target_pairs={{0,1},{1,0},{2,3},{3,2},{4,5},{5,4},{6,7},{7,6},{8,9},{9,8},{10,11... | collective-permute-start | bytes 1376264 | tf_op jit(solution)/shard_map/ppermute | solution.py:230
  26.3 34.0 %copy-start.1 = (bf16[128,1792]{1,0:T(8,128)(2,1)}, bf16[128,1792]{1,0:T(8,128)(2,1)S(1)}, u32[]{:S(2)}) copy-start(bf16[128,1792]{1,0:T(8,128)(2,1)S(1)} %collective-permute-done.3.refs_4_) | copy-start | bytes 1376260
  26.3 12.6 %collective-permute-start.7 = (bf16[128,1792]{1,0:T(8,128)(2,1)S(1)}, bf16[128,1792]{1,0:T(8,128)(2,1)S(1)}, u32[]{:S(2)}, u32[]{:S(2)}) collective-permute-start(bf16[128,1792]{1,0:T(8,128)(2,1)S(1)} %collective-permute-done.3.refs_4_), channel_id=1, source_target_pairs={{0,12},{1,13},{2,14},{3,15},{4,0},{5,1},{6,2},{7,3},{8,4},{9,5},{1... | collective-permute-start | bytes 1376264 | tf_op jit(solution)/shard_map/ppermute | solution.py:230
  29.3 14.6 %collective-permute-start.15 = (bf16[128,1792]{1,0:T(8,128)(2,1)S(1)}, bf16[128,1792]{1,0:T(8,128)(2,1)S(1)}, u32[]{:S(2)}, u32[]{:S(2)}) collective-permute-start(bf16[128,1792]{1,0:T(8,128)(2,1)S(1)} %collective-permute-done.3.refs_4_), channel_id=1, source_target_pairs={{0,4},{1,5},{2,6},{3,7},{4,8},{5,9},{6,10},{7,11},{8,12},{9,13},{1... | collective-permute-start | bytes 1376264 | tf_op jit(solution)/shard_map/ppermute | solution.py:230
  29.3 30.9 %copy-start.2 = (bf16[128,1792]{1,0:T(8,128)(2,1)}, bf16[128,1792]{1,0:T(8,128)(2,1)S(1)}, u32[]{:S(2)}) copy-start(bf16[128,1792]{1,0:T(8,128)(2,1)S(1)} %collective-permute-done.9.refs_14_) | copy-start | bytes 1376260
  29.3 21.0 %collective-permute-start.10 = (bf16[128,1792]{1,0:T(8,128)(2,1)S(1)}, bf16[128,1792]{1,0:T(8,128)(2,1)}, u32[]{:S(2)}, u32[]{:S(2)}) collective-permute-start(bf16[128,1792]{1,0:T(8,128)(2,1)S(1)} %collective-permute-done.9.refs_14_), channel_id=1, source_target_pairs={{0,4},{1,5},{2,6},{3,7},{4,8},{5,9},{6,10},{7,11},{8,12},{9,13},{1... | collective-permute-start | bytes 1376264 | tf_op jit(solution)/shard_map/ppermute | solution.py:230
  31.5 28.8 %copy-start.3 = (bf16[128,1792]{1,0:T(8,128)(2,1)}, bf16[128,1792]{1,0:T(8,128)(2,1)S(1)}, u32[]{:S(2)}) copy-start(bf16[128,1792]{1,0:T(8,128)(2,1)S(1)} %collective-permute-done.5.refs_6_) | copy-start | bytes 1376260
  31.5 18.8 %collective-permute-start.4 = (bf16[128,1792]{1,0:T(8,128)(2,1)S(1)}, bf16[128,1792]{1,0:T(8,128)(2,1)S(1)}, u32[]{:S(2)}, u32[]{:S(2)}) collective-permute-start(bf16[128,1792]{1,0:T(8,128)(2,1)S(1)} %collective-permute-done.3.refs_4_), channel_id=1, source_target_pairs={{0,1},{1,0},{2,3},{3,2},{4,5},{5,4},{6,7},{7,6},{8,9},{9,8},{10,11... | collective-permute-start | bytes 1376264 | tf_op jit(solution)/shard_map/ppermute | solution.py:230
  31.5 28.8 %copy-start.4 = (bf16[128,1792]{1,0:T(8,128)(2,1)}, bf16[128,1792]{1,0:T(8,128)(2,1)S(1)}, u32[]{:S(2)}) copy-start(bf16[128,1792]{1,0:T(8,128)(2,1)S(1)} %collective-permute-done.2.refs_3_) | copy-start | bytes 1376260
  31.5 19.3 %collective-permute-start.14 = (bf16[128,1792]{1,0:T(8,128)(2,1)S(1)}, bf16[128,1792]{1,0:T(8,128)(2,1)S(1)}, u32[]{:S(2)}, u32[]{:S(2)}) collective-permute-start(bf16[128,1792]{1,0:T(8,128)(2,1)S(1)} %collective-permute-done.9.refs_14_), channel_id=1, source_target_pairs={{0,1},{1,0},{2,3},{3,2},{4,5},{5,4},{6,7},{7,6},{8,9},{9,8},{10,11... | collective-permute-start | bytes 1376264 | tf_op jit(solution)/shard_map/ppermute | solution.py:230
  38.9 12.1 %collective-permute-start.12 = (bf16[128,1792]{1,0:T(8,128)(2,1)S(1)}, bf16[128,1792]{1,0:T(8,128)(2,1)}, u32[]{:S(2)}, u32[]{:S(2)}) collective-permute-start(bf16[128,1792]{1,0:T(8,128)(2,1)S(1)} %collective-permute-done.7.refs_8_), channel_id=1, source_target_pairs={{0,12},{1,13},{2,14},{3,15},{4,0},{5,1},{6,2},{7,3},{8,4},{9,5},{1... | collective-permute-start | bytes 1376264 | tf_op jit(solution)/shard_map/ppermute | solution.py:230
  43.9 16.3 %collective-permute-start.6 = (bf16[128,1792]{1,0:T(8,128)(2,1)S(1)}, bf16[128,1792]{1,0:T(8,128)(2,1)}, u32[]{:S(2)}, u32[]{:S(2)}) collective-permute-start(bf16[128,1792]{1,0:T(8,128)(2,1)S(1)} %collective-permute-done.5.refs_6_), channel_id=1, source_target_pairs={{0,1},{1,0},{2,3},{3,2},{4,5},{5,4},{6,7},{7,6},{8,9},{9,8},{10,11... | collective-permute-start | bytes 1376264 | tf_op jit(solution)/shard_map/ppermute | solution.py:230
  50.3 9.9 %collective-permute-start.8 = (bf16[128,1792]{1,0:T(8,128)(2,1)S(1)}, bf16[128,1792]{1,0:T(8,128)(2,1)}, u32[]{:S(2)}, u32[]{:S(2)}) collective-permute-start(bf16[128,1792]{1,0:T(8,128)(2,1)S(1)} %collective-permute-done.7.refs_8_), channel_id=1, source_target_pairs={{0,1},{1,0},{2,3},{3,2},{4,5},{5,4},{6,7},{7,6},{8,9},{9,8},{10,11... | collective-permute-start | bytes 1376264 | tf_op jit(solution)/shard_map/ppermute | solution.py:230
  50.3 9.9 %collective-permute-start.16 = (bf16[128,1792]{1,0:T(8,128)(2,1)S(1)}, bf16[128,1792]{1,0:T(8,128)(2,1)}, u32[]{:S(2)}, u32[]{:S(2)}) collective-permute-start(bf16[128,1792]{1,0:T(8,128)(2,1)S(1)} %collective-permute-done.15.refs_16_), channel_id=1, source_target_pairs={{0,1},{1,0},{2,3},{3,2},{4,5},{5,4},{6,7},{7,6},{8,9},{9,8},{10,11... | collective-permute-start | bytes 1376264 | tf_op jit(solution)/shard_map/ppermute | solution.py:230
  50.8 9.4 %collective-permute-start.11 = (bf16[128,1792]{1,0:T(8,128)(2,1)}, bf16[128,1792]{1,0:T(8,128)(2,1)}, u32[]{:S(2)}, u32[]{:S(2)}) collective-permute-start(bf16[128,1792]{1,0:T(8,128)(2,1)} %collective-permute-done.10.refs_10_), channel_id=1, source_target_pairs={{0,1},{1,0},{2,3},{3,2},{4,5},{5,4},{6,7},{7,6},{8,9},{9,8},{10,11... | collective-permute-start | bytes 1376264 | tf_op jit(solution)/shard_map/ppermute | solution.py:230
  51.1 9.1 %collective-permute-start.13 = (bf16[128,1792]{1,0:T(8,128)(2,1)}, bf16[128,1792]{1,0:T(8,128)(2,1)}, u32[]{:S(2)}, u32[]{:S(2)}) collective-permute-start(bf16[128,1792]{1,0:T(8,128)(2,1)} %collective-permute-done.12.refs_12_), channel_id=1, source_target_pairs={{0,1},{1,0},{2,3},{3,2},{4,5},{5,4},{6,7},{7,6},{8,9},{9,8},{10,11... | collective-permute-start | bytes 1376264 | tf_op jit(solution)/shard_map/ppermute | solution.py:230
  74.1 17.6 %collective-permute-start.17 = (f32[2,768]{1,0:T(2,128)S(1)}, f32[2,768]{1,0:T(2,128)S(1)}, u32[]{:S(2)}, u32[]{:S(2)}) collective-permute-start(f32[2,768]{1,0:T(2,128)S(1)} %slice.48), channel_id=1, source_target_pairs={{1,0},{2,1},{3,2},{4,3},{5,4},{6,5},{7,6},{8,7},{9,8},{10,9},{11,1... | collective-permute-start | bytes 18440 | tf_op jit(solution)/shard_map/ppermute | solution.py:277
  95.5 3.8 %collective-permute-start.18 = (f32[3,1024]{1,0:T(4,128)S(1)}, f32[3,1024]{1,0:T(4,128)S(1)}, u32[]{:S(2)}, u32[]{:S(2)}) collective-permute-start(f32[3,1024]{1,0:T(4,128)S(1)} %slice_select_fusion), channel_id=1, source_target_pairs={{0,16},{16,0},{32,48},{48,32},{64,80},{80,64},{96,112},{112,96},{1... | collective-permute-start | bytes 36872 | tf_op jit(solution)/shard_map/ppermute | solution.py:230
  100.1 5.0 %collective-permute-start.19 = (f32[3,1024]{1,0:T(4,128)S(1)}, f32[3,1024]{1,0:T(4,128)S(1)}, u32[]{:S(2)}, u32[]{:S(2)}) collective-permute-start(f32[3,1024]{1,0:T(4,128)S(1)} %fusion.12), channel_id=1, source_target_pairs={{0,48},{16,32},{32,16},{48,0},{64,112},{80,96},{96,80},{112,64},{1... | collective-permute-start | bytes 36872 | tf_op jit(solution)/shard_map/ppermute | solution.py:230
  105.1 3.7 %collective-permute-start.20 = (f32[3,1024]{1,0:T(4,128)S(1)}, f32[3,1024]{1,0:T(4,128)S(1)}, u32[]{:S(2)}, u32[]{:S(2)}) collective-permute-start(f32[3,1024]{1,0:T(4,128)S(1)} %add.103), channel_id=1, source_target_pairs={{0,64},{16,80},{32,96},{48,112},{64,0},{80,16},{96,32},{112,48},{1... | collective-permute-start | bytes 36872 | tf_op jit(solution)/shard_map/ppermute | solution.py:230
  110.2 1.4 collective-permute-start.21
  112.8 5.9 %collective-permute-start.22 = (f32[1]{0:T(128)}, f32[1]{0:T(128)}, u32[]{:S(2)}, u32[]{:S(2)}) collective-permute-start(f32[1]{0:T(128)} %add.109), channel_id=1, source_target_pairs={{0,2},{1,3},{2,0},{3,1},{4,6},{5,7},{6,4},{7,5},{8,10},{9,11},{10,... | collective-permute-start | bytes 20 | tf_op jit(solution)/shard_map/ppermute | solution.py:230
  119.4 6.1 %collective-permute-start.23 = (f32[1]{0:T(128)}, f32[1]{0:T(128)}, u32[]{:S(2)}, u32[]{:S(2)}) collective-permute-start(f32[1]{0:T(128)} %add.111), channel_id=1, source_target_pairs={{0,4},{1,5},{2,6},{3,7},{4,0},{5,1},{6,2},{7,3},{8,12},{9,13},{10,... | collective-permute-start | bytes 20 | tf_op jit(solution)/shard_map/ppermute | solution.py:230
  126.1 4.8 %collective-permute-start.24 = (f32[1]{0:T(128)}, f32[1]{0:T(128)}, u32[]{:S(2)}, u32[]{:S(2)}) collective-permute-start(f32[1]{0:T(128)} %add.113), channel_id=1, source_target_pairs={{0,12},{1,13},{2,14},{3,15},{4,8},{5,9},{6,10},{7,11},{8,4},{9,5},... | collective-permute-start | bytes 20 | tf_op jit(solution)/shard_map/ppermute | solution.py:230
  (4 other events, 39.4 us)

commit v2 on v1

v2 whole, which is shorter than its diff:
```python
import jax
import jax.numpy as jnp
from jax import lax
from jax.experimental import pallas as pl
from jax.experimental.pallas import tpu as pltpu
from jax.sharding import PartitionSpec as P


GUARD = 128
LANES = 128
VMEM = pl.BlockSpec(memory_space=pltpu.VMEM)
SMEM = pl.BlockSpec(memory_space=pltpu.SMEM)
HBM = pl.BlockSpec(memory_space=pltpu.HBM)

PIO2_HI = 1.5707964
PIO2_LO = -4.371139e-8


def sine_cosine(x):
    turns = jnp.round(x * 0.63661975)
    r = (x - turns * PIO2_HI) - turns * PIO2_LO
    r2 = r * r
    sine = r + r * r2 * (-1.6666654611e-1 + r2 * (8.3321608736e-3 + r2 * -1.9515295891e-4))
    cosine = 1.0 - 0.5 * r2 + r2 * r2 * (
        4.166664568298827e-2 + r2 * (-1.388731625493765e-3 + r2 * 2.443315711809948e-5)
    )
    quadrant = turns.astype(jnp.int32)
    odd = (quadrant & 1) == 1
    first = jnp.where(odd, cosine, sine)
    second = jnp.where(odd, sine, cosine)
    sine = jnp.where((quadrant & 2) == 2, -first, first)
    cosine = jnp.where(((quadrant + 1) & 2) == 2, -second, second)
    return sine, cosine


def kernel_call(body, out_shape, *args, scalars=0, vmem_mib=8):
    return pl.pallas_call(
        body,
        in_specs=[SMEM] * scalars + [VMEM] * (len(args) - scalars),
        out_specs=[VMEM] * len(out_shape),
        out_shape=out_shape,
        compiler_params=pltpu.CompilerParams(vmem_limit_bytes=vmem_mib << 20),
    )(*args)


def steering_kernel(scale, phase_hbm, re_hbm, im_hbm, edge_hbm, phases, re_ref, im_ref, edge_ref, sems, done):
    pings, hydrophones, cells = phases.shape
    rows = 2 * hydrophones
    for p in range(pings):
        pltpu.make_async_copy(phase_hbm.at[p], phases.at[p], sems.at[p]).start()
    lane = lax.broadcasted_iota(jnp.int32, (rows, LANES), 1)
    for p in range(pings):
        pltpu.make_async_copy(phase_hbm.at[p], phases.at[p], sems.at[p]).wait()
        here = pl.ds(rows * p, rows)
        upper = pl.ds(rows * p, hydrophones)
        lower = pl.ds(rows * p + hydrophones, hydrophones)
        sine, cosine = sine_cosine(phases[p])
        steer_re = (cosine * scale).astype(jnp.bfloat16)
        steer_im = (sine * scale).astype(jnp.bfloat16)
        re_ref[upper] = steer_re
        re_ref[lower] = -steer_im
        im_ref[upper] = steer_im
        im_ref[lower] = steer_re
        pltpu.make_async_copy(re_ref.at[here], re_hbm.at[here], done.at[0]).start()
        pltpu.make_async_copy(im_ref.at[here], im_hbm.at[here], done.at[1]).start()
    for p in range(pings):
        here = pl.ds(rows * p, rows)
        first_re = re_ref[here, :LANES].astype(jnp.float32)
        first_im = pltpu.roll(im_ref[here, :LANES].astype(jnp.float32), 1, 1)
        last_re = pltpu.roll(re_ref[here, cells - LANES :].astype(jnp.float32), LANES - 1, 1)
        last_im = im_ref[here, cells - LANES :].astype(jnp.float32)
        mixed = jnp.where(
            lane < 64,
            jnp.where(lane == 0, first_re, first_im),
            jnp.where(lane == LANES - 1, last_im, last_re),
        )
        edge_ref[:, here] = mixed.T.astype(jnp.bfloat16)
    edge_copy = pltpu.make_async_copy(edge_ref, edge_hbm, done.at[2])
    edge_copy.start()
    pltpu.make_async_copy(re_ref, re_hbm, done.at[0]).wait()
    pltpu.make_async_copy(im_ref, im_hbm, done.at[1]).wait()
    edge_copy.wait()


def steering(phases):
    pings, hydrophones, cells = phases.shape
    rows = pings * 2 * hydrophones
    scale = float(1.0 / (pings * hydrophones) ** 0.5)
    out = jax.ShapeDtypeStruct((rows, cells), jnp.bfloat16)
    edge = jax.ShapeDtypeStruct((LANES, rows), jnp.bfloat16)
    return pl.pallas_call(
        lambda *refs: steering_kernel(scale, *refs),
        in_specs=[HBM],
        out_specs=[HBM] * 3,
        out_shape=[pltpu.HBM(o.shape, o.dtype) for o in (out, out, edge)],
        scratch_shapes=[
            pltpu.VMEM(phases.shape, jnp.float32),
            pltpu.VMEM((rows, cells), jnp.bfloat16),
            pltpu.VMEM((rows, cells), jnp.bfloat16),
            pltpu.VMEM((LANES, rows), jnp.bfloat16),
            pltpu.SemaphoreType.DMA((pings,)),
            pltpu.SemaphoreType.DMA((3,)),
        ],
        compiler_params=pltpu.CompilerParams(vmem_limit_bytes=12 << 20),
        name="steering",
    )(pltpu.with_memory_space_constraint(phases, pltpu.HBM))


def focus_kernel(n_slots, place_ref, ping_ref, start_ref, *refs):
    slots = refs[:n_slots]
    ends = refs[n_slots : n_slots + n_slots // 2]
    interp_ref, weight_hbm, out_ref, edge_ref, window, weight_ref, sems = refs[
        n_slots + n_slots // 2 :
    ]
    pings, range_cells, band = interp_ref.shape
    rows, width = slots[0].shape
    blocks = start_ref.shape[0] // pings
    cells = range_cells // blocks
    span = band + LANES
    for s in range(n_slots):
        k = place_ref[s]
        end = ends[s // 4 * 2 + s % 2].at[s // 2 % 2]

        @pl.when(k >= 0)
        def _():
            for source, low in (
                (slots[s], GUARD),
                (end.at[:, pl.ds(0, GUARD)], 0),
                (end.at[:, pl.ds(GUARD, GUARD)], GUARD + width),
            ):
                part = window.at[k, :, pl.ds(low, source.shape[1])]
                pltpu.make_async_copy(source, part, sems.at[k]).start()

    weight_copy = pltpu.make_async_copy(weight_hbm, weight_ref, sems.at[pings])
    weight_copy.start()
    for k in range(pings):
        pltpu.make_async_copy(window.at[k], window.at[k], sems.at[k]).wait()
        p = ping_ref[k]
        column = pl.ds(pl.multiple_of(p * rows, LANES), rows)
        for b in range(blocks):
            start = start_ref[b * pings + p]
            aligned = jnp.minimum((start // LANES) * LANES, width + 2 * GUARD - span)
            aligned = pl.multiple_of(aligned, LANES)
            wide = window[k, :, pl.ds(aligned, span)]
            slab = pltpu.roll(wide, span - (start - aligned), 1)[:, :band]
            kernel = interp_ref[p, b * cells : (b + 1) * cells, :]
            got = lax.dot_general(
                kernel, slab, (((1,), (1,)), ((), ())), preferred_element_type=jnp.float32
            )
            out_ref[b * cells : (b + 1) * cells, column] = got.astype(jnp.bfloat16)

    weight_copy.wait()
    got = lax.dot_general(
        weight_ref[...], out_ref[...], (((1,), (1,)), ((), ())), preferred_element_type=jnp.float32
    )
    edge_ref[0:2, :] = got[0:2].astype(jnp.bfloat16).astype(jnp.float32)
    edge_ref[2:4, :] = got[LANES - 2 :].astype(jnp.bfloat16).astype(jnp.float32)


def focus(slots, ends, places, ping_at, starts, interp, edge_weights):
    pings, range_cells, _ = interp.shape
    rows, width = slots[0].shape
    call = pl.pallas_call(
        lambda *refs: focus_kernel(len(slots), *refs),
        in_specs=[SMEM] * 3 + [HBM] * (len(slots) + len(ends)) + [VMEM, HBM],
        out_specs=[VMEM] * 2,
        out_shape=[
            jax.ShapeDtypeStruct((range_cells, pings * rows), jnp.bfloat16),
            jax.ShapeDtypeStruct((4, range_cells), jnp.float32),
        ],
        scratch_shapes=[
            pltpu.VMEM((pings, rows, width + 2 * GUARD), jnp.bfloat16),
            pltpu.VMEM(edge_weights.shape, jnp.bfloat16),
            pltpu.SemaphoreType.DMA((pings + 1,)),
        ],
        compiler_params=pltpu.CompilerParams(vmem_limit_bytes=16 << 20),
        name="focus",
    )
    local = [pltpu.with_memory_space_constraint(x, pltpu.HBM) for x in (*slots, *ends)]
    edge_weights = pltpu.with_memory_space_constraint(edge_weights, pltpu.HBM)
    return call(places, ping_at, starts, *local, interp, edge_weights)


def image_kernel(focused_ref, re_ref, im_ref, out_re, out_im, stats_ref):
    tile = 512
    rows, cells = out_re.shape
    focused = focused_ref[...]
    for n in range(cells // tile):
        part = slice(n * tile, (n + 1) * tile)
        out_re[:, part] = jnp.dot(
            focused, re_ref[:, part], preferred_element_type=jnp.float32
        ).astype(jnp.bfloat16)
        out_im[:, part] = jnp.dot(
            focused, im_ref[:, part], preferred_element_type=jnp.float32
        ).astype(jnp.bfloat16)
    step = 16
    half = 512

    def fold(x):
        return x[:8] + x[8:]

    stats_ref[...] = jnp.zeros_like(stats_ref)
    for low in range(0, cells, half):
        last = low + half == cells
        span = half if last else half + LANES

        def body(i, carry):
            power, real, imag = carry
            here = pl.ds(pl.multiple_of(i * step, step), step)
            a = out_re[here, low : low + span].astype(jnp.float32)
            b = out_im[here, low : low + span].astype(jnp.float32)
            na = pltpu.roll(a, span - 1, 1)[:, :half]
            nb = pltpu.roll(b, span - 1, 1)[:, :half]
            a, b = a[:, :half], b[:, :half]
            power = power + fold(a * a + b * b)
            real = real + fold(a * na + b * nb)
            imag = imag + fold(a * nb - b * na)
            return power, real, imag

        zero = jnp.zeros((8, half), jnp.float32)
        sums = lax.fori_loop(0, rows // step, body, (zero, zero, zero), unroll=8)
        for k, value in enumerate(sums):
            stats_ref[k : k + 1, low : low + half] = jnp.sum(value, axis=0, keepdims=True)


def image(focused, steer_re, steer_im):
    rows, cells = focused.shape[0], steer_re.shape[1]
    out = jax.ShapeDtypeStruct((rows, cells), jnp.bfloat16)
    return kernel_call(
        image_kernel,
        [out, out, jax.ShapeDtypeStruct((8, cells), jnp.float32)],
        focused,
        steer_re,
        steer_im,
    )


def seam_kernel(stats_ref, edges_ref, halo_ref, out_ref):
    cells = stats_ref.shape[1]
    last_re, last_im = edges_ref[2:3, :], edges_ref[3:4, :]
    next_re, next_im = halo_ref[0:1, :], halo_ref[1:2, :]
    real = jnp.sum(last_re * next_re + last_im * next_im, axis=1, keepdims=True)
    imag = jnp.sum(last_re * next_im - last_im * next_re, axis=1, keepdims=True)
    at = lax.broadcasted_iota(jnp.int32, (1, cells), 1) == cells - 1
    out_ref[...] = stats_ref[...]
    out_ref[1:2, :] = jnp.where(at, real, stats_ref[1:2, :])
    out_ref[2:3, :] = jnp.where(at, imag, stats_ref[2:3, :])


def slope_kernel(stats_ref, more_ref, phase_ref, total_ref):
    cells = stats_ref.shape[1]
    stats = stats_ref[...] + more_ref[...]
    power, real, imag = stats[0:1] + 1e-06, stats[1:2], stats[2:3]
    first = imag / power
    second = (imag * jnp.cos(first) - real * jnp.sin(first)) / power
    slope = first + second
    lane = lax.broadcasted_iota(jnp.int32, (1, cells), 1)
    summed = slope
    step = 1
    while step < cells:
        summed = summed + jnp.where(lane >= step, pltpu.roll(summed, step, 1), 0.0)
        step *= 2
    phase_ref[...] = summed - slope
    total_ref[...] = jnp.broadcast_to(jnp.sum(slope, axis=1, keepdims=True), total_ref.shape)


def apply_kernel(re_ref, im_ref, phase_ref, before_ref, out_ref, scratch, cos_ref, sin_ref):
    step = scratch.shape[0] * LANES // (2 * re_ref.shape[1])
    tiles = re_ref.shape[1] // LANES

    @pl.when(pl.program_id(0) == 0)
    def _():
        phase = phase_ref[...] + before_ref[0:1, 0:1]
        cos_ref[...] = jnp.cos(phase)
        sin_ref[...] = jnp.sin(phase)

    here = pl.ds(pl.multiple_of(pl.program_id(0) * step, step), step)
    for t in range(tiles):
        part = slice(t * LANES, (t + 1) * LANES)
        a = re_ref[here, part].astype(jnp.float32)
        b = im_ref[here, part].astype(jnp.float32)
        cosine = cos_ref[:, part]
        sine = sin_ref[:, part]
        scratch[pl.ds(2 * t, step, stride=2 * tiles), :] = a * cosine + b * sine
        scratch[pl.ds(2 * t + 1, step, stride=2 * tiles), :] = b * cosine - a * sine
    out_ref[...] = scratch[...].astype(jnp.bfloat16)


def apply(real, imag, phase, before):
    rows, cells = real.shape
    tiles = cells // LANES
    step = 128
    out = pl.pallas_call(
        apply_kernel,
        grid=(rows // step,),
        in_specs=[VMEM] * 4,
        out_specs=pl.BlockSpec((step * 2 * tiles, LANES), lambda i: (i, 0)),
        out_shape=jax.ShapeDtypeStruct((rows * 2 * tiles, LANES), jnp.bfloat16),
        scratch_shapes=[
            pltpu.VMEM((step * 2 * tiles, LANES), jnp.float32),
            pltpu.VMEM((1, cells), jnp.float32),
            pltpu.VMEM((1, cells), jnp.float32),
        ],
        compiler_params=pltpu.CompilerParams(vmem_limit_bytes=12 << 20),
        name="apply",
    )(real, imag, phase, before)
    out = out.reshape(rows, tiles, 2, LANES).transpose(0, 2, 1, 3)
    return out.reshape(rows, 2, cells)


def send(x, axis, move):
    n = lax.axis_size(axis)
    return lax.ppermute(x, axis, [(i, move(i)) for i in range(n)])


def up(x):
    return send(x, "az", lambda i: (i + 4) % 16)


def down(x):
    return send(x, "az", lambda i: (i - 4) % 16)


def across(x):
    return send(x, "az", lambda i: i ^ 2)


def partner(x):
    return send(x, "az", lambda i: i ^ 1)


def spread(block):
    n = lax.axis_size("rng")
    width = block.shape[1]
    above, below, other = up(block), down(block), across(block)
    low = lax.ppermute(block[:, width - GUARD :], "rng", [(i, i + 1) for i in range(n - 1)])
    high = lax.ppermute(block[:, :GUARD], "rng", [(i + 1, i) for i in range(n - 1)])
    ends = jnp.concatenate([low, high], axis=1)
    passed = jnp.where(lax.axis_index("az") & 1 == 0, above, below)
    opposite = send(passed, "az", lambda i: (i + (4, -4)[i & 1]) % 16)
    slots = {(0, 0): block, (3, 0): above, (1, 0): below, (2, 0): opposite, (0, 1): other}
    slots[3, 1] = up(other)
    slots[1, 1] = down(other)
    slots[2, 1] = across(opposite)
    ends = jnp.stack([ends, across(ends)])
    far = send(ends, "az", lambda i: (i + 8) % 16)
    ends = [ends, down(ends), far, up(ends)]
    out_slots, out_ends = [], []
    for y in range(4):
        out_ends += [ends[y], partner(ends[y])]
        for z in range(2):
            out_slots += [slots[y, z], partner(slots[y, z])]
    return out_slots, out_ends


def per_device_body(echoes, owner_map, band_start, interp, steer_phase):
    hydrophones, samples = echoes.shape[2:]
    n_az = lax.axis_size("az")
    me = lax.axis_index("az")
    relative = ((((owner_map >> 2) - (me >> 2)) & 3) << 2) | ((owner_map ^ me) & 3)
    slot = jnp.arange(n_az, dtype=jnp.int32)
    place = jnp.sum(relative[None, :] < relative[:, None], axis=1).astype(jnp.int32)
    matches = relative[None, :] == slot[:, None]
    places = jnp.sum(jnp.where(matches, place[None, :] + 1, 0), axis=1) - 1
    number = jnp.arange(owner_map.shape[0], dtype=jnp.int32)
    ping_at = jnp.sum(jnp.where(place[None, :] == number[:, None], number[None, :], 0), axis=1)
    starts = band_start.reshape(-1)
    steer_re, steer_im, edge_weights = steering(steer_phase)
    slots, ends = spread(echoes[0].reshape(2 * hydrophones, samples))
    focused, edges = focus(
        slots, ends, places, ping_at, starts, interp[:, 0], edge_weights
    )
    halo = lax.ppermute(edges[:2], "az", [(i + 1, i) for i in range(n_az - 1)])
    real, imag, stats = image(focused, steer_re, steer_im)
    (stats,) = kernel_call(
        seam_kernel, [jax.ShapeDtypeStruct(stats.shape, jnp.float32)], stats, edges, halo,
    )
    for mask in (1, 3):
        stats = stats + send(stats, "rng", lambda i: i ^ mask)
    phase, total = kernel_call(
        slope_kernel,
        [
            jax.ShapeDtypeStruct((1, stats.shape[1]), jnp.float32),
            jax.ShapeDtypeStruct((8, LANES), jnp.float32),
        ],
        stats,
        send(stats, "rng", lambda i: i ^ 4),
    )
    before = jnp.zeros_like(total)
    for mask, bit in ((1, 1), (2, 2), (4, 4), (12, 8)):
        got = send(total, "az", lambda i: i ^ mask)
        before = before + jnp.where((me & bit) != 0, got, 0.0)
        total = total + got
    return apply(real, imag, phase, before)


def solution(mesh):
    in_specs = (
        P("az", None, None, "rng"),
        P(),
        P("rng", "az", None),
        P(None, "az", "rng", None),
        P(None, None, "az"),
    )
    out_specs = P("rng", None, "az")
    return jax.shard_map(
        per_device_body, mesh=mesh, in_specs=in_specs, out_specs=out_specs, check_vma=False
    )
```

time: 144 us -> 111 us (0.77); the launches traced: 143 us -> 111 us
  Pallas kernels: 46.3 us -> 23.2 us
  between operations: 5.46 us -> 0.27 us
  starting transfers between devices: 34.3 us -> 38.9 us
  waiting for transfers between devices: 45.1 us -> 40.9 us
  other arithmetic: 7.65 us -> 5.01 us
    pallas_call x4 -> x6, Pallas kernels: 46.3 us -> 23.2 us  [the longest x3 6.42 us: kernel_call(): pl.pallas_call(body, in_specs=[SMEM] * scalars + [VMEM] * (len(args) - sc...]
    ppermute x22 -> x30, starting transfers between devices: 27.2 us -> 31.7 us  [send(): return lax.ppermute(x, axis, [(i, move(i)) for i in range(n)])]
    ppermute x22 -> x30, waiting for transfers between devices: 39.3 us -> 35.7 us  [send(): return lax.ppermute(x, axis, [(i, move(i)) for i in range(n)])]
  transfers between devices with their start and end apart: 25 -> 33, of which waited for: 11 -> 16; matrix products, arithmetic and copies ran while one was open for 1% -> 6% of each run, Pallas kernels for 17% -> 10%
where the time goes in v2:
time: 111 us
  waiting for transfers between devices  40.9 us (37%)
  starting transfers between devices  38.9 us (35%)
  Pallas kernels  23.2 us (21%)
  other arithmetic  5.01 us (5%)
  local copies, waits for them, and re-layouts  2.94 us (3%)
    ppermute x30, waiting for transfers between devices, send(): return lax.ppermute(x, axis, [(i, move(i)) for i in range(n)])  35.7 us
    ppermute x30, starting transfers between devices, send(): return lax.ppermute(x, axis, [(i, move(i)) for i in range(n)])  31.7 us
    pallas_call x3, Pallas kernels, kernel_call(): pl.pallas_call(body, in_specs=[SMEM] * scalars + [VMEM] * (len(args) - sc...  6.42 us
    pallas_call x1, Pallas kernels, focus(): return call(places, ping_at, starts, *local, interp, edge_weights)  6.13 us
    pallas_call x1, Pallas kernels, steering(): pl.pallas_call(lambda *refs: steering_kernel(scale, *refs), in_specs=[HBM...  5.4 us
    pallas_call x1, Pallas kernels, apply(): pl.pallas_call(apply_kernel, grid=(rows // step,), in_specs=[VMEM] * 4, o...  5.25 us
    ppermute x1, waiting for transfers between devices, spread(): lax.ppermute(block[:, :GUARD], 'rng', [(i + 1, i) for i in range(n - 1)])  5.18 us
    ppermute x1, starting transfers between devices, spread(): lax.ppermute(block[:, width - GUARD:], 'rng', [(i, i + 1) for i in range(...  3.86 us
  transfers between devices with their start and end apart: 33, of which 16 were waited for; matrix products, arithmetic and copies ran while one was open for 6% of the time, Pallas kernels for 10%

profile of v2, /device:TPU:6, one launch (start us, length us, event | category | flops | bytes accessed | tf_op | source)
XLA Modules:
  0.0 111.2 jit_solution(11909574474602336239)
XLA Ops:
  0.9 3.9 %collective-permute-start.15 = (bf16[128,128]{1,0:T(8,128)(2,1)S(1)}, bf16[128,128]{1,0:T(8,128)(2,1)S(1)}, u32[]{:S(2)}, u32[]{:S(2)}) collective-permute-start(bf16[128,128]{1,0:T(8,128)(2,1)S(1)} %get-tuple-element.26), channel_id=1, source_target_pairs={{0,16},{16,32},{32,48},{48,64},{64,80},{80,96},{96,112},{1,17},{17... | collective-permute-start | bytes 98312 | tf_op jit(solution)/shard_map/ppermute | solution.py:336
  4.8 3.1 %collective-permute-start.3 = (bf16[128,1536]{1,0:T(8,128)(2,1)}, bf16[128,1536]{1,0:T(8,128)(2,1)S(1)}, u32[]{:S(2)}, u32[]{:S(2)}) collective-permute-start(bf16[128,1536]{1,0:T(8,128)(2,1)} %bitcast.11), channel_id=1, source_target_pairs={{0,12},{1,13},{2,14},{3,15},{4,0},{5,1},{6,2},{7,3},{8,4},{9,5},{1... | collective-permute-start | bytes 1179656 | tf_op jit(solution)/shard_map/ppermute | solution.py:313
  7.9 2.1 %collective-permute-start.16 = (bf16[128,128]{1,0:T(8,128)(2,1)S(1)}, bf16[128,128]{1,0:T(8,128)(2,1)S(1)}, u32[]{:S(2)}, u32[]{:S(2)}) collective-permute-start(bf16[128,128]{1,0:T(8,128)(2,1)S(1)} %get-tuple-element.25), channel_id=1, source_target_pairs={{16,0},{32,16},{48,32},{64,48},{80,64},{96,80},{112,96},{17,1},{33... | collective-permute-start | bytes 98312 | tf_op jit(solution)/shard_map/ppermute | solution.py:337
  10.6 5.2 %collective-permute-done.16 = bf16[128,128]{1,0:T(8,128)(2,1)S(1)} collective-permute-done((bf16[128,128]{1,0:T(8,128)(2,1)S(1)}, bf16[128,128]{1,0:T(8,128)(2,1)S(1)}, u32[]{:S(2)}, u32[]{:S(2)}) %collective-permute-start.16) | collective-permute-done | bytes 32800 | tf_op jit(solution)/shard_map/ppermute | solution.py:337
  16.4 3.6 %collective-permute-start.17 = (bf16[128,256]{1,0:T(8,128)(2,1)}, bf16[128,256]{1,0:T(8,128)(2,1)}, u32[]{:S(2)}, u32[]{:S(2)}) collective-permute-start(bf16[128,256]{1,0:T(8,128)(2,1)} %constant_dynamic-update-slice_fusion), channel_id=1, source_target_pairs={{0,2},{1,3},{2,0},{3,1},{4,6},{5,7},{6,4},{7,5},{8,10},{9,11},{10,... | collective-permute-start | bytes 196616 | tf_op jit(solution)/shard_map/ppermute | solution.py:313
  20.0 2.8 %collective-permute-done.17 = bf16[128,256]{1,0:T(8,128)(2,1)} collective-permute-done((bf16[128,256]{1,0:T(8,128)(2,1)}, bf16[128,256]{1,0:T(8,128)(2,1)}, u32[]{:S(2)}, u32[]{:S(2)}) %collective-permute-start.17) | collective-permute-done | bytes 65568 | tf_op jit(solution)/shard_map/ppermute | solution.py:313
  23.7 3.6 %collective-permute-start.19 = (bf16[2,128,256]{2,1,0:T(8,128)(2,1)S(1)}, bf16[2,128,256]{2,1,0:T(8,128)(2,1)S(1)}, u32[]{:S(2)}, u32[]{:S(2)}) collective-permute-start(bf16[2,128,256]{2,1,0:T(8,128)(2,1)S(1)} %pad_maximum_fusion.refs_19_), channel_id=1, source_target_pairs={{0,12},{1,13},{2,14},{3,15},{4,0},{5,1},{6,2},{7,3},{8,4},{9,5},{1... | collective-permute-start | bytes 393224 | tf_op jit(solution)/shard_map/ppermute | solution.py:313
  27.3 1.0 collective-permute-start.23
  28.3 1.8 %broadcast_select_fusion = bf16[128,1536]{1,0:T(8,128)(2,1)} fusion(bf16[128,1536]{1,0:T(8,128)(2,1)} %collective-permute-done.7.refs_15_, bf16[128,1536]{1,0:T(8,128)(2,1)S(1)} %collective-permute-done.3.refs_7_, pred[]{:T(512)S(6)} %eq.35), kind=kLoop, calls=%fused_computation | loop fusion | flops 196608 | bytes 1179649 | tf_op jit(solution)/shard_map/jit(_where)/select_n | solution.py:339
  30.1 1.2 %collective-permute-done.19.refs_21_ = bf16[2,128,256]{2,1,0:T(8,128)(2,1)S(1)} collective-permute-done((bf16[2,128,256]{2,1,0:T(8,128)(2,1)S(1)}, bf16[2,128,256]{2,1,0:T(8,128)(2,1)S(1)}, u32[]{:S(2)}, u32[]{:S(2)}) %collective-permute-start.19) | collective-permute-done | bytes 131104 | tf_op jit(solution)/shard_map/ppermute | solution.py:313
  31.2 1.4 %collective-permute-start.8 = (bf16[128,1536]{1,0:T(8,128)(2,1)}, bf16[128,1536]{1,0:T(8,128)(2,1)}, u32[]{:S(2)}, u32[]{:S(2)}) collective-permute-start(bf16[128,1536]{1,0:T(8,128)(2,1)} %broadcast_select_fusion), channel_id=1, source_target_pairs={{0,4},{1,13},{2,6},{3,15},{4,8},{5,1},{6,10},{7,3},{8,12},{9,5},{1... | collective-permute-start | bytes 1179656 | tf_op jit(solution)/shard_map/ppermute | solution.py:313
  32.6 1.4 %collective-permute-done.21.refs_23_ = bf16[2,128,256]{2,1,0:T(8,128)(2,1)} collective-permute-done((bf16[2,128,256]{2,1,0:T(8,128)(2,1)S(1)}, bf16[2,128,256]{2,1,0:T(8,128)(2,1)}, u32[]{:S(2)}, u32[]{:S(2)}) %collective-permute-start.21) | collective-permute-done | bytes 131104 | tf_op jit(solution)/shard_map/ppermute | solution.py:313
  34.0 1.1 collective-permute-done.23.refs_25_
  37.3 3.2 %collective-permute-start.5 = (bf16[128,1536]{1,0:T(8,128)(2,1)}, bf16[128,1536]{1,0:T(8,128)(2,1)}, u32[]{:S(2)}, u32[]{:S(2)}) collective-permute-start(bf16[128,1536]{1,0:T(8,128)(2,1)} %collective-permute-done.1.refs_5_), channel_id=1, source_target_pairs={{0,12},{1,13},{2,14},{3,15},{4,0},{5,1},{6,2},{7,3},{8,4},{9,5},{1... | collective-permute-start | bytes 1179656 | tf_op jit(solution)/shard_map/ppermute | solution.py:313
  41.0 3.7 %collective-permute-start.10 = (bf16[128,1536]{1,0:T(8,128)(2,1)}, bf16[128,1536]{1,0:T(8,128)(2,1)}, u32[]{:S(2)}, u32[]{:S(2)}) collective-permute-start(bf16[128,1536]{1,0:T(8,128)(2,1)} %collective-permute-done.8.refs_11_), channel_id=1, source_target_pairs={{0,2},{1,3},{2,0},{3,1},{4,6},{5,7},{6,4},{7,5},{8,10},{9,11},{10,... | collective-permute-start | bytes 1179656 | tf_op jit(solution)/shard_map/ppermute | solution.py:313
  46.1 4.0 %collective-permute-done.13.refs_17_ = bf16[128,1536]{1,0:T(8,128)(2,1)} collective-permute-done((bf16[128,1536]{1,0:T(8,128)(2,1)}, bf16[128,1536]{1,0:T(8,128)(2,1)}, u32[]{:S(2)}, u32[]{:S(2)}) %collective-permute-start.13) | collective-permute-done | bytes 393248 | tf_op jit(solution)/shard_map/ppermute | solution.py:313
  51.2 3.2 %collective-permute-done.10.refs_13_ = bf16[128,1536]{1,0:T(8,128)(2,1)} collective-permute-done((bf16[128,1536]{1,0:T(8,128)(2,1)}, bf16[128,1536]{1,0:T(8,128)(2,1)}, u32[]{:S(2)}, u32[]{:S(2)}) %collective-permute-start.10) | collective-permute-done | bytes 393248 | tf_op jit(solution)/shard_map/ppermute | solution.py:313
  54.5 5.4 %steering.1 = (bf16[1024,1024]{1,0:T(8,128)(2,1)}, bf16[1024,1024]{1,0:T(8,128)(2,1)}, bf16[128,1024]{1,0:T(8,128)(2,1)}) custom-call(f32[8,64,1024]{2,1,0:T(8,128)} %refs_0_.1), custom_call_target="tpu_custom_call" | custom-call | tf_op jit(solution)/shard_map/steering/pallas_call | solution.py:91
  60.9 6.1 %focus.1 = (bf16[768,1024]{1,0:T(8,128)(2,1)S(1)}, f32[4,768]{1,0:T(4,128)S(1)}) custom-call(s32[16]{0:T(128)S(1)} %broadcast_add_fusion.refs_0_, s32[8]{0:T(128)S(1)} %select_reduce_fusion.refs_1_, s32[48]{0:T(128)S(1)} %reshape.16.refs_2_, bf16[128,1536]{1,0:T(8,128)(2,1)} %bitcast.15, bf16[128,1536]{1,0:T(8,128)(2,1)} %collective-permute-done.refs_4_, ...), custom_call_target="tpu_custom_call" | custom-call | tf_op jit(solution)/shard_map/focus/pallas_call | solution.py:181
  67.0 1.3 %collective-permute-start.25 = (f32[2,768]{1,0:T(2,128)S(1)}, f32[2,768]{1,0:T(2,128)S(1)}, u32[]{:S(2)}, u32[]{:S(2)}) collective-permute-start(f32[2,768]{1,0:T(2,128)S(1)} %slice.11), channel_id=1, source_target_pairs={{1,0},{2,1},{3,2},{4,3},{5,4},{6,5},{7,6},{8,7},{9,8},{10,9},{11,1... | collective-permute-start | bytes 18440 | tf_op jit(solution)/shard_map/ppermute | solution.py:373
  68.3 5.6 %shard_map.55 = (bf16[768,1024]{1,0:T(8,128)(2,1)S(1)}, bf16[768,1024]{1,0:T(8,128)(2,1)S(1)}, f32[8,1024]{1,0:T(8,128)S(1)}) custom-call(bf16[768,1024]{1,0:T(8,128)(2,1)S(1)} %get-tuple-element.16.focused_ref, bf16[1024,1024]{1,0:T(8,128)(2,1)S(1)} %copy-done.1, bf16[1024,1024]{1,0:T(8,128)(2,1)S(1)} %copy-done.2), custom_call_target="tpu_custom_call" | custom-call | tf_op jit(solution)/shard_map/pallas_call | solution.py:37
  74.1 4.1 %collective-permute-done.26 = f32[8,1024]{1,0:T(8,128)S(1)} collective-permute-done((f32[8,1024]{1,0:T(8,128)S(1)}, f32[8,1024]{1,0:T(8,128)S(1)}, u32[]{:S(2)}, u32[]{:S(2)}) %collective-permute-start.26) | collective-permute-done | bytes 32800 | tf_op jit(solution)/shard_map/ppermute | solution.py:313
  78.2 5.1 %collective-permute-done.27 = f32[8,1024]{1,0:T(8,128)S(1)} collective-permute-done((f32[8,1024]{1,0:T(8,128)S(1)}, f32[8,1024]{1,0:T(8,128)S(1)}, u32[]{:S(2)}, u32[]{:S(2)}) %collective-permute-start.27) | collective-permute-done | bytes 32800 | tf_op jit(solution)/shard_map/ppermute | solution.py:313
  83.3 3.9 %collective-permute-done.28.more_ref = f32[8,1024]{1,0:T(8,128)S(1)} collective-permute-done((f32[8,1024]{1,0:T(8,128)S(1)}, f32[8,1024]{1,0:T(8,128)S(1)}, u32[]{:S(2)}, u32[]{:S(2)}) %collective-permute-start.28) | collective-permute-done | bytes 32800 | tf_op jit(solution)/shard_map/ppermute | solution.py:313
  88.0 1.2 %collective-permute-done.29 = f32[8,128]{1,0:T(8,128)S(1)} collective-permute-done((f32[8,128]{1,0:T(8,128)S(1)}, f32[8,128]{1,0:T(8,128)S(1)}, u32[]{:S(2)}, u32[]{:S(2)}) %collective-permute-start.29) | collective-permute-done | bytes 4128 | tf_op jit(solution)/shard_map/ppermute | solution.py:313
  89.2 4.1 %collective-permute-start.30 = (f32[8,128]{1,0:T(8,128)S(1)}, f32[8,128]{1,0:T(8,128)S(1)}, u32[]{:S(2)}, u32[]{:S(2)}) collective-permute-start(f32[8,128]{1,0:T(8,128)S(1)} %add.36), channel_id=1, source_target_pairs={{0,2},{1,3},{2,0},{3,1},{4,6},{5,7},{6,4},{7,5},{8,10},{9,11},{10,... | collective-permute-start | bytes 12296 | tf_op jit(solution)/shard_map/ppermute | solution.py:313
  93.3 1.6 %collective-permute-done.30 = f32[8,128]{1,0:T(8,128)S(1)} collective-permute-done((f32[8,128]{1,0:T(8,128)S(1)}, f32[8,128]{1,0:T(8,128)S(1)}, u32[]{:S(2)}, u32[]{:S(2)}) %collective-permute-start.30) | collective-permute-done | bytes 4128 | tf_op jit(solution)/shard_map/ppermute | solution.py:313
  94.9 4.7 %collective-permute-start.31 = (f32[8,128]{1,0:T(8,128)S(1)}, f32[8,128]{1,0:T(8,128)S(1)}, u32[]{:S(2)}, u32[]{:S(2)}) collective-permute-start(f32[8,128]{1,0:T(8,128)S(1)} %add.38), channel_id=1, source_target_pairs={{0,4},{1,5},{2,6},{3,7},{4,0},{5,1},{6,2},{7,3},{8,12},{9,13},{10,... | collective-permute-start | bytes 12296 | tf_op jit(solution)/shard_map/ppermute | solution.py:313
  99.5 1.6 %collective-permute-done.31 = f32[8,128]{1,0:T(8,128)S(1)} collective-permute-done((f32[8,128]{1,0:T(8,128)S(1)}, f32[8,128]{1,0:T(8,128)S(1)}, u32[]{:S(2)}, u32[]{:S(2)}) %collective-permute-start.31) | collective-permute-done | bytes 4128 | tf_op jit(solution)/shard_map/ppermute | solution.py:313
  101.1 1.3 %collective-permute-start.32 = (f32[8,128]{1,0:T(8,128)S(1)}, f32[8,128]{1,0:T(8,128)S(1)}, u32[]{:S(2)}, u32[]{:S(2)}) collective-permute-start(f32[8,128]{1,0:T(8,128)S(1)} %add.40), channel_id=1, source_target_pairs={{0,12},{1,13},{2,14},{3,15},{4,8},{5,9},{6,10},{7,11},{8,4},{9,5},... | collective-permute-start | bytes 12296 | tf_op jit(solution)/shard_map/ppermute | solution.py:313
  102.4 3.5 %collective-permute-done.32 = f32[8,128]{1,0:T(8,128)S(1)} collective-permute-done((f32[8,128]{1,0:T(8,128)S(1)}, f32[8,128]{1,0:T(8,128)S(1)}, u32[]{:S(2)}, u32[]{:S(2)}) %collective-permute-start.32) | collective-permute-done | bytes 4128 | tf_op jit(solution)/shard_map/ppermute | solution.py:313
  105.9 5.3 %apply.1 = bf16[12288,128]{1,0:T(8,128)(2,1)} custom-call(bf16[768,1024]{1,0:T(8,128)(2,1)S(1)} %get-tuple-element.19.re_ref, bf16[768,1024]{1,0:T(8,128)(2,1)S(1)} %get-tuple-element.20.im_ref, f32[1,1024]{1,0:T(1,128)S(1)} %get-tuple-element.23.phase_ref, f32[8,128]{1,0:T(8,128)S(1)} %select_add_fusion.before_ref), custom_call_target="tpu_custom_call" | custom-call | tf_op jit(solution)/shard_map/apply/pallas_call | solution.py:293
  (82 shorter events, 10.2 us)
Async XLA Ops:
  0.9 9.1 %collective-permute-start.15 = (bf16[128,128]{1,0:T(8,128)(2,1)S(1)}, bf16[128,128]{1,0:T(8,128)(2,1)S(1)}, u32[]{:S(2)}, u32[]{:S(2)}) collective-permute-start(bf16[128,128]{1,0:T(8,128)(2,1)S(1)} %get-tuple-element.26), channel_id=1, source_target_pairs={{0,16},{16,32},{32,48},{48,64},{64,80},{80,96},{96,112},{1,17},{17... | collective-permute-start | bytes 98312 | tf_op jit(solution)/shard_map/ppermute | solution.py:336
  4.8 22.5 %collective-permute-start.3 = (bf16[128,1536]{1,0:T(8,128)(2,1)}, bf16[128,1536]{1,0:T(8,128)(2,1)S(1)}, u32[]{:S(2)}, u32[]{:S(2)}) collective-permute-start(bf16[128,1536]{1,0:T(8,128)(2,1)} %bitcast.11), channel_id=1, source_target_pairs={{0,12},{1,13},{2,14},{3,15},{4,0},{5,1},{6,2},{7,3},{8,4},{9,5},{1... | collective-permute-start | bytes 1179656 | tf_op jit(solution)/shard_map/ppermute | solution.py:313
  7.9 19.4 %collective-permute-start.7 = (bf16[128,1536]{1,0:T(8,128)(2,1)}, bf16[128,1536]{1,0:T(8,128)(2,1)}, u32[]{:S(2)}, u32[]{:S(2)}) collective-permute-start(bf16[128,1536]{1,0:T(8,128)(2,1)} %bitcast.12), channel_id=1, source_target_pairs={{0,4},{1,5},{2,6},{3,7},{4,8},{5,9},{6,10},{7,11},{8,12},{9,13},{1... | collective-permute-start | bytes 1179656 | tf_op jit(solution)/shard_map/ppermute | solution.py:313
  7.9 7.9 %collective-permute-start.16 = (bf16[128,128]{1,0:T(8,128)(2,1)S(1)}, bf16[128,128]{1,0:T(8,128)(2,1)S(1)}, u32[]{:S(2)}, u32[]{:S(2)}) collective-permute-start(bf16[128,128]{1,0:T(8,128)(2,1)S(1)} %get-tuple-element.25), channel_id=1, source_target_pairs={{16,0},{32,16},{48,32},{64,48},{80,64},{96,80},{112,96},{17,1},{33... | collective-permute-start | bytes 98312 | tf_op jit(solution)/shard_map/ppermute | solution.py:337
  16.4 6.4 %collective-permute-start.17 = (bf16[128,256]{1,0:T(8,128)(2,1)}, bf16[128,256]{1,0:T(8,128)(2,1)}, u32[]{:S(2)}, u32[]{:S(2)}) collective-permute-start(bf16[128,256]{1,0:T(8,128)(2,1)} %constant_dynamic-update-slice_fusion), channel_id=1, source_target_pairs={{0,2},{1,3},{2,0},{3,1},{4,6},{5,7},{6,4},{7,5},{8,10},{9,11},{10,... | collective-permute-start | bytes 196616 | tf_op jit(solution)/shard_map/ppermute | solution.py:313
  20.0 17.3 %collective-permute-start.1 = (bf16[128,1536]{1,0:T(8,128)(2,1)}, bf16[128,1536]{1,0:T(8,128)(2,1)}, u32[]{:S(2)}, u32[]{:S(2)}) collective-permute-start(bf16[128,1536]{1,0:T(8,128)(2,1)} %bitcast.13), channel_id=1, source_target_pairs={{0,2},{1,3},{2,0},{3,1},{4,6},{5,7},{6,4},{7,5},{8,10},{9,11},{10,... | collective-permute-start | bytes 1179656 | tf_op jit(solution)/shard_map/ppermute | solution.py:313
  20.0 20.5 %collective-permute-start = (bf16[128,1536]{1,0:T(8,128)(2,1)}, bf16[128,1536]{1,0:T(8,128)(2,1)}, u32[]{:S(2)}, u32[]{:S(2)}) collective-permute-start(bf16[128,1536]{1,0:T(8,128)(2,1)} %bitcast.14), channel_id=1, source_target_pairs={{0,1},{1,0},{2,3},{3,2},{4,5},{5,4},{6,7},{7,6},{8,9},{9,8},{10,11... | collective-permute-start | bytes 1179656 | tf_op jit(solution)/shard_map/ppermute | solution.py:313
  23.7 7.5 %collective-permute-start.19 = (bf16[2,128,256]{2,1,0:T(8,128)(2,1)S(1)}, bf16[2,128,256]{2,1,0:T(8,128)(2,1)S(1)}, u32[]{:S(2)}, u32[]{:S(2)}) collective-permute-start(bf16[2,128,256]{2,1,0:T(8,128)(2,1)S(1)} %pad_maximum_fusion.refs_19_), channel_id=1, source_target_pairs={{0,12},{1,13},{2,14},{3,15},{4,0},{5,1},{6,2},{7,3},{8,4},{9,5},{1... | collective-permute-start | bytes 393224 | tf_op jit(solution)/shard_map/ppermute | solution.py:313
  27.3 6.7 %collective-permute-start.21 = (bf16[2,128,256]{2,1,0:T(8,128)(2,1)S(1)}, bf16[2,128,256]{2,1,0:T(8,128)(2,1)}, u32[]{:S(2)}, u32[]{:S(2)}) collective-permute-start(bf16[2,128,256]{2,1,0:T(8,128)(2,1)S(1)} %pad_maximum_fusion.refs_19_), channel_id=1, source_target_pairs={{0,8},{1,9},{2,10},{3,11},{4,12},{5,13},{6,14},{7,15},{8,0},{9,1},... | collective-permute-start | bytes 393224 | tf_op jit(solution)/shard_map/ppermute | solution.py:313
  27.3 7.8 %collective-permute-start.23 = (bf16[2,128,256]{2,1,0:T(8,128)(2,1)S(1)}, bf16[2,128,256]{2,1,0:T(8,128)(2,1)}, u32[]{:S(2)}, u32[]{:S(2)}) collective-permute-start(bf16[2,128,256]{2,1,0:T(8,128)(2,1)S(1)} %pad_maximum_fusion.refs_19_), channel_id=1, source_target_pairs={{0,4},{1,5},{2,6},{3,7},{4,8},{5,9},{6,10},{7,11},{8,12},{9,13},{1... | collective-permute-start | bytes 393224 | tf_op jit(solution)/shard_map/ppermute | solution.py:313
  31.2 9.8 %collective-permute-start.8 = (bf16[128,1536]{1,0:T(8,128)(2,1)}, bf16[128,1536]{1,0:T(8,128)(2,1)}, u32[]{:S(2)}, u32[]{:S(2)}) collective-permute-start(bf16[128,1536]{1,0:T(8,128)(2,1)} %broadcast_select_fusion), channel_id=1, source_target_pairs={{0,4},{1,13},{2,6},{3,15},{4,8},{5,1},{6,10},{7,3},{8,12},{9,5},{1... | collective-permute-start | bytes 1179656 | tf_op jit(solution)/shard_map/ppermute | solution.py:313
  34.0 1.3 %collective-permute-start.18 = (bf16[2,128,256]{2,1,0:T(8,128)(2,1)S(1)}, bf16[2,128,256]{2,1,0:T(8,128)(2,1)S(1)}, u32[]{:S(2)}, u32[]{:S(2)}) collective-permute-start(bf16[2,128,256]{2,1,0:T(8,128)(2,1)S(1)} %pad_maximum_fusion.refs_19_), channel_id=1, source_target_pairs={{0,1},{1,0},{2,3},{3,2},{4,5},{5,4},{6,7},{7,6},{8,9},{9,8},{10,11... | collective-permute-start | bytes 393224 | tf_op jit(solution)/shard_map/ppermute | solution.py:313
  35.1 1.3 %collective-permute-start.20 = (bf16[2,128,256]{2,1,0:T(8,128)(2,1)S(1)}, bf16[2,128,256]{2,1,0:T(8,128)(2,1)S(1)}, u32[]{:S(2)}, u32[]{:S(2)}) collective-permute-start(bf16[2,128,256]{2,1,0:T(8,128)(2,1)S(1)} %collective-permute-done.19.refs_21_), channel_id=1, source_target_pairs={{0,1},{1,0},{2,3},{3,2},{4,5},{5,4},{6,7},{7,6},{8,9},{9,8},{10,11... | collective-permute-start | bytes 393224 | tf_op jit(solution)/shard_map/ppermute | solution.py:313
  35.4 1.9 %collective-permute-start.22 = (bf16[2,128,256]{2,1,0:T(8,128)(2,1)}, bf16[2,128,256]{2,1,0:T(8,128)(2,1)}, u32[]{:S(2)}, u32[]{:S(2)}) collective-permute-start(bf16[2,128,256]{2,1,0:T(8,128)(2,1)} %collective-permute-done.21.refs_23_), channel_id=1, source_target_pairs={{0,1},{1,0},{2,3},{3,2},{4,5},{5,4},{6,7},{7,6},{8,9},{9,8},{10,11... | collective-permute-start | bytes 393224 | tf_op jit(solution)/shard_map/ppermute | solution.py:313
  37.1 3.4 %collective-permute-start.24 = (bf16[2,128,256]{2,1,0:T(8,128)(2,1)}, bf16[2,128,256]{2,1,0:T(8,128)(2,1)}, u32[]{:S(2)}, u32[]{:S(2)}) collective-permute-start(bf16[2,128,256]{2,1,0:T(8,128)(2,1)} %collective-permute-done.23.refs_25_), channel_id=1, source_target_pairs={{0,1},{1,0},{2,3},{3,2},{4,5},{5,4},{6,7},{7,6},{8,9},{9,8},{10,11... | collective-permute-start | bytes 393224 | tf_op jit(solution)/shard_map/ppermute | solution.py:313
  37.2 12.9 %collective-permute-start.13 = (bf16[128,1536]{1,0:T(8,128)(2,1)}, bf16[128,1536]{1,0:T(8,128)(2,1)}, u32[]{:S(2)}, u32[]{:S(2)}) collective-permute-start(bf16[128,1536]{1,0:T(8,128)(2,1)} %collective-permute-done.1.refs_5_), channel_id=1, source_target_pairs={{0,4},{1,5},{2,6},{3,7},{4,8},{5,9},{6,10},{7,11},{8,12},{9,13},{1... | collective-permute-start | bytes 1179656 | tf_op jit(solution)/shard_map/ppermute | solution.py:313
  37.3 12.9 %collective-permute-start.5 = (bf16[128,1536]{1,0:T(8,128)(2,1)}, bf16[128,1536]{1,0:T(8,128)(2,1)}, u32[]{:S(2)}, u32[]{:S(2)}) collective-permute-start(bf16[128,1536]{1,0:T(8,128)(2,1)} %collective-permute-done.1.refs_5_), channel_id=1, source_target_pairs={{0,12},{1,13},{2,14},{3,15},{4,0},{5,1},{6,2},{7,3},{8,4},{9,5},{1... | collective-permute-start | bytes 1179656 | tf_op jit(solution)/shard_map/ppermute | solution.py:313
  40.5 10.2 %collective-permute-start.2 = (bf16[128,1536]{1,0:T(8,128)(2,1)}, bf16[128,1536]{1,0:T(8,128)(2,1)S(1)}, u32[]{:S(2)}, u32[]{:S(2)}) collective-permute-start(bf16[128,1536]{1,0:T(8,128)(2,1)} %collective-permute-done.1.refs_5_), channel_id=1, source_target_pairs={{0,1},{1,0},{2,3},{3,2},{4,5},{5,4},{6,7},{7,6},{8,9},{9,8},{10,11... | collective-permute-start | bytes 1179656 | tf_op jit(solution)/shard_map/ppermute | solution.py:313
  40.5 10.3 %collective-permute-start.12 = (bf16[128,1536]{1,0:T(8,128)(2,1)}, bf16[128,1536]{1,0:T(8,128)(2,1)S(1)}, u32[]{:S(2)}, u32[]{:S(2)}) collective-permute-start(bf16[128,1536]{1,0:T(8,128)(2,1)} %collective-permute-done.7.refs_15_), channel_id=1, source_target_pairs={{0,1},{1,0},{2,3},{3,2},{4,5},{5,4},{6,7},{7,6},{8,9},{9,8},{10,11... | collective-permute-start | bytes 1179656 | tf_op jit(solution)/shard_map/ppermute | solution.py:313
  41.0 13.4 %collective-permute-start.10 = (bf16[128,1536]{1,0:T(8,128)(2,1)}, bf16[128,1536]{1,0:T(8,128)(2,1)}, u32[]{:S(2)}, u32[]{:S(2)}) collective-permute-start(bf16[128,1536]{1,0:T(8,128)(2,1)} %collective-permute-done.8.refs_11_), channel_id=1, source_target_pairs={{0,2},{1,3},{2,0},{3,1},{4,6},{5,7},{6,4},{7,5},{8,10},{9,11},{10,... | collective-permute-start | bytes 1179656 | tf_op jit(solution)/shard_map/ppermute | solution.py:313
  50.2 10.6 %collective-permute-start.4 = (bf16[128,1536]{1,0:T(8,128)(2,1)S(1)}, bf16[128,1536]{1,0:T(8,128)(2,1)}, u32[]{:S(2)}, u32[]{:S(2)}) collective-permute-start(bf16[128,1536]{1,0:T(8,128)(2,1)S(1)} %collective-permute-done.3.refs_7_), channel_id=1, source_target_pairs={{0,1},{1,0},{2,3},{3,2},{4,5},{5,4},{6,7},{7,6},{8,9},{9,8},{10,11... | collective-permute-start | bytes 1179656 | tf_op jit(solution)/shard_map/ppermute | solution.py:313
  50.2 10.6 %collective-permute-start.9 = (bf16[128,1536]{1,0:T(8,128)(2,1)}, bf16[128,1536]{1,0:T(8,128)(2,1)}, u32[]{:S(2)}, u32[]{:S(2)}) collective-permute-start(bf16[128,1536]{1,0:T(8,128)(2,1)} %collective-permute-done.8.refs_11_), channel_id=1, source_target_pairs={{0,1},{1,0},{2,3},{3,2},{4,5},{5,4},{6,7},{7,6},{8,9},{9,8},{10,11... | collective-permute-start | bytes 1179656 | tf_op jit(solution)/shard_map/ppermute | solution.py:313
  50.7 10.1 %collective-permute-start.14 = (bf16[128,1536]{1,0:T(8,128)(2,1)}, bf16[128,1536]{1,0:T(8,128)(2,1)}, u32[]{:S(2)}, u32[]{:S(2)}) collective-permute-start(bf16[128,1536]{1,0:T(8,128)(2,1)} %collective-permute-done.13.refs_17_), channel_id=1, source_target_pairs={{0,1},{1,0},{2,3},{3,2},{4,5},{5,4},{6,7},{7,6},{8,9},{9,8},{10,11... | collective-permute-start | bytes 1179656 | tf_op jit(solution)/shard_map/ppermute | solution.py:313
  50.8 10.0 %collective-permute-start.6 = (bf16[128,1536]{1,0:T(8,128)(2,1)}, bf16[128,1536]{1,0:T(8,128)(2,1)}, u32[]{:S(2)}, u32[]{:S(2)}) collective-permute-start(bf16[128,1536]{1,0:T(8,128)(2,1)} %collective-permute-done.5.refs_9_), channel_id=1, source_target_pairs={{0,1},{1,0},{2,3},{3,2},{4,5},{5,4},{6,7},{7,6},{8,9},{9,8},{10,11... | collective-permute-start | bytes 1179656 | tf_op jit(solution)/shard_map/ppermute | solution.py:313
  54.4 6.4 %collective-permute-start.11 = (bf16[128,1536]{1,0:T(8,128)(2,1)}, bf16[128,1536]{1,0:T(8,128)(2,1)}, u32[]{:S(2)}, u32[]{:S(2)}) collective-permute-start(bf16[128,1536]{1,0:T(8,128)(2,1)} %collective-permute-done.10.refs_13_), channel_id=1, source_target_pairs={{0,1},{1,0},{2,3},{3,2},{4,5},{5,4},{6,7},{7,6},{8,9},{9,8},{10,11... | collective-permute-start | bytes 1179656 | tf_op jit(solution)/shard_map/ppermute | solution.py:313
  67.0 7.0 %collective-permute-start.25 = (f32[2,768]{1,0:T(2,128)S(1)}, f32[2,768]{1,0:T(2,128)S(1)}, u32[]{:S(2)}, u32[]{:S(2)}) collective-permute-start(f32[2,768]{1,0:T(2,128)S(1)} %slice.11), channel_id=1, source_target_pairs={{1,0},{2,1},{3,2},{4,3},{5,4},{6,5},{7,6},{8,7},{9,8},{10,9},{11,1... | collective-permute-start | bytes 18440 | tf_op jit(solution)/shard_map/ppermute | solution.py:373
  74.1 4.1 %collective-permute-start.26 = (f32[8,1024]{1,0:T(8,128)S(1)}, f32[8,1024]{1,0:T(8,128)S(1)}, u32[]{:S(2)}, u32[]{:S(2)}) collective-permute-start(f32[8,1024]{1,0:T(8,128)S(1)} %shard_map.56), channel_id=1, source_target_pairs={{0,16},{16,0},{32,48},{48,32},{64,80},{80,64},{96,112},{112,96},{1... | collective-permute-start | bytes 98312 | tf_op jit(solution)/shard_map/ppermute | solution.py:313
  78.2 5.1 %collective-permute-start.27 = (f32[8,1024]{1,0:T(8,128)S(1)}, f32[8,1024]{1,0:T(8,128)S(1)}, u32[]{:S(2)}, u32[]{:S(2)}) collective-permute-start(f32[8,1024]{1,0:T(8,128)S(1)} %add.34), channel_id=1, source_target_pairs={{0,48},{16,32},{32,16},{48,0},{64,112},{80,96},{96,80},{112,64},{1... | collective-permute-start | bytes 98312 | tf_op jit(solution)/shard_map/ppermute | solution.py:313
  83.3 3.9 %collective-permute-start.28 = (f32[8,1024]{1,0:T(8,128)S(1)}, f32[8,1024]{1,0:T(8,128)S(1)}, u32[]{:S(2)}, u32[]{:S(2)}) collective-permute-start(f32[8,1024]{1,0:T(8,128)S(1)} %add.35.stats_ref), channel_id=1, source_target_pairs={{0,64},{16,80},{32,96},{48,112},{64,0},{80,16},{96,32},{112,48},{1... | collective-permute-start | bytes 98312 | tf_op jit(solution)/shard_map/ppermute | solution.py:313
  89.2 5.7 %collective-permute-start.30 = (f32[8,128]{1,0:T(8,128)S(1)}, f32[8,128]{1,0:T(8,128)S(1)}, u32[]{:S(2)}, u32[]{:S(2)}) collective-permute-start(f32[8,128]{1,0:T(8,128)S(1)} %add.36), channel_id=1, source_target_pairs={{0,2},{1,3},{2,0},{3,1},{4,6},{5,7},{6,4},{7,5},{8,10},{9,11},{10,... | collective-permute-start | bytes 12296 | tf_op jit(solution)/shard_map/ppermute | solution.py:313
  94.9 6.3 %collective-permute-start.31 = (f32[8,128]{1,0:T(8,128)S(1)}, f32[8,128]{1,0:T(8,128)S(1)}, u32[]{:S(2)}, u32[]{:S(2)}) collective-permute-start(f32[8,128]{1,0:T(8,128)S(1)} %add.38), channel_id=1, source_target_pairs={{0,4},{1,5},{2,6},{3,7},{4,0},{5,1},{6,2},{7,3},{8,12},{9,13},{10,... | collective-permute-start | bytes 12296 | tf_op jit(solution)/shard_map/ppermute | solution.py:313
  101.1 4.8 %collective-permute-start.32 = (f32[8,128]{1,0:T(8,128)S(1)}, f32[8,128]{1,0:T(8,128)S(1)}, u32[]{:S(2)}, u32[]{:S(2)}) collective-permute-start(f32[8,128]{1,0:T(8,128)S(1)} %add.40), channel_id=1, source_target_pairs={{0,12},{1,13},{2,14},{3,15},{4,8},{5,9},{6,10},{7,11},{8,4},{9,5},... | collective-permute-start | bytes 12296 | tf_op jit(solution)/shard_map/ppermute | solution.py:313
  (12 other events, 193.9 us)

commit v3 on v2

--- a/solution.py
+++ b/solution.py
@@ -11,6 +11,7 @@
 VMEM = pl.BlockSpec(memory_space=pltpu.VMEM)
 SMEM = pl.BlockSpec(memory_space=pltpu.SMEM)
 HBM = pl.BlockSpec(memory_space=pltpu.HBM)
+ANY = pl.BlockSpec(memory_space=pl.ANY)
 
 PIO2_HI = 1.5707964
 PIO2_LO = -4.371139e-8
@@ -106,17 +107,26 @@
     )(pltpu.with_memory_space_constraint(phases, pltpu.HBM))
 
 
-def focus_kernel(n_slots, place_ref, ping_ref, start_ref, *refs):
+def focus_kernel(n_slots, me_ref, owner_ref, start_ref, *refs):
     slots = refs[:n_slots]
     ends = refs[n_slots : n_slots + n_slots // 2]
-    interp_ref, weight_hbm, out_ref, edge_ref, window, weight_ref, sems = refs[
+    interp_ref, weight_hbm, out_ref, edge_ref, window, weight_ref, place_ref, ping_ref, sems = refs[
         n_slots + n_slots // 2 :
     ]
+    me = me_ref[0]
     pings, range_cells, band = interp_ref.shape
     rows, width = slots[0].shape
-    blocks = start_ref.shape[0] // pings
+    blocks = start_ref.shape[0]
     cells = range_cells // blocks
     span = band + LANES
+    for s in range(n_slots):
+        place_ref[s] = -1
+    owners = [owner_ref[p] for p in range(pings)]
+    relative = [((((o >> 2) - (me >> 2)) & 3) << 2) | ((o ^ me) & 3) for o in owners]
+    for p in range(pings):
+        k = sum((relative[q] < relative[p]).astype(jnp.int32) for q in range(pings) if q != p)
+        place_ref[relative[p]] = k
+        ping_ref[k] = p
     for s in range(n_slots):
         k = place_ref[s]
         end = ends[s // 4 * 2 + s % 2].at[s // 2 % 2]
@@ -138,7 +148,7 @@
         p = ping_ref[k]
         column = pl.ds(pl.multiple_of(p * rows, LANES), rows)
         for b in range(blocks):
-            start = start_ref[b * pings + p]
+            start = start_ref[b, 0, p]
             aligned = jnp.minimum((start // LANES) * LANES, width + 2 * GUARD - span)
             aligned = pl.multiple_of(aligned, LANES)
             wide = window[k, :, pl.ds(aligned, span)]
@@ -157,12 +167,12 @@
     edge_ref[2:4, :] = got[LANES - 2 :].astype(jnp.bfloat16).astype(jnp.float32)
 
 
-def focus(slots, ends, places, ping_at, starts, interp, edge_weights):
+def focus(slots, ends, me, owner_map, starts, interp, edge_weights):
     pings, range_cells, _ = interp.shape
     rows, width = slots[0].shape
     call = pl.pallas_call(
         lambda *refs: focus_kernel(len(slots), *refs),
-        in_specs=[SMEM] * 3 + [HBM] * (len(slots) + len(ends)) + [VMEM, HBM],
+        in_specs=[SMEM] * 3 + [ANY] * (len(slots) + len(ends)) + [VMEM, HBM],
         out_specs=[VMEM] * 2,
         out_shape=[
             jax.ShapeDtypeStruct((range_cells, pings * rows), jnp.bfloat16),
@@ -171,14 +181,15 @@
         scratch_shapes=[
             pltpu.VMEM((pings, rows, width + 2 * GUARD), jnp.bfloat16),
             pltpu.VMEM(edge_weights.shape, jnp.bfloat16),
+            pltpu.SMEM((len(slots),), jnp.int32),
+            pltpu.SMEM((pings,), jnp.int32),
             pltpu.SemaphoreType.DMA((pings + 1,)),
         ],
         compiler_params=pltpu.CompilerParams(vmem_limit_bytes=16 << 20),
         name="focus",
     )
-    local = [pltpu.with_memory_space_constraint(x, pltpu.HBM) for x in (*slots, *ends)]
     edge_weights = pltpu.with_memory_space_constraint(edge_weights, pltpu.HBM)
-    return call(places, ping_at, starts, *local, interp, edge_weights)
+    return call(me, owner_map, starts, *slots, *ends, interp, edge_weights)
 
 
 def image_kernel(focused_ref, re_ref, im_ref, out_re, out_im, stats_ref):
@@ -228,7 +239,7 @@
     out = jax.ShapeDtypeStruct((rows, cells), jnp.bfloat16)
     return kernel_call(
         image_kernel,
-        [out, out, jax.ShapeDtypeStruct((8, cells), jnp.float32)],
+        [out, out, jax.ShapeDtypeStruct((4, cells), jnp.float32)],
         focused,
         steer_re,
         steer_im,
@@ -265,8 +276,9 @@
 
 
 def apply_kernel(re_ref, im_ref, phase_ref, before_ref, out_ref, scratch, cos_ref, sin_ref):
-    step = scratch.shape[0] * LANES // (2 * re_ref.shape[1])
     tiles = re_ref.shape[1] // LANES
+    step = out_ref.shape[0] // (2 * tiles)
+    stride = scratch.shape[0] // step
 
     @pl.when(pl.program_id(0) == 0)
     def _():
@@ -281,9 +293,11 @@
         b = im_ref[here, part].astype(jnp.float32)
         cosine = cos_ref[:, part]
         sine = sin_ref[:, part]
-        scratch[pl.ds(2 * t, step, stride=2 * tiles), :] = a * cosine + b * sine
-        scratch[pl.ds(2 * t + 1, step, stride=2 * tiles), :] = b * cosine - a * sine
-    out_ref[...] = scratch[...].astype(jnp.bfloat16)
+        scratch[pl.ds(2 * t, step, stride=stride), :] = a * cosine + b * sine
+        scratch[pl.ds(2 * t + 1, step, stride=stride), :] = b * cosine - a * sine
+    for r in range(step):
+        cell = scratch[r * stride : r * stride + 2 * tiles, :]
+        out_ref[2 * tiles * r : 2 * tiles * (r + 1), :] = cell.astype(jnp.bfloat16)
 
 
 def apply(real, imag, phase, before):
@@ -297,7 +311,7 @@
         out_specs=pl.BlockSpec((step * 2 * tiles, LANES), lambda i: (i, 0)),
         out_shape=jax.ShapeDtypeStruct((rows * 2 * tiles, LANES), jnp.bfloat16),
         scratch_shapes=[
-            pltpu.VMEM((step * 2 * tiles, LANES), jnp.float32),
+            pltpu.VMEM((step * (2 * tiles + 2), LANES), jnp.float32),
             pltpu.VMEM((1, cells), jnp.float32),
             pltpu.VMEM((1, cells), jnp.float32),
         ],
@@ -329,14 +343,40 @@
     return send(x, "az", lambda i: i ^ 1)
 
 
+def join_kernel(low_ref, high_ref, out_ref):
+    out_ref[:, :GUARD] = low_ref[...]
+    out_ref[:, GUARD:] = high_ref[...]
+
+
+def select_kernel(me_ref, above_ref, below_ref, out_ref):
+    even = me_ref[0] & 1 == 0
+
+    @pl.when(even)
+    def _():
+        out_ref[...] = above_ref[...]
+
+    @pl.when(jnp.logical_not(even))
+    def _():
+        out_ref[...] = below_ref[...]
+
+
 def spread(block):
     n = lax.axis_size("rng")
     width = block.shape[1]
     above, below, other = up(block), down(block), across(block)
     low = lax.ppermute(block[:, width - GUARD :], "rng", [(i, i + 1) for i in range(n - 1)])
     high = lax.ppermute(block[:, :GUARD], "rng", [(i + 1, i) for i in range(n - 1)])
-    ends = jnp.concatenate([low, high], axis=1)
-    passed = jnp.where(lax.axis_index("az") & 1 == 0, above, below)
+    (ends,) = kernel_call(
+        join_kernel, [jax.ShapeDtypeStruct((block.shape[0], 2 * GUARD), jnp.bfloat16)], low, high
+    )
+    (passed,) = kernel_call(
+        select_kernel,
+        [jax.ShapeDtypeStruct(block.shape, jnp.bfloat16)],
+        lax.axis_index("az").reshape(1),
+        above,
+        below,
+        scalars=1,
+    )
     opposite = send(passed, "az", lambda i: (i + (4, -4)[i & 1]) % 16)
     slots = {(0, 0): block, (3, 0): above, (1, 0): below, (2, 0): opposite, (0, 1): other}
     slots[3, 1] = up(other)
@@ -357,18 +397,10 @@
     hydrophones, samples = echoes.shape[2:]
     n_az = lax.axis_size("az")
     me = lax.axis_index("az")
-    relative = ((((owner_map >> 2) - (me >> 2)) & 3) << 2) | ((owner_map ^ me) & 3)
-    slot = jnp.arange(n_az, dtype=jnp.int32)
-    place = jnp.sum(relative[None, :] < relative[:, None], axis=1).astype(jnp.int32)
-    matches = relative[None, :] == slot[:, None]
-    places = jnp.sum(jnp.where(matches, place[None, :] + 1, 0), axis=1) - 1
-    number = jnp.arange(owner_map.shape[0], dtype=jnp.int32)
-    ping_at = jnp.sum(jnp.where(place[None, :] == number[:, None], number[None, :], 0), axis=1)
-    starts = band_start.reshape(-1)
     steer_re, steer_im, edge_weights = steering(steer_phase)
     slots, ends = spread(echoes[0].reshape(2 * hydrophones, samples))
     focused, edges = focus(
-        slots, ends, places, ping_at, starts, interp[:, 0], edge_weights
+        slots, ends, me.reshape(1), owner_map, band_start, interp[:, 0], edge_weights
     )
     halo = lax.ppermute(edges[:2], "az", [(i + 1, i) for i in range(n_az - 1)])
     real, imag, stats = image(focused, steer_re, steer_im)

time: 111 us -> 105 us (0.946)
  other arithmetic: 5.01 us -> 0.69 us
  waiting for transfers between devices: 40.9 us -> 44.7 us
  starting transfers between devices: 38.9 us -> 36.3 us
  local copies, waits for them, and re-layouts: 2.94 us -> 0.86 us
    ppermute x30, waiting for transfers between devices: 35.7 us -> 38.9 us  [send(): return lax.ppermute(x, axis, [(i, move(i)) for i in range(n)])]
    ppermute x30, starting transfers between devices: 31.7 us -> 29.1 us  [send(): return lax.ppermute(x, axis, [(i, move(i)) for i in range(n)])]
    select_n x1 -> x0, other arithmetic: 1.78 us -> none  [spread(): passed = jnp.where(lax.axis_index('az') & 1 == 0, above, below)]
    pallas_call x1, Pallas kernels: 5.25 us -> 3.54 us  [apply(): pl.pallas_call(apply_kernel, grid=(rows // step,), in_specs=[VMEM] * 4, o...]
    unnamed x23 -> x12, local copies, waits for them, and re-layouts: 1.31 us -> 0.03 us
    pallas_call x3 -> x5, Pallas kernels: 6.42 us -> 7.39 us  [kernel_call(): pl.pallas_call(body, in_specs=[SMEM] * scalars + [VMEM] * (len(args) - sc...]
  transfers between devices with their start and end apart: 33 -> 33, of which waited for: 16 -> 16; matrix products, arithmetic and copies ran while one was open for 6% -> 1% of each run, Pallas kernels for 10% -> 11%
where the time goes in v3:
time: 105 us
  waiting for transfers between devices  44.7 us (43%)
  starting transfers between devices  36.3 us (35%)
  Pallas kernels  22.4 us (21%)
    ppermute x30, waiting for transfers between devices, send(): return lax.ppermute(x, axis, [(i, move(i)) for i in range(n)])  38.9 us
    ppermute x30, starting transfers between devices, send(): return lax.ppermute(x, axis, [(i, move(i)) for i in range(n)])  29.1 us
    pallas_call x5, Pallas kernels, kernel_call(): pl.pallas_call(body, in_specs=[SMEM] * scalars + [VMEM] * (len(args) - sc...  7.39 us
    pallas_call x1, Pallas kernels, focus(): return call(me, owner_map, starts, *slots, *ends, interp, edge_weights)  6.08 us
    ppermute x1, waiting for transfers between devices, spread(): lax.ppermute(block[:, :GUARD], 'rng', [(i + 1, i) for i in range(n - 1)])  5.82 us
    pallas_call x1, Pallas kernels, steering(): pl.pallas_call(lambda *refs: steering_kernel(scale, *refs), in_specs=[HBM...  5.39 us
    ppermute x1, starting transfers between devices, spread(): lax.ppermute(block[:, width - GUARD:], 'rng', [(i, i + 1) for i in range(...  3.73 us
    pallas_call x1, Pallas kernels, apply(): pl.pallas_call(apply_kernel, grid=(rows // step,), in_specs=[VMEM] * 4, o...  3.54 us
  transfers between devices with their start and end apart: 33, of which 16 were waited for; matrix products, arithmetic and copies ran while one was open for 1% of the time, Pallas kernels for 11%

profile of v3, /device:TPU:6, one launch (start us, length us, event | category | flops | bytes accessed | tf_op | source)
XLA Modules:
  0.0 105.2 jit_solution(14263184841953959361)
XLA Ops:
  0.0 3.1 %collective-permute-start.3 = (bf16[128,1536]{1,0:T(8,128)(2,1)}, bf16[128,1536]{1,0:T(8,128)(2,1)S(1)}, u32[]{:S(2)}, u32[]{:S(2)}) collective-permute-start(bf16[128,1536]{1,0:T(8,128)(2,1)} %bitcast.11), channel_id=1, source_target_pairs={{0,12},{1,13},{2,14},{3,15},{4,0},{5,1},{6,2},{7,3},{8,4},{9,5},{1... | collective-permute-start | bytes 1179656 | tf_op jit(solution)/shard_map/ppermute | solution.py:327
  3.9 3.7 %collective-permute-start.15 = (bf16[128,128]{1,0:T(8,128)(2,1)S(1)}, bf16[128,128]{1,0:T(8,128)(2,1)S(1)}, u32[]{:S(2)}, u32[]{:S(2)}) collective-permute-start(bf16[128,128]{1,0:T(8,128)(2,1)S(1)} %get-tuple-element.26), channel_id=1, source_target_pairs={{0,16},{16,32},{32,48},{48,64},{64,80},{80,96},{96,112},{1,17},{17... | collective-permute-start | bytes 98312 | tf_op jit(solution)/shard_map/ppermute | solution.py:367
  7.7 2.1 %collective-permute-start.16 = (bf16[128,128]{1,0:T(8,128)(2,1)S(1)}, bf16[128,128]{1,0:T(8,128)(2,1)S(1)}, u32[]{:S(2)}, u32[]{:S(2)}) collective-permute-start(bf16[128,128]{1,0:T(8,128)(2,1)S(1)} %get-tuple-element.25), channel_id=1, source_target_pairs={{16,0},{32,16},{48,32},{64,48},{80,64},{96,80},{112,96},{17,1},{33... | collective-permute-start | bytes 98312 | tf_op jit(solution)/shard_map/ppermute | solution.py:368
  9.8 5.8 %collective-permute-done.16.high_ref = bf16[128,128]{1,0:T(8,128)(2,1)S(1)} collective-permute-done((bf16[128,128]{1,0:T(8,128)(2,1)S(1)}, bf16[128,128]{1,0:T(8,128)(2,1)S(1)}, u32[]{:S(2)}, u32[]{:S(2)}) %collective-permute-start.16) | collective-permute-done | bytes 32800 | tf_op jit(solution)/shard_map/ppermute | solution.py:368
  15.6 3.7 %collective-permute-start.17 = (bf16[128,256]{1,0:T(8,128)(2,1)S(1)}, bf16[128,256]{1,0:T(8,128)(2,1)S(1)}, u32[]{:S(2)}, u32[]{:S(2)}) collective-permute-start(bf16[128,256]{1,0:T(8,128)(2,1)S(1)} %shard_map.56), channel_id=1, source_target_pairs={{0,2},{1,3},{2,0},{3,1},{4,6},{5,7},{6,4},{7,5},{8,10},{9,11},{10,... | collective-permute-start | bytes 196616 | tf_op jit(solution)/shard_map/ppermute | solution.py:327
  19.3 2.2 %collective-permute-done.17 = bf16[128,256]{1,0:T(8,128)(2,1)S(1)} collective-permute-done((bf16[128,256]{1,0:T(8,128)(2,1)S(1)}, bf16[128,256]{1,0:T(8,128)(2,1)S(1)}, u32[]{:S(2)}, u32[]{:S(2)}) %collective-permute-start.17) | collective-permute-done | bytes 65568 | tf_op jit(solution)/shard_map/ppermute | solution.py:327
  22.2 3.2 %collective-permute-start.19 = (bf16[2,128,256]{2,1,0:T(8,128)(2,1)}, bf16[2,128,256]{2,1,0:T(8,128)(2,1)}, u32[]{:S(2)}, u32[]{:S(2)}) collective-permute-start(bf16[2,128,256]{2,1,0:T(8,128)(2,1)} %pad_maximum_fusion.refs_19_), channel_id=1, source_target_pairs={{0,12},{1,13},{2,14},{3,15},{4,0},{5,1},{6,2},{7,3},{8,4},{9,5},{1... | collective-permute-start | bytes 393224 | tf_op jit(solution)/shard_map/ppermute | solution.py:327
  25.4 3.5 %collective-permute-start.1 = (bf16[128,1536]{1,0:T(8,128)(2,1)}, bf16[128,1536]{1,0:T(8,128)(2,1)}, u32[]{:S(2)}, u32[]{:S(2)}) collective-permute-start(bf16[128,1536]{1,0:T(8,128)(2,1)} %bitcast.14), channel_id=1, source_target_pairs={{0,2},{1,3},{2,0},{3,1},{4,6},{5,7},{6,4},{7,5},{8,10},{9,11},{10,... | collective-permute-start | bytes 1179656 | tf_op jit(solution)/shard_map/ppermute | solution.py:327
  28.9 0.9 collective-permute-start.23
  29.8 1.0 shard_map.55
  30.8 2.7 %collective-permute-start.8 = (bf16[128,1536]{1,0:T(8,128)(2,1)S(1)}, bf16[128,1536]{1,0:T(8,128)(2,1)S(1)}, u32[]{:S(2)}, u32[]{:S(2)}) collective-permute-start(bf16[128,1536]{1,0:T(8,128)(2,1)S(1)} %shard_map.55), channel_id=1, source_target_pairs={{0,4},{1,13},{2,6},{3,15},{4,8},{5,1},{6,10},{7,3},{8,12},{9,5},{1... | collective-permute-start | bytes 1179656 | tf_op jit(solution)/shard_map/ppermute | solution.py:327
  33.5 2.2 %collective-permute-done.21.refs_23_ = bf16[2,128,256]{2,1,0:T(8,128)(2,1)S(1)} collective-permute-done((bf16[2,128,256]{2,1,0:T(8,128)(2,1)}, bf16[2,128,256]{2,1,0:T(8,128)(2,1)S(1)}, u32[]{:S(2)}, u32[]{:S(2)}) %collective-permute-start.21) | collective-permute-done | bytes 131104 | tf_op jit(solution)/shard_map/ppermute | solution.py:327
  35.7 1.1 %collective-permute-done.23.refs_25_ = bf16[2,128,256]{2,1,0:T(8,128)(2,1)S(1)} collective-permute-done((bf16[2,128,256]{2,1,0:T(8,128)(2,1)}, bf16[2,128,256]{2,1,0:T(8,128)(2,1)S(1)}, u32[]{:S(2)}, u32[]{:S(2)}) %collective-permute-start.23) | collective-permute-done | bytes 131104 | tf_op jit(solution)/shard_map/ppermute | solution.py:327
  37.4 0.9 collective-permute-done.20.refs_22_
  38.6 3.1 %collective-permute-start.5 = (bf16[128,1536]{1,0:T(8,128)(2,1)}, bf16[128,1536]{1,0:T(8,128)(2,1)S(1)}, u32[]{:S(2)}, u32[]{:S(2)}) collective-permute-start(bf16[128,1536]{1,0:T(8,128)(2,1)} %collective-permute-done.1.refs_5_), channel_id=1, source_target_pairs={{0,12},{1,13},{2,14},{3,15},{4,0},{5,1},{6,2},{7,3},{8,4},{9,5},{1... | collective-permute-start | bytes 1179656 | tf_op jit(solution)/shard_map/ppermute | solution.py:327
  42.6 8.7 %collective-permute-done.13.refs_17_ = bf16[128,1536]{1,0:T(8,128)(2,1)S(1)} collective-permute-done((bf16[128,1536]{1,0:T(8,128)(2,1)}, bf16[128,1536]{1,0:T(8,128)(2,1)S(1)}, u32[]{:S(2)}, u32[]{:S(2)}) %collective-permute-start.13) | collective-permute-done | bytes 393248 | tf_op jit(solution)/shard_map/ppermute | solution.py:327
  52.3 2.5 %collective-permute-done.10.refs_13_ = bf16[128,1536]{1,0:T(8,128)(2,1)S(1)} collective-permute-done((bf16[128,1536]{1,0:T(8,128)(2,1)S(1)}, bf16[128,1536]{1,0:T(8,128)(2,1)S(1)}, u32[]{:S(2)}, u32[]{:S(2)}) %collective-permute-start.10) | collective-permute-done | bytes 393248 | tf_op jit(solution)/shard_map/ppermute | solution.py:327
  54.9 5.4 %steering.1 = (bf16[1024,1024]{1,0:T(8,128)(2,1)}, bf16[1024,1024]{1,0:T(8,128)(2,1)}, bf16[128,1024]{1,0:T(8,128)(2,1)}) custom-call(f32[8,64,1024]{2,1,0:T(8,128)} %refs_0_.1), custom_call_target="tpu_custom_call" | custom-call | tf_op jit(solution)/shard_map/steering/pallas_call | solution.py:92
  60.4 6.1 %focus.1 = (bf16[768,1024]{1,0:T(8,128)(2,1)S(1)}, f32[4,768]{1,0:T(4,128)S(1)}) custom-call(s32[1]{0:T(128)} %bitcast.me_ref.refs_0_, s32[8]{0:T(128)S(1)} %copy-done.5, s32[6,1,8]{2,1,0:T(1,128)S(1)} %copy-done.4, bf16[128,1536]{1,0:T(8,128)(2,1)S(1)} %bitcast.16, bf16[128,1536]{1,0:T(8,128)(2,1)S(1)} %collective-permute-done.refs_4_, ...), custom_call_target="tpu_custom_call" | custom-call | tf_op jit(solution)/shard_map/focus/pallas_call | solution.py:192
  66.5 1.3 %collective-permute-start.25 = (f32[2,768]{1,0:T(2,128)S(1)}, f32[2,768]{1,0:T(2,128)S(1)}, u32[]{:S(2)}, u32[]{:S(2)}) collective-permute-start(f32[2,768]{1,0:T(2,128)S(1)} %slice.11), channel_id=1, source_target_pairs={{1,0},{2,1},{3,2},{4,3},{5,4},{6,5},{7,6},{8,7},{9,8},{10,9},{11,1... | collective-permute-start | bytes 18440 | tf_op jit(solution)/shard_map/ppermute | solution.py:405
  67.8 5.6 %shard_map.57 = (bf16[768,1024]{1,0:T(8,128)(2,1)S(1)}, bf16[768,1024]{1,0:T(8,128)(2,1)S(1)}, f32[4,1024]{1,0:T(4,128)S(1)}) custom-call(bf16[768,1024]{1,0:T(8,128)(2,1)S(1)} %get-tuple-element.16.focused_ref, bf16[1024,1024]{1,0:T(8,128)(2,1)S(1)} %copy-done.1, bf16[1024,1024]{1,0:T(8,128)(2,1)S(1)} %copy-done.2), custom_call_target="tpu_custom_call" | custom-call | tf_op jit(solution)/shard_map/pallas_call | solution.py:38
  73.6 3.7 %collective-permute-done.26 = f32[4,1024]{1,0:T(4,128)S(1)} collective-permute-done((f32[4,1024]{1,0:T(4,128)S(1)}, f32[4,1024]{1,0:T(4,128)S(1)}, u32[]{:S(2)}, u32[]{:S(2)}) %collective-permute-start.26) | collective-permute-done | bytes 16416 | tf_op jit(solution)/shard_map/ppermute | solution.py:327
  77.3 4.9 %collective-permute-done.27 = f32[4,1024]{1,0:T(4,128)S(1)} collective-permute-done((f32[4,1024]{1,0:T(4,128)S(1)}, f32[4,1024]{1,0:T(4,128)S(1)}, u32[]{:S(2)}, u32[]{:S(2)}) %collective-permute-start.27) | collective-permute-done | bytes 16416 | tf_op jit(solution)/shard_map/ppermute | solution.py:327
  82.3 3.7 %collective-permute-done.28.more_ref = f32[4,1024]{1,0:T(4,128)S(1)} collective-permute-done((f32[4,1024]{1,0:T(4,128)S(1)}, f32[4,1024]{1,0:T(4,128)S(1)}, u32[]{:S(2)}, u32[]{:S(2)}) %collective-permute-start.28) | collective-permute-done | bytes 16416 | tf_op jit(solution)/shard_map/ppermute | solution.py:327
  86.7 1.2 %collective-permute-done.29 = f32[8,128]{1,0:T(8,128)S(1)} collective-permute-done((f32[8,128]{1,0:T(8,128)S(1)}, f32[8,128]{1,0:T(8,128)S(1)}, u32[]{:S(2)}, u32[]{:S(2)}) %collective-permute-start.29) | collective-permute-done | bytes 4128 | tf_op jit(solution)/shard_map/ppermute | solution.py:327
  87.9 3.7 %collective-permute-start.30 = (f32[8,128]{1,0:T(8,128)S(1)}, f32[8,128]{1,0:T(8,128)S(1)}, u32[]{:S(2)}, u32[]{:S(2)}) collective-permute-start(f32[8,128]{1,0:T(8,128)S(1)} %add.26), channel_id=1, source_target_pairs={{0,2},{1,3},{2,0},{3,1},{4,6},{5,7},{6,4},{7,5},{8,10},{9,11},{10,... | collective-permute-start | bytes 12296 | tf_op jit(solution)/shard_map/ppermute | solution.py:327
  91.6 1.6 %collective-permute-done.30 = f32[8,128]{1,0:T(8,128)S(1)} collective-permute-done((f32[8,128]{1,0:T(8,128)S(1)}, f32[8,128]{1,0:T(8,128)S(1)}, u32[]{:S(2)}, u32[]{:S(2)}) %collective-permute-start.30) | collective-permute-done | bytes 4128 | tf_op jit(solution)/shard_map/ppermute | solution.py:327
  93.2 2.0 %collective-permute-start.31 = (f32[8,128]{1,0:T(8,128)S(1)}, f32[8,128]{1,0:T(8,128)S(1)}, u32[]{:S(2)}, u32[]{:S(2)}) collective-permute-start(f32[8,128]{1,0:T(8,128)S(1)} %add.28), channel_id=1, source_target_pairs={{0,4},{1,5},{2,6},{3,7},{4,0},{5,1},{6,2},{7,3},{8,12},{9,13},{10,... | collective-permute-start | bytes 12296 | tf_op jit(solution)/shard_map/ppermute | solution.py:327
  95.2 1.6 %collective-permute-done.31 = f32[8,128]{1,0:T(8,128)S(1)} collective-permute-done((f32[8,128]{1,0:T(8,128)S(1)}, f32[8,128]{1,0:T(8,128)S(1)}, u32[]{:S(2)}, u32[]{:S(2)}) %collective-permute-start.31) | collective-permute-done | bytes 4128 | tf_op jit(solution)/shard_map/ppermute | solution.py:327
  96.8 1.1 %collective-permute-start.32 = (f32[8,128]{1,0:T(8,128)S(1)}, f32[8,128]{1,0:T(8,128)S(1)}, u32[]{:S(2)}, u32[]{:S(2)}) collective-permute-start(f32[8,128]{1,0:T(8,128)S(1)} %add.30), channel_id=1, source_target_pairs={{0,12},{1,13},{2,14},{3,15},{4,8},{5,9},{6,10},{7,11},{8,4},{9,5},... | collective-permute-start | bytes 12296 | tf_op jit(solution)/shard_map/ppermute | solution.py:327
  97.9 3.8 %collective-permute-done.32 = f32[8,128]{1,0:T(8,128)S(1)} collective-permute-done((f32[8,128]{1,0:T(8,128)S(1)}, f32[8,128]{1,0:T(8,128)S(1)}, u32[]{:S(2)}, u32[]{:S(2)}) %collective-permute-start.32) | collective-permute-done | bytes 4128 | tf_op jit(solution)/shard_map/ppermute | solution.py:327
  101.6 3.5 %apply.1 = bf16[12288,128]{1,0:T(8,128)(2,1)} custom-call(bf16[768,1024]{1,0:T(8,128)(2,1)S(1)} %get-tuple-element.19.re_ref, bf16[768,1024]{1,0:T(8,128)(2,1)S(1)} %get-tuple-element.20.im_ref, f32[1,1024]{1,0:T(1,128)S(1)} %get-tuple-element.23.phase_ref, f32[8,128]{1,0:T(8,128)S(1)} %select_add_fusion.before_ref), custom_call_target="tpu_custom_call" | custom-call | tf_op jit(solution)/shard_map/apply/pallas_call | solution.py:307
  (63 shorter events, 5.2 us)
Async XLA Ops:
  0.0 28.9 %collective-permute-start.3 = (bf16[128,1536]{1,0:T(8,128)(2,1)}, bf16[128,1536]{1,0:T(8,128)(2,1)S(1)}, u32[]{:S(2)}, u32[]{:S(2)}) collective-permute-start(bf16[128,1536]{1,0:T(8,128)(2,1)} %bitcast.11), channel_id=1, source_target_pairs={{0,12},{1,13},{2,14},{3,15},{4,0},{5,1},{6,2},{7,3},{8,4},{9,5},{1... | collective-permute-start | bytes 1179656 | tf_op jit(solution)/shard_map/ppermute | solution.py:327
  3.1 26.7 %collective-permute-start.7 = (bf16[128,1536]{1,0:T(8,128)(2,1)}, bf16[128,1536]{1,0:T(8,128)(2,1)}, u32[]{:S(2)}, u32[]{:S(2)}) collective-permute-start(bf16[128,1536]{1,0:T(8,128)(2,1)} %bitcast.12), channel_id=1, source_target_pairs={{0,4},{1,5},{2,6},{3,7},{4,8},{5,9},{6,10},{7,11},{8,12},{9,13},{1... | collective-permute-start | bytes 1179656 | tf_op jit(solution)/shard_map/ppermute | solution.py:327
  3.9 5.8 %collective-permute-start.15 = (bf16[128,128]{1,0:T(8,128)(2,1)S(1)}, bf16[128,128]{1,0:T(8,128)(2,1)S(1)}, u32[]{:S(2)}, u32[]{:S(2)}) collective-permute-start(bf16[128,128]{1,0:T(8,128)(2,1)S(1)} %get-tuple-element.26), channel_id=1, source_target_pairs={{0,16},{16,32},{32,48},{48,64},{64,80},{80,96},{96,112},{1,17},{17... | collective-permute-start | bytes 98312 | tf_op jit(solution)/shard_map/ppermute | solution.py:367
  7.7 7.9 %collective-permute-start.16 = (bf16[128,128]{1,0:T(8,128)(2,1)S(1)}, bf16[128,128]{1,0:T(8,128)(2,1)S(1)}, u32[]{:S(2)}, u32[]{:S(2)}) collective-permute-start(bf16[128,128]{1,0:T(8,128)(2,1)S(1)} %get-tuple-element.25), channel_id=1, source_target_pairs={{16,0},{32,16},{48,32},{64,48},{80,64},{96,80},{112,96},{17,1},{33... | collective-permute-start | bytes 98312 | tf_op jit(solution)/shard_map/ppermute | solution.py:368
  15.6 5.9 %collective-permute-start.17 = (bf16[128,256]{1,0:T(8,128)(2,1)S(1)}, bf16[128,256]{1,0:T(8,128)(2,1)S(1)}, u32[]{:S(2)}, u32[]{:S(2)}) collective-permute-start(bf16[128,256]{1,0:T(8,128)(2,1)S(1)} %shard_map.56), channel_id=1, source_target_pairs={{0,2},{1,3},{2,0},{3,1},{4,6},{5,7},{6,4},{7,5},{8,10},{9,11},{10,... | collective-permute-start | bytes 196616 | tf_op jit(solution)/shard_map/ppermute | solution.py:327
  22.2 8.6 %collective-permute-start.19 = (bf16[2,128,256]{2,1,0:T(8,128)(2,1)}, bf16[2,128,256]{2,1,0:T(8,128)(2,1)}, u32[]{:S(2)}, u32[]{:S(2)}) collective-permute-start(bf16[2,128,256]{2,1,0:T(8,128)(2,1)} %pad_maximum_fusion.refs_19_), channel_id=1, source_target_pairs={{0,12},{1,13},{2,14},{3,15},{4,0},{5,1},{6,2},{7,3},{8,4},{9,5},{1... | collective-permute-start | bytes 393224 | tf_op jit(solution)/shard_map/ppermute | solution.py:327
  25.4 13.1 %collective-permute-start.1 = (bf16[128,1536]{1,0:T(8,128)(2,1)}, bf16[128,1536]{1,0:T(8,128)(2,1)}, u32[]{:S(2)}, u32[]{:S(2)}) collective-permute-start(bf16[128,1536]{1,0:T(8,128)(2,1)} %bitcast.14), channel_id=1, source_target_pairs={{0,2},{1,3},{2,0},{3,1},{4,6},{5,7},{6,4},{7,5},{8,10},{9,11},{10,... | collective-permute-start | bytes 1179656 | tf_op jit(solution)/shard_map/ppermute | solution.py:327
  28.9 6.8 %collective-permute-start.21 = (bf16[2,128,256]{2,1,0:T(8,128)(2,1)}, bf16[2,128,256]{2,1,0:T(8,128)(2,1)S(1)}, u32[]{:S(2)}, u32[]{:S(2)}) collective-permute-start(bf16[2,128,256]{2,1,0:T(8,128)(2,1)} %pad_maximum_fusion.refs_19_), channel_id=1, source_target_pairs={{0,8},{1,9},{2,10},{3,11},{4,12},{5,13},{6,14},{7,15},{8,0},{9,1},... | collective-permute-start | bytes 393224 | tf_op jit(solution)/shard_map/ppermute | solution.py:327
  28.9 7.9 %collective-permute-start.23 = (bf16[2,128,256]{2,1,0:T(8,128)(2,1)}, bf16[2,128,256]{2,1,0:T(8,128)(2,1)S(1)}, u32[]{:S(2)}, u32[]{:S(2)}) collective-permute-start(bf16[2,128,256]{2,1,0:T(8,128)(2,1)} %pad_maximum_fusion.refs_19_), channel_id=1, source_target_pairs={{0,4},{1,5},{2,6},{3,7},{4,8},{5,9},{6,10},{7,11},{8,12},{9,13},{1... | collective-permute-start | bytes 393224 | tf_op jit(solution)/shard_map/ppermute | solution.py:327
  29.8 12.0 %collective-permute-start = (bf16[128,1536]{1,0:T(8,128)(2,1)}, bf16[128,1536]{1,0:T(8,128)(2,1)S(1)}, u32[]{:S(2)}, u32[]{:S(2)}) collective-permute-start(bf16[128,1536]{1,0:T(8,128)(2,1)} %bitcast.15), channel_id=1, source_target_pairs={{0,1},{1,0},{2,3},{3,2},{4,5},{5,4},{6,7},{7,6},{8,9},{9,8},{10,11... | collective-permute-start | bytes 1179656 | tf_op jit(solution)/shard_map/ppermute | solution.py:327
  30.8 11.4 %collective-permute-start.8 = (bf16[128,1536]{1,0:T(8,128)(2,1)S(1)}, bf16[128,1536]{1,0:T(8,128)(2,1)S(1)}, u32[]{:S(2)}, u32[]{:S(2)}) collective-permute-start(bf16[128,1536]{1,0:T(8,128)(2,1)S(1)} %shard_map.55), channel_id=1, source_target_pairs={{0,4},{1,13},{2,6},{3,15},{4,8},{5,1},{6,10},{7,3},{8,12},{9,5},{1... | collective-permute-start | bytes 1179656 | tf_op jit(solution)/shard_map/ppermute | solution.py:327
  35.7 1.6 %collective-permute-start.18 = (bf16[2,128,256]{2,1,0:T(8,128)(2,1)}, bf16[2,128,256]{2,1,0:T(8,128)(2,1)S(1)}, u32[]{:S(2)}, u32[]{:S(2)}) collective-permute-start(bf16[2,128,256]{2,1,0:T(8,128)(2,1)} %pad_maximum_fusion.refs_19_), channel_id=1, source_target_pairs={{0,1},{1,0},{2,3},{3,2},{4,5},{5,4},{6,7},{7,6},{8,9},{9,8},{10,11... | collective-permute-start | bytes 393224 | tf_op jit(solution)/shard_map/ppermute | solution.py:327
  36.8 1.6 %collective-permute-start.20 = (bf16[2,128,256]{2,1,0:T(8,128)(2,1)}, bf16[2,128,256]{2,1,0:T(8,128)(2,1)S(1)}, u32[]{:S(2)}, u32[]{:S(2)}) collective-permute-start(bf16[2,128,256]{2,1,0:T(8,128)(2,1)} %collective-permute-done.19.refs_21_), channel_id=1, source_target_pairs={{0,1},{1,0},{2,3},{3,2},{4,5},{5,4},{6,7},{7,6},{8,9},{9,8},{10,11... | collective-permute-start | bytes 393224 | tf_op jit(solution)/shard_map/ppermute | solution.py:327
  37.3 1.3 %collective-permute-start.22 = (bf16[2,128,256]{2,1,0:T(8,128)(2,1)S(1)}, bf16[2,128,256]{2,1,0:T(8,128)(2,1)S(1)}, u32[]{:S(2)}, u32[]{:S(2)}) collective-permute-start(bf16[2,128,256]{2,1,0:T(8,128)(2,1)S(1)} %collective-permute-done.21.refs_23_), channel_id=1, source_target_pairs={{0,1},{1,0},{2,3},{3,2},{4,5},{5,4},{6,7},{7,6},{8,9},{9,8},{10,11... | collective-permute-start | bytes 393224 | tf_op jit(solution)/shard_map/ppermute | solution.py:327
  38.3 3.4 %collective-permute-start.24 = (bf16[2,128,256]{2,1,0:T(8,128)(2,1)S(1)}, bf16[2,128,256]{2,1,0:T(8,128)(2,1)S(1)}, u32[]{:S(2)}, u32[]{:S(2)}) collective-permute-start(bf16[2,128,256]{2,1,0:T(8,128)(2,1)S(1)} %collective-permute-done.23.refs_25_), channel_id=1, source_target_pairs={{0,1},{1,0},{2,3},{3,2},{4,5},{5,4},{6,7},{7,6},{8,9},{9,8},{10,11... | collective-permute-start | bytes 393224 | tf_op jit(solution)/shard_map/ppermute | solution.py:327
  38.5 12.8 %collective-permute-start.13 = (bf16[128,1536]{1,0:T(8,128)(2,1)}, bf16[128,1536]{1,0:T(8,128)(2,1)S(1)}, u32[]{:S(2)}, u32[]{:S(2)}) collective-permute-start(bf16[128,1536]{1,0:T(8,128)(2,1)} %collective-permute-done.1.refs_5_), channel_id=1, source_target_pairs={{0,4},{1,5},{2,6},{3,7},{4,8},{5,9},{6,10},{7,11},{8,12},{9,13},{1... | collective-permute-start | bytes 1179656 | tf_op jit(solution)/shard_map/ppermute | solution.py:327
  38.6 12.7 %collective-permute-start.5 = (bf16[128,1536]{1,0:T(8,128)(2,1)}, bf16[128,1536]{1,0:T(8,128)(2,1)S(1)}, u32[]{:S(2)}, u32[]{:S(2)}) collective-permute-start(bf16[128,1536]{1,0:T(8,128)(2,1)} %collective-permute-done.1.refs_5_), channel_id=1, source_target_pairs={{0,12},{1,13},{2,14},{3,15},{4,0},{5,1},{6,2},{7,3},{8,4},{9,5},{1... | collective-permute-start | bytes 1179656 | tf_op jit(solution)/shard_map/ppermute | solution.py:327
  41.7 10.1 %collective-permute-start.2 = (bf16[128,1536]{1,0:T(8,128)(2,1)}, bf16[128,1536]{1,0:T(8,128)(2,1)S(1)}, u32[]{:S(2)}, u32[]{:S(2)}) collective-permute-start(bf16[128,1536]{1,0:T(8,128)(2,1)} %collective-permute-done.1.refs_5_), channel_id=1, source_target_pairs={{0,1},{1,0},{2,3},{3,2},{4,5},{5,4},{6,7},{7,6},{8,9},{9,8},{10,11... | collective-permute-start | bytes 1179656 | tf_op jit(solution)/shard_map/ppermute | solution.py:327
  41.7 10.2 %collective-permute-start.12 = (bf16[128,1536]{1,0:T(8,128)(2,1)}, bf16[128,1536]{1,0:T(8,128)(2,1)S(1)}, u32[]{:S(2)}, u32[]{:S(2)}) collective-permute-start(bf16[128,1536]{1,0:T(8,128)(2,1)} %collective-permute-done.7.above_ref.refs_15_), channel_id=1, source_target_pairs={{0,1},{1,0},{2,3},{3,2},{4,5},{5,4},{6,7},{7,6},{8,9},{9,8},{10,11... | collective-permute-start | bytes 1179656 | tf_op jit(solution)/shard_map/ppermute | solution.py:327
  42.3 12.6 %collective-permute-start.10 = (bf16[128,1536]{1,0:T(8,128)(2,1)S(1)}, bf16[128,1536]{1,0:T(8,128)(2,1)S(1)}, u32[]{:S(2)}, u32[]{:S(2)}) collective-permute-start(bf16[128,1536]{1,0:T(8,128)(2,1)S(1)} %collective-permute-done.8.refs_11_), channel_id=1, source_target_pairs={{0,2},{1,3},{2,0},{3,1},{4,6},{5,7},{6,4},{7,5},{8,10},{9,11},{10,... | collective-permute-start | bytes 1179656 | tf_op jit(solution)/shard_map/ppermute | solution.py:327
  51.3 9.0 %collective-permute-start.4 = (bf16[128,1536]{1,0:T(8,128)(2,1)S(1)}, bf16[128,1536]{1,0:T(8,128)(2,1)S(1)}, u32[]{:S(2)}, u32[]{:S(2)}) collective-permute-start(bf16[128,1536]{1,0:T(8,128)(2,1)S(1)} %collective-permute-done.3.below_ref.refs_7_), channel_id=1, source_target_pairs={{0,1},{1,0},{2,3},{3,2},{4,5},{5,4},{6,7},{7,6},{8,9},{9,8},{10,11... | collective-permute-start | bytes 1179656 | tf_op jit(solution)/shard_map/ppermute | solution.py:327
  51.3 9.0 %collective-permute-start.9 = (bf16[128,1536]{1,0:T(8,128)(2,1)S(1)}, bf16[128,1536]{1,0:T(8,128)(2,1)S(1)}, u32[]{:S(2)}, u32[]{:S(2)}) collective-permute-start(bf16[128,1536]{1,0:T(8,128)(2,1)S(1)} %collective-permute-done.8.refs_11_), channel_id=1, source_target_pairs={{0,1},{1,0},{2,3},{3,2},{4,5},{5,4},{6,7},{7,6},{8,9},{9,8},{10,11... | collective-permute-start | bytes 1179656 | tf_op jit(solution)/shard_map/ppermute | solution.py:327
  51.8 8.5 %collective-permute-start.14 = (bf16[128,1536]{1,0:T(8,128)(2,1)S(1)}, bf16[128,1536]{1,0:T(8,128)(2,1)S(1)}, u32[]{:S(2)}, u32[]{:S(2)}) collective-permute-start(bf16[128,1536]{1,0:T(8,128)(2,1)S(1)} %collective-permute-done.13.refs_17_), channel_id=1, source_target_pairs={{0,1},{1,0},{2,3},{3,2},{4,5},{5,4},{6,7},{7,6},{8,9},{9,8},{10,11... | collective-permute-start | bytes 1179656 | tf_op jit(solution)/shard_map/ppermute | solution.py:327
  51.9 8.4 %collective-permute-start.6 = (bf16[128,1536]{1,0:T(8,128)(2,1)S(1)}, bf16[128,1536]{1,0:T(8,128)(2,1)S(1)}, u32[]{:S(2)}, u32[]{:S(2)}) collective-permute-start(bf16[128,1536]{1,0:T(8,128)(2,1)S(1)} %collective-permute-done.5.refs_9_), channel_id=1, source_target_pairs={{0,1},{1,0},{2,3},{3,2},{4,5},{5,4},{6,7},{7,6},{8,9},{9,8},{10,11... | collective-permute-start | bytes 1179656 | tf_op jit(solution)/shard_map/ppermute | solution.py:327
  54.9 5.5 %collective-permute-start.11 = (bf16[128,1536]{1,0:T(8,128)(2,1)S(1)}, bf16[128,1536]{1,0:T(8,128)(2,1)S(1)}, u32[]{:S(2)}, u32[]{:S(2)}) collective-permute-start(bf16[128,1536]{1,0:T(8,128)(2,1)S(1)} %collective-permute-done.10.refs_13_), channel_id=1, source_target_pairs={{0,1},{1,0},{2,3},{3,2},{4,5},{5,4},{6,7},{7,6},{8,9},{9,8},{10,11... | collective-permute-start | bytes 1179656 | tf_op jit(solution)/shard_map/ppermute | solution.py:327
  66.5 7.0 %collective-permute-start.25 = (f32[2,768]{1,0:T(2,128)S(1)}, f32[2,768]{1,0:T(2,128)S(1)}, u32[]{:S(2)}, u32[]{:S(2)}) collective-permute-start(f32[2,768]{1,0:T(2,128)S(1)} %slice.11), channel_id=1, source_target_pairs={{1,0},{2,1},{3,2},{4,3},{5,4},{6,5},{7,6},{8,7},{9,8},{10,9},{11,1... | collective-permute-start | bytes 18440 | tf_op jit(solution)/shard_map/ppermute | solution.py:405
  73.5 3.8 %collective-permute-start.26 = (f32[4,1024]{1,0:T(4,128)S(1)}, f32[4,1024]{1,0:T(4,128)S(1)}, u32[]{:S(2)}, u32[]{:S(2)}) collective-permute-start(f32[4,1024]{1,0:T(4,128)S(1)} %shard_map.58), channel_id=1, source_target_pairs={{0,16},{16,0},{32,48},{48,32},{64,80},{80,64},{96,112},{112,96},{1... | collective-permute-start | bytes 49160 | tf_op jit(solution)/shard_map/ppermute | solution.py:327
  77.3 4.9 %collective-permute-start.27 = (f32[4,1024]{1,0:T(4,128)S(1)}, f32[4,1024]{1,0:T(4,128)S(1)}, u32[]{:S(2)}, u32[]{:S(2)}) collective-permute-start(f32[4,1024]{1,0:T(4,128)S(1)} %add.24), channel_id=1, source_target_pairs={{0,48},{16,32},{32,16},{48,0},{64,112},{80,96},{96,80},{112,64},{1... | collective-permute-start | bytes 49160 | tf_op jit(solution)/shard_map/ppermute | solution.py:327
  82.3 3.7 %collective-permute-start.28 = (f32[4,1024]{1,0:T(4,128)S(1)}, f32[4,1024]{1,0:T(4,128)S(1)}, u32[]{:S(2)}, u32[]{:S(2)}) collective-permute-start(f32[4,1024]{1,0:T(4,128)S(1)} %add.25.stats_ref), channel_id=1, source_target_pairs={{0,64},{16,80},{32,96},{48,112},{64,0},{80,16},{96,32},{112,48},{1... | collective-permute-start | bytes 49160 | tf_op jit(solution)/shard_map/ppermute | solution.py:327
  87.9 5.3 %collective-permute-start.30 = (f32[8,128]{1,0:T(8,128)S(1)}, f32[8,128]{1,0:T(8,128)S(1)}, u32[]{:S(2)}, u32[]{:S(2)}) collective-permute-start(f32[8,128]{1,0:T(8,128)S(1)} %add.26), channel_id=1, source_target_pairs={{0,2},{1,3},{2,0},{3,1},{4,6},{5,7},{6,4},{7,5},{8,10},{9,11},{10,... | collective-permute-start | bytes 12296 | tf_op jit(solution)/shard_map/ppermute | solution.py:327
  93.2 3.6 %collective-permute-start.31 = (f32[8,128]{1,0:T(8,128)S(1)}, f32[8,128]{1,0:T(8,128)S(1)}, u32[]{:S(2)}, u32[]{:S(2)}) collective-permute-start(f32[8,128]{1,0:T(8,128)S(1)} %add.28), channel_id=1, source_target_pairs={{0,4},{1,5},{2,6},{3,7},{4,0},{5,1},{6,2},{7,3},{8,12},{9,13},{10,... | collective-permute-start | bytes 12296 | tf_op jit(solution)/shard_map/ppermute | solution.py:327
  96.8 4.8 %collective-permute-start.32 = (f32[8,128]{1,0:T(8,128)S(1)}, f32[8,128]{1,0:T(8,128)S(1)}, u32[]{:S(2)}, u32[]{:S(2)}) collective-permute-start(f32[8,128]{1,0:T(8,128)S(1)} %add.30), channel_id=1, source_target_pairs={{0,12},{1,13},{2,14},{3,15},{4,8},{5,9},{6,10},{7,11},{8,4},{9,5},... | collective-permute-start | bytes 12296 | tf_op jit(solution)/shard_map/ppermute | solution.py:327
  (7 other events, 228.5 us)

commit v4 on v3

--- a/solution.py
+++ b/solution.py
@@ -343,40 +343,14 @@
     return send(x, "az", lambda i: i ^ 1)
 
 
-def join_kernel(low_ref, high_ref, out_ref):
-    out_ref[:, :GUARD] = low_ref[...]
-    out_ref[:, GUARD:] = high_ref[...]
-
-
-def select_kernel(me_ref, above_ref, below_ref, out_ref):
-    even = me_ref[0] & 1 == 0
-
-    @pl.when(even)
-    def _():
-        out_ref[...] = above_ref[...]
-
-    @pl.when(jnp.logical_not(even))
-    def _():
-        out_ref[...] = below_ref[...]
-
-
 def spread(block):
     n = lax.axis_size("rng")
     width = block.shape[1]
     above, below, other = up(block), down(block), across(block)
     low = lax.ppermute(block[:, width - GUARD :], "rng", [(i, i + 1) for i in range(n - 1)])
     high = lax.ppermute(block[:, :GUARD], "rng", [(i + 1, i) for i in range(n - 1)])
-    (ends,) = kernel_call(
-        join_kernel, [jax.ShapeDtypeStruct((block.shape[0], 2 * GUARD), jnp.bfloat16)], low, high
-    )
-    (passed,) = kernel_call(
-        select_kernel,
-        [jax.ShapeDtypeStruct(block.shape, jnp.bfloat16)],
-        lax.axis_index("az").reshape(1),
-        above,
-        below,
-        scalars=1,
-    )
+    ends = jnp.concatenate([low, high], axis=1)
+    passed = jnp.where(lax.axis_index("az") & 1 == 0, above, below)
     opposite = send(passed, "az", lambda i: (i + (4, -4)[i & 1]) % 16)
     slots = {(0, 0): block, (3, 0): above, (1, 0): below, (2, 0): opposite, (0, 1): other}
     slots[3, 1] = up(other)

time: 105 us -> 107 us (1.019)
  starting transfers between devices: 36.3 us -> 39.5 us
  waiting for transfers between devices: 44.7 us -> 41.5 us
  Pallas kernels: 22.4 us -> 20.8 us
  local copies, waits for them, and re-layouts: 0.86 us -> 2.2 us
  other arithmetic: 0.69 us -> 1.95 us
    ppermute x30, starting transfers between devices: 29.1 us -> 32.3 us  [send(): return lax.ppermute(x, axis, [(i, move(i)) for i in range(n)])]
    ppermute x30, waiting for transfers between devices: 38.9 us -> 36.3 us  [send(): return lax.ppermute(x, axis, [(i, move(i)) for i in range(n)])]
    pallas_call x5 -> x3, Pallas kernels: 7.39 us -> 6.38 us  [kernel_call(): pl.pallas_call(body, in_specs=[SMEM] * scalars + [VMEM] * (len(args) - sc...]
  transfers between devices with their start and end apart: 33 -> 33, of which waited for: 16 -> 18; matrix products, arithmetic and copies ran while one was open for 1% -> 3% of each run, Pallas kernels for 11% -> 10%
where the time goes in v4:
time: 107 us; the launch traced here: 106 us
  waiting for transfers between devices  41.5 us (39%)
  starting transfers between devices  39.5 us (37%)
  Pallas kernels  20.8 us (19%)
  local copies, waits for them, and re-layouts  2.2 us (2%)
  other arithmetic  1.95 us (2%)
    ppermute x30, waiting for transfers between devices, send(): return lax.ppermute(x, axis, [(i, move(i)) for i in range(n)])  36.3 us
    ppermute x30, starting transfers between devices, send(): return lax.ppermute(x, axis, [(i, move(i)) for i in range(n)])  32.3 us
    pallas_call x3, Pallas kernels, kernel_call(): pl.pallas_call(body, in_specs=[SMEM] * scalars + [VMEM] * (len(args) - sc...  6.38 us
    pallas_call x1, Pallas kernels, focus(): return call(me, owner_map, starts, *slots, *ends, interp, edge_weights)  5.55 us
    pallas_call x1, Pallas kernels, steering(): pl.pallas_call(lambda *refs: steering_kernel(scale, *refs), in_specs=[HBM...  5.38 us
    ppermute x1, waiting for transfers between devices, spread(): lax.ppermute(block[:, :GUARD], 'rng', [(i + 1, i) for i in range(n - 1)])  5.18 us
    ppermute x1, starting transfers between devices, spread(): lax.ppermute(block[:, width - GUARD:], 'rng', [(i, i + 1) for i in range(...  3.86 us
    pallas_call x1, Pallas kernels, apply(): pl.pallas_call(apply_kernel, grid=(rows // step,), in_specs=[VMEM] * 4, o...  3.54 us
  transfers between devices with their start and end apart: 33, of which 18 were waited for; matrix products, arithmetic and copies ran while one was open for 3% of the time, Pallas kernels for 10%

profile of v4, /device:TPU:6, one launch (start us, length us, event | category | flops | bytes accessed | tf_op | source)
XLA Modules:
  0.0 106.3 jit_solution(18405350743761991237)
XLA Ops:
  0.9 3.9 %collective-permute-start.15 = (bf16[128,128]{1,0:T(8,128)(2,1)S(1)}, bf16[128,128]{1,0:T(8,128)(2,1)S(1)}, u32[]{:S(2)}, u32[]{:S(2)}) collective-permute-start(bf16[128,128]{1,0:T(8,128)(2,1)S(1)} %get-tuple-element.26), channel_id=1, source_target_pairs={{0,16},{16,32},{32,48},{48,64},{64,80},{80,96},{96,112},{1,17},{17... | collective-permute-start | bytes 98312 | tf_op jit(solution)/shard_map/ppermute | solution.py:350
  4.8 3.1 %collective-permute-start.3 = (bf16[128,1536]{1,0:T(8,128)(2,1)}, bf16[128,1536]{1,0:T(8,128)(2,1)S(1)}, u32[]{:S(2)}, u32[]{:S(2)}) collective-permute-start(bf16[128,1536]{1,0:T(8,128)(2,1)} %bitcast.12), channel_id=1, source_target_pairs={{0,12},{1,13},{2,14},{3,15},{4,0},{5,1},{6,2},{7,3},{8,4},{9,5},{1... | collective-permute-start | bytes 1179656 | tf_op jit(solution)/shard_map/ppermute | solution.py:327
  7.9 2.1 %collective-permute-start.16 = (bf16[128,128]{1,0:T(8,128)(2,1)S(1)}, bf16[128,128]{1,0:T(8,128)(2,1)S(1)}, u32[]{:S(2)}, u32[]{:S(2)}) collective-permute-start(bf16[128,128]{1,0:T(8,128)(2,1)S(1)} %get-tuple-element.25), channel_id=1, source_target_pairs={{16,0},{32,16},{48,32},{64,48},{80,64},{96,80},{112,96},{17,1},{33... | collective-permute-start | bytes 98312 | tf_op jit(solution)/shard_map/ppermute | solution.py:351
  10.6 5.2 %collective-permute-done.16 = bf16[128,128]{1,0:T(8,128)(2,1)S(1)} collective-permute-done((bf16[128,128]{1,0:T(8,128)(2,1)S(1)}, bf16[128,128]{1,0:T(8,128)(2,1)S(1)}, u32[]{:S(2)}, u32[]{:S(2)}) %collective-permute-start.16) | collective-permute-done | bytes 32800 | tf_op jit(solution)/shard_map/ppermute | solution.py:351
  16.4 3.6 %collective-permute-start.17 = (bf16[128,256]{1,0:T(8,128)(2,1)}, bf16[128,256]{1,0:T(8,128)(2,1)}, u32[]{:S(2)}, u32[]{:S(2)}) collective-permute-start(bf16[128,256]{1,0:T(8,128)(2,1)} %constant_dynamic-update-slice_fusion), channel_id=1, source_target_pairs={{0,2},{1,3},{2,0},{3,1},{4,6},{5,7},{6,4},{7,5},{8,10},{9,11},{10,... | collective-permute-start | bytes 196616 | tf_op jit(solution)/shard_map/ppermute | solution.py:327
  20.0 2.8 %collective-permute-done.17 = bf16[128,256]{1,0:T(8,128)(2,1)} collective-permute-done((bf16[128,256]{1,0:T(8,128)(2,1)}, bf16[128,256]{1,0:T(8,128)(2,1)}, u32[]{:S(2)}, u32[]{:S(2)}) %collective-permute-start.17) | collective-permute-done | bytes 65568 | tf_op jit(solution)/shard_map/ppermute | solution.py:327
  23.7 3.6 %collective-permute-start.19 = (bf16[2,128,256]{2,1,0:T(8,128)(2,1)S(1)}, bf16[2,128,256]{2,1,0:T(8,128)(2,1)S(1)}, u32[]{:S(2)}, u32[]{:S(2)}) collective-permute-start(bf16[2,128,256]{2,1,0:T(8,128)(2,1)S(1)} %pad_maximum_fusion.refs_19_), channel_id=1, source_target_pairs={{0,12},{1,13},{2,14},{3,15},{4,0},{5,1},{6,2},{7,3},{8,4},{9,5},{1... | collective-permute-start | bytes 393224 | tf_op jit(solution)/shard_map/ppermute | solution.py:327
  27.3 1.0 collective-permute-start.23
  28.3 1.0 broadcast_select_fusion
  29.3 1.9 %collective-permute-done.19.refs_21_ = bf16[2,128,256]{2,1,0:T(8,128)(2,1)S(1)} collective-permute-done((bf16[2,128,256]{2,1,0:T(8,128)(2,1)S(1)}, bf16[2,128,256]{2,1,0:T(8,128)(2,1)S(1)}, u32[]{:S(2)}, u32[]{:S(2)}) %collective-permute-start.19) | collective-permute-done | bytes 131104 | tf_op jit(solution)/shard_map/ppermute | solution.py:327
  31.2 1.4 %collective-permute-start.8 = (bf16[128,1536]{1,0:T(8,128)(2,1)S(1)}, bf16[128,1536]{1,0:T(8,128)(2,1)S(1)}, u32[]{:S(2)}, u32[]{:S(2)}) collective-permute-start(bf16[128,1536]{1,0:T(8,128)(2,1)S(1)} %broadcast_select_fusion), channel_id=1, source_target_pairs={{0,4},{1,13},{2,6},{3,15},{4,8},{5,1},{6,10},{7,3},{8,12},{9,5},{1... | collective-permute-start | bytes 1179656 | tf_op jit(solution)/shard_map/ppermute | solution.py:327
  32.7 1.2 %collective-permute-done.21.refs_23_ = bf16[2,128,256]{2,1,0:T(8,128)(2,1)S(1)} collective-permute-done((bf16[2,128,256]{2,1,0:T(8,128)(2,1)S(1)}, bf16[2,128,256]{2,1,0:T(8,128)(2,1)S(1)}, u32[]{:S(2)}, u32[]{:S(2)}) %collective-permute-start.21) | collective-permute-done | bytes 131104 | tf_op jit(solution)/shard_map/ppermute | solution.py:327
  33.9 1.1 %collective-permute-done.23.refs_25_ = bf16[2,128,256]{2,1,0:T(8,128)(2,1)S(1)} collective-permute-done((bf16[2,128,256]{2,1,0:T(8,128)(2,1)S(1)}, bf16[2,128,256]{2,1,0:T(8,128)(2,1)S(1)}, u32[]{:S(2)}, u32[]{:S(2)}) %collective-permute-start.23) | collective-permute-done | bytes 131104 | tf_op jit(solution)/shard_map/ppermute | solution.py:327
  36.6 3.1 %collective-permute-start.5 = (bf16[128,1536]{1,0:T(8,128)(2,1)}, bf16[128,1536]{1,0:T(8,128)(2,1)S(1)}, u32[]{:S(2)}, u32[]{:S(2)}) collective-permute-start(bf16[128,1536]{1,0:T(8,128)(2,1)} %collective-permute-done.1.refs_5_), channel_id=1, source_target_pairs={{0,12},{1,13},{2,14},{3,15},{4,0},{5,1},{6,2},{7,3},{8,4},{9,5},{1... | collective-permute-start | bytes 1179656 | tf_op jit(solution)/shard_map/ppermute | solution.py:327
  40.6 3.7 %collective-permute-start.10 = (bf16[128,1536]{1,0:T(8,128)(2,1)S(1)}, bf16[128,1536]{1,0:T(8,128)(2,1)S(1)}, u32[]{:S(2)}, u32[]{:S(2)}) collective-permute-start(bf16[128,1536]{1,0:T(8,128)(2,1)S(1)} %collective-permute-done.8.refs_11_), channel_id=1, source_target_pairs={{0,2},{1,3},{2,0},{3,1},{4,6},{5,7},{6,4},{7,5},{8,10},{9,11},{10,... | collective-permute-start | bytes 1179656 | tf_op jit(solution)/shard_map/ppermute | solution.py:327
  44.3 5.0 %collective-permute-done.13.refs_17_ = bf16[128,1536]{1,0:T(8,128)(2,1)S(1)} collective-permute-done((bf16[128,1536]{1,0:T(8,128)(2,1)}, bf16[128,1536]{1,0:T(8,128)(2,1)S(1)}, u32[]{:S(2)}, u32[]{:S(2)}) %collective-permute-start.13) | collective-permute-done | bytes 393248 | tf_op jit(solution)/shard_map/ppermute | solution.py:327
  50.3 3.0 %collective-permute-done.10.refs_13_ = bf16[128,1536]{1,0:T(8,128)(2,1)S(1)} collective-permute-done((bf16[128,1536]{1,0:T(8,128)(2,1)S(1)}, bf16[128,1536]{1,0:T(8,128)(2,1)S(1)}, u32[]{:S(2)}, u32[]{:S(2)}) %collective-permute-start.10) | collective-permute-done | bytes 393248 | tf_op jit(solution)/shard_map/ppermute | solution.py:327
  53.3 5.4 %steering.1 = (bf16[1024,1024]{1,0:T(8,128)(2,1)}, bf16[1024,1024]{1,0:T(8,128)(2,1)}, bf16[128,1024]{1,0:T(8,128)(2,1)}) custom-call(f32[8,64,1024]{2,1,0:T(8,128)} %refs_0_.1), custom_call_target="tpu_custom_call" | custom-call | tf_op jit(solution)/shard_map/steering/pallas_call | solution.py:92
  58.8 5.6 %focus.1 = (bf16[768,1024]{1,0:T(8,128)(2,1)S(1)}, f32[4,768]{1,0:T(4,128)S(1)}) custom-call(s32[1]{0:T(128)} %bitcast.refs_0_, s32[8]{0:T(128)S(1)} %copy-done.5, s32[6,1,8]{2,1,0:T(1,128)S(1)} %copy-done.4, bf16[128,1536]{1,0:T(8,128)(2,1)S(1)} %bitcast.16, bf16[128,1536]{1,0:T(8,128)(2,1)} %collective-permute-done.refs_4_, ...), custom_call_target="tpu_custom_call" | custom-call | tf_op jit(solution)/shard_map/focus/pallas_call | solution.py:192
  64.4 1.3 %collective-permute-start.25 = (f32[2,768]{1,0:T(2,128)S(1)}, f32[2,768]{1,0:T(2,128)S(1)}, u32[]{:S(2)}, u32[]{:S(2)}) collective-permute-start(f32[2,768]{1,0:T(2,128)S(1)} %slice.11), channel_id=1, source_target_pairs={{1,0},{2,1},{3,2},{4,3},{5,4},{6,5},{7,6},{8,7},{9,8},{10,9},{11,1... | collective-permute-start | bytes 18440 | tf_op jit(solution)/shard_map/ppermute | solution.py:379
  65.7 5.6 %shard_map.55 = (bf16[768,1024]{1,0:T(8,128)(2,1)S(1)}, bf16[768,1024]{1,0:T(8,128)(2,1)S(1)}, f32[4,1024]{1,0:T(4,128)S(1)}) custom-call(bf16[768,1024]{1,0:T(8,128)(2,1)S(1)} %get-tuple-element.16.focused_ref, bf16[1024,1024]{1,0:T(8,128)(2,1)S(1)} %copy-done.1, bf16[1024,1024]{1,0:T(8,128)(2,1)S(1)} %copy-done.2), custom_call_target="tpu_custom_call" | custom-call | tf_op jit(solution)/shard_map/pallas_call | solution.py:38
  71.5 3.7 %collective-permute-done.26 = f32[4,1024]{1,0:T(4,128)S(1)} collective-permute-done((f32[4,1024]{1,0:T(4,128)S(1)}, f32[4,1024]{1,0:T(4,128)S(1)}, u32[]{:S(2)}, u32[]{:S(2)}) %collective-permute-start.26) | collective-permute-done | bytes 16416 | tf_op jit(solution)/shard_map/ppermute | solution.py:327
  75.2 4.9 %collective-permute-done.27 = f32[4,1024]{1,0:T(4,128)S(1)} collective-permute-done((f32[4,1024]{1,0:T(4,128)S(1)}, f32[4,1024]{1,0:T(4,128)S(1)}, u32[]{:S(2)}, u32[]{:S(2)}) %collective-permute-start.27) | collective-permute-done | bytes 16416 | tf_op jit(solution)/shard_map/ppermute | solution.py:327
  80.2 3.7 %collective-permute-done.28.more_ref = f32[4,1024]{1,0:T(4,128)S(1)} collective-permute-done((f32[4,1024]{1,0:T(4,128)S(1)}, f32[4,1024]{1,0:T(4,128)S(1)}, u32[]{:S(2)}, u32[]{:S(2)}) %collective-permute-start.28) | collective-permute-done | bytes 16416 | tf_op jit(solution)/shard_map/ppermute | solution.py:327
  84.6 1.2 %collective-permute-done.29 = f32[8,128]{1,0:T(8,128)S(1)} collective-permute-done((f32[8,128]{1,0:T(8,128)S(1)}, f32[8,128]{1,0:T(8,128)S(1)}, u32[]{:S(2)}, u32[]{:S(2)}) %collective-permute-start.29) | collective-permute-done | bytes 4128 | tf_op jit(solution)/shard_map/ppermute | solution.py:327
  85.8 5.0 %collective-permute-start.30 = (f32[8,128]{1,0:T(8,128)S(1)}, f32[8,128]{1,0:T(8,128)S(1)}, u32[]{:S(2)}, u32[]{:S(2)}) collective-permute-start(f32[8,128]{1,0:T(8,128)S(1)} %add.26), channel_id=1, source_target_pairs={{0,2},{1,3},{2,0},{3,1},{4,6},{5,7},{6,4},{7,5},{8,10},{9,11},{10,... | collective-permute-start | bytes 12296 | tf_op jit(solution)/shard_map/ppermute | solution.py:327
  90.8 1.6 %collective-permute-done.30 = f32[8,128]{1,0:T(8,128)S(1)} collective-permute-done((f32[8,128]{1,0:T(8,128)S(1)}, f32[8,128]{1,0:T(8,128)S(1)}, u32[]{:S(2)}, u32[]{:S(2)}) %collective-permute-start.30) | collective-permute-done | bytes 4128 | tf_op jit(solution)/shard_map/ppermute | solution.py:327
  92.3 4.0 %collective-permute-start.31 = (f32[8,128]{1,0:T(8,128)S(1)}, f32[8,128]{1,0:T(8,128)S(1)}, u32[]{:S(2)}, u32[]{:S(2)}) collective-permute-start(f32[8,128]{1,0:T(8,128)S(1)} %add.28), channel_id=1, source_target_pairs={{0,4},{1,5},{2,6},{3,7},{4,0},{5,1},{6,2},{7,3},{8,12},{9,13},{10,... | collective-permute-start | bytes 12296 | tf_op jit(solution)/shard_map/ppermute | solution.py:327
  96.3 1.6 %collective-permute-done.31 = f32[8,128]{1,0:T(8,128)S(1)} collective-permute-done((f32[8,128]{1,0:T(8,128)S(1)}, f32[8,128]{1,0:T(8,128)S(1)}, u32[]{:S(2)}, u32[]{:S(2)}) %collective-permute-start.31) | collective-permute-done | bytes 4128 | tf_op jit(solution)/shard_map/ppermute | solution.py:327
  97.9 1.8 %collective-permute-start.32 = (f32[8,128]{1,0:T(8,128)S(1)}, f32[8,128]{1,0:T(8,128)S(1)}, u32[]{:S(2)}, u32[]{:S(2)}) collective-permute-start(f32[8,128]{1,0:T(8,128)S(1)} %add.30), channel_id=1, source_target_pairs={{0,12},{1,13},{2,14},{3,15},{4,8},{5,9},{6,10},{7,11},{8,4},{9,5},... | collective-permute-start | bytes 12296 | tf_op jit(solution)/shard_map/ppermute | solution.py:327
  99.7 3.0 %collective-permute-done.32 = f32[8,128]{1,0:T(8,128)S(1)} collective-permute-done((f32[8,128]{1,0:T(8,128)S(1)}, f32[8,128]{1,0:T(8,128)S(1)}, u32[]{:S(2)}, u32[]{:S(2)}) %collective-permute-start.32) | collective-permute-done | bytes 4128 | tf_op jit(solution)/shard_map/ppermute | solution.py:327
  102.7 3.5 %apply.1 = bf16[12288,128]{1,0:T(8,128)(2,1)} custom-call(bf16[768,1024]{1,0:T(8,128)(2,1)S(1)} %get-tuple-element.19.re_ref, bf16[768,1024]{1,0:T(8,128)(2,1)S(1)} %get-tuple-element.20.im_ref, f32[1,1024]{1,0:T(1,128)S(1)} %get-tuple-element.23.phase_ref, f32[8,128]{1,0:T(8,128)S(1)} %select_add_fusion.before_ref), custom_call_target="tpu_custom_call" | custom-call | tf_op jit(solution)/shard_map/apply/pallas_call | solution.py:307
  (64 shorter events, 7.6 us)
Async XLA Ops:
  0.9 9.1 %collective-permute-start.15 = (bf16[128,128]{1,0:T(8,128)(2,1)S(1)}, bf16[128,128]{1,0:T(8,128)(2,1)S(1)}, u32[]{:S(2)}, u32[]{:S(2)}) collective-permute-start(bf16[128,128]{1,0:T(8,128)(2,1)S(1)} %get-tuple-element.26), channel_id=1, source_target_pairs={{0,16},{16,32},{32,48},{48,64},{64,80},{80,96},{96,112},{1,17},{17... | collective-permute-start | bytes 98312 | tf_op jit(solution)/shard_map/ppermute | solution.py:350
  4.8 22.5 %collective-permute-start.3 = (bf16[128,1536]{1,0:T(8,128)(2,1)}, bf16[128,1536]{1,0:T(8,128)(2,1)S(1)}, u32[]{:S(2)}, u32[]{:S(2)}) collective-permute-start(bf16[128,1536]{1,0:T(8,128)(2,1)} %bitcast.12), channel_id=1, source_target_pairs={{0,12},{1,13},{2,14},{3,15},{4,0},{5,1},{6,2},{7,3},{8,4},{9,5},{1... | collective-permute-start | bytes 1179656 | tf_op jit(solution)/shard_map/ppermute | solution.py:327
  7.9 19.4 %collective-permute-start.7 = (bf16[128,1536]{1,0:T(8,128)(2,1)}, bf16[128,1536]{1,0:T(8,128)(2,1)}, u32[]{:S(2)}, u32[]{:S(2)}) collective-permute-start(bf16[128,1536]{1,0:T(8,128)(2,1)} %bitcast.13), channel_id=1, source_target_pairs={{0,4},{1,5},{2,6},{3,7},{4,8},{5,9},{6,10},{7,11},{8,12},{9,13},{1... | collective-permute-start | bytes 1179656 | tf_op jit(solution)/shard_map/ppermute | solution.py:327
  7.9 7.9 %collective-permute-start.16 = (bf16[128,128]{1,0:T(8,128)(2,1)S(1)}, bf16[128,128]{1,0:T(8,128)(2,1)S(1)}, u32[]{:S(2)}, u32[]{:S(2)}) collective-permute-start(bf16[128,128]{1,0:T(8,128)(2,1)S(1)} %get-tuple-element.25), channel_id=1, source_target_pairs={{16,0},{32,16},{48,32},{64,48},{80,64},{96,80},{112,96},{17,1},{33... | collective-permute-start | bytes 98312 | tf_op jit(solution)/shard_map/ppermute | solution.py:351
  16.4 6.4 %collective-permute-start.17 = (bf16[128,256]{1,0:T(8,128)(2,1)}, bf16[128,256]{1,0:T(8,128)(2,1)}, u32[]{:S(2)}, u32[]{:S(2)}) collective-permute-start(bf16[128,256]{1,0:T(8,128)(2,1)} %constant_dynamic-update-slice_fusion), channel_id=1, source_target_pairs={{0,2},{1,3},{2,0},{3,1},{4,6},{5,7},{6,4},{7,5},{8,10},{9,11},{10,... | collective-permute-start | bytes 196616 | tf_op jit(solution)/shard_map/ppermute | solution.py:327
  20.0 16.5 %collective-permute-start.1 = (bf16[128,1536]{1,0:T(8,128)(2,1)}, bf16[128,1536]{1,0:T(8,128)(2,1)}, u32[]{:S(2)}, u32[]{:S(2)}) collective-permute-start(bf16[128,1536]{1,0:T(8,128)(2,1)} %bitcast.14), channel_id=1, source_target_pairs={{0,2},{1,3},{2,0},{3,1},{4,6},{5,7},{6,4},{7,5},{8,10},{9,11},{10,... | collective-permute-start | bytes 1179656 | tf_op jit(solution)/shard_map/ppermute | solution.py:327
  20.0 19.7 %collective-permute-start = (bf16[128,1536]{1,0:T(8,128)(2,1)}, bf16[128,1536]{1,0:T(8,128)(2,1)}, u32[]{:S(2)}, u32[]{:S(2)}) collective-permute-start(bf16[128,1536]{1,0:T(8,128)(2,1)} %bitcast.15), channel_id=1, source_target_pairs={{0,1},{1,0},{2,3},{3,2},{4,5},{5,4},{6,7},{7,6},{8,9},{9,8},{10,11... | collective-permute-start | bytes 1179656 | tf_op jit(solution)/shard_map/ppermute | solution.py:327
  23.7 7.5 %collective-permute-start.19 = (bf16[2,128,256]{2,1,0:T(8,128)(2,1)S(1)}, bf16[2,128,256]{2,1,0:T(8,128)(2,1)S(1)}, u32[]{:S(2)}, u32[]{:S(2)}) collective-permute-start(bf16[2,128,256]{2,1,0:T(8,128)(2,1)S(1)} %pad_maximum_fusion.refs_19_), channel_id=1, source_target_pairs={{0,12},{1,13},{2,14},{3,15},{4,0},{5,1},{6,2},{7,3},{8,4},{9,5},{1... | collective-permute-start | bytes 393224 | tf_op jit(solution)/shard_map/ppermute | solution.py:327
  27.3 6.6 %collective-permute-start.21 = (bf16[2,128,256]{2,1,0:T(8,128)(2,1)S(1)}, bf16[2,128,256]{2,1,0:T(8,128)(2,1)S(1)}, u32[]{:S(2)}, u32[]{:S(2)}) collective-permute-start(bf16[2,128,256]{2,1,0:T(8,128)(2,1)S(1)} %pad_maximum_fusion.refs_19_), channel_id=1, source_target_pairs={{0,8},{1,9},{2,10},{3,11},{4,12},{5,13},{6,14},{7,15},{8,0},{9,1},... | collective-permute-start | bytes 393224 | tf_op jit(solution)/shard_map/ppermute | solution.py:327
  27.3 7.7 %collective-permute-start.23 = (bf16[2,128,256]{2,1,0:T(8,128)(2,1)S(1)}, bf16[2,128,256]{2,1,0:T(8,128)(2,1)S(1)}, u32[]{:S(2)}, u32[]{:S(2)}) collective-permute-start(bf16[2,128,256]{2,1,0:T(8,128)(2,1)S(1)} %pad_maximum_fusion.refs_19_), channel_id=1, source_target_pairs={{0,4},{1,5},{2,6},{3,7},{4,8},{5,9},{6,10},{7,11},{8,12},{9,13},{1... | collective-permute-start | bytes 393224 | tf_op jit(solution)/shard_map/ppermute | solution.py:327
  31.2 9.4 %collective-permute-start.8 = (bf16[128,1536]{1,0:T(8,128)(2,1)S(1)}, bf16[128,1536]{1,0:T(8,128)(2,1)S(1)}, u32[]{:S(2)}, u32[]{:S(2)}) collective-permute-start(bf16[128,1536]{1,0:T(8,128)(2,1)S(1)} %broadcast_select_fusion), channel_id=1, source_target_pairs={{0,4},{1,13},{2,6},{3,15},{4,8},{5,1},{6,10},{7,3},{8,12},{9,5},{1... | collective-permute-start | bytes 1179656 | tf_op jit(solution)/shard_map/ppermute | solution.py:327
  33.9 1.3 %collective-permute-start.18 = (bf16[2,128,256]{2,1,0:T(8,128)(2,1)S(1)}, bf16[2,128,256]{2,1,0:T(8,128)(2,1)S(1)}, u32[]{:S(2)}, u32[]{:S(2)}) collective-permute-start(bf16[2,128,256]{2,1,0:T(8,128)(2,1)S(1)} %pad_maximum_fusion.refs_19_), channel_id=1, source_target_pairs={{0,1},{1,0},{2,3},{3,2},{4,5},{5,4},{6,7},{7,6},{8,9},{9,8},{10,11... | collective-permute-start | bytes 393224 | tf_op jit(solution)/shard_map/ppermute | solution.py:327
  35.0 1.3 %collective-permute-start.20 = (bf16[2,128,256]{2,1,0:T(8,128)(2,1)S(1)}, bf16[2,128,256]{2,1,0:T(8,128)(2,1)S(1)}, u32[]{:S(2)}, u32[]{:S(2)}) collective-permute-start(bf16[2,128,256]{2,1,0:T(8,128)(2,1)S(1)} %collective-permute-done.19.refs_21_), channel_id=1, source_target_pairs={{0,1},{1,0},{2,3},{3,2},{4,5},{5,4},{6,7},{7,6},{8,9},{9,8},{10,11... | collective-permute-start | bytes 393224 | tf_op jit(solution)/shard_map/ppermute | solution.py:327
  35.2 1.3 %collective-permute-start.22 = (bf16[2,128,256]{2,1,0:T(8,128)(2,1)S(1)}, bf16[2,128,256]{2,1,0:T(8,128)(2,1)S(1)}, u32[]{:S(2)}, u32[]{:S(2)}) collective-permute-start(bf16[2,128,256]{2,1,0:T(8,128)(2,1)S(1)} %collective-permute-done.21.refs_23_), channel_id=1, source_target_pairs={{0,1},{1,0},{2,3},{3,2},{4,5},{5,4},{6,7},{7,6},{8,9},{9,8},{10,11... | collective-permute-start | bytes 393224 | tf_op jit(solution)/shard_map/ppermute | solution.py:327
  36.3 3.4 %collective-permute-start.24 = (bf16[2,128,256]{2,1,0:T(8,128)(2,1)S(1)}, bf16[2,128,256]{2,1,0:T(8,128)(2,1)S(1)}, u32[]{:S(2)}, u32[]{:S(2)}) collective-permute-start(bf16[2,128,256]{2,1,0:T(8,128)(2,1)S(1)} %collective-permute-done.23.refs_25_), channel_id=1, source_target_pairs={{0,1},{1,0},{2,3},{3,2},{4,5},{5,4},{6,7},{7,6},{8,9},{9,8},{10,11... | collective-permute-start | bytes 393224 | tf_op jit(solution)/shard_map/ppermute | solution.py:327
  36.5 12.8 %collective-permute-start.13 = (bf16[128,1536]{1,0:T(8,128)(2,1)}, bf16[128,1536]{1,0:T(8,128)(2,1)S(1)}, u32[]{:S(2)}, u32[]{:S(2)}) collective-permute-start(bf16[128,1536]{1,0:T(8,128)(2,1)} %collective-permute-done.1.refs_5_), channel_id=1, source_target_pairs={{0,4},{1,5},{2,6},{3,7},{4,8},{5,9},{6,10},{7,11},{8,12},{9,13},{1... | collective-permute-start | bytes 1179656 | tf_op jit(solution)/shard_map/ppermute | solution.py:327
  36.6 12.7 %collective-permute-start.5 = (bf16[128,1536]{1,0:T(8,128)(2,1)}, bf16[128,1536]{1,0:T(8,128)(2,1)S(1)}, u32[]{:S(2)}, u32[]{:S(2)}) collective-permute-start(bf16[128,1536]{1,0:T(8,128)(2,1)} %collective-permute-done.1.refs_5_), channel_id=1, source_target_pairs={{0,12},{1,13},{2,14},{3,15},{4,0},{5,1},{6,2},{7,3},{8,4},{9,5},{1... | collective-permute-start | bytes 1179656 | tf_op jit(solution)/shard_map/ppermute | solution.py:327
  39.7 10.1 %collective-permute-start.2 = (bf16[128,1536]{1,0:T(8,128)(2,1)}, bf16[128,1536]{1,0:T(8,128)(2,1)S(1)}, u32[]{:S(2)}, u32[]{:S(2)}) collective-permute-start(bf16[128,1536]{1,0:T(8,128)(2,1)} %collective-permute-done.1.refs_5_), channel_id=1, source_target_pairs={{0,1},{1,0},{2,3},{3,2},{4,5},{5,4},{6,7},{7,6},{8,9},{9,8},{10,11... | collective-permute-start | bytes 1179656 | tf_op jit(solution)/shard_map/ppermute | solution.py:327
  39.7 10.2 %collective-permute-start.12 = (bf16[128,1536]{1,0:T(8,128)(2,1)}, bf16[128,1536]{1,0:T(8,128)(2,1)S(1)}, u32[]{:S(2)}, u32[]{:S(2)}) collective-permute-start(bf16[128,1536]{1,0:T(8,128)(2,1)} %collective-permute-done.7.refs_15_), channel_id=1, source_target_pairs={{0,1},{1,0},{2,3},{3,2},{4,5},{5,4},{6,7},{7,6},{8,9},{9,8},{10,11... | collective-permute-start | bytes 1179656 | tf_op jit(solution)/shard_map/ppermute | solution.py:327
  40.6 12.6 %collective-permute-start.10 = (bf16[128,1536]{1,0:T(8,128)(2,1)S(1)}, bf16[128,1536]{1,0:T(8,128)(2,1)S(1)}, u32[]{:S(2)}, u32[]{:S(2)}) collective-permute-start(bf16[128,1536]{1,0:T(8,128)(2,1)S(1)} %collective-permute-done.8.refs_11_), channel_id=1, source_target_pairs={{0,2},{1,3},{2,0},{3,1},{4,6},{5,7},{6,4},{7,5},{8,10},{9,11},{10,... | collective-permute-start | bytes 1179656 | tf_op jit(solution)/shard_map/ppermute | solution.py:327
  49.3 9.4 %collective-permute-start.4 = (bf16[128,1536]{1,0:T(8,128)(2,1)S(1)}, bf16[128,1536]{1,0:T(8,128)(2,1)S(1)}, u32[]{:S(2)}, u32[]{:S(2)}) collective-permute-start(bf16[128,1536]{1,0:T(8,128)(2,1)S(1)} %collective-permute-done.3.refs_7_), channel_id=1, source_target_pairs={{0,1},{1,0},{2,3},{3,2},{4,5},{5,4},{6,7},{7,6},{8,9},{9,8},{10,11... | collective-permute-start | bytes 1179656 | tf_op jit(solution)/shard_map/ppermute | solution.py:327
  49.3 9.4 %collective-permute-start.9 = (bf16[128,1536]{1,0:T(8,128)(2,1)S(1)}, bf16[128,1536]{1,0:T(8,128)(2,1)S(1)}, u32[]{:S(2)}, u32[]{:S(2)}) collective-permute-start(bf16[128,1536]{1,0:T(8,128)(2,1)S(1)} %collective-permute-done.8.refs_11_), channel_id=1, source_target_pairs={{0,1},{1,0},{2,3},{3,2},{4,5},{5,4},{6,7},{7,6},{8,9},{9,8},{10,11... | collective-permute-start | bytes 1179656 | tf_op jit(solution)/shard_map/ppermute | solution.py:327
  49.8 8.9 %collective-permute-start.14 = (bf16[128,1536]{1,0:T(8,128)(2,1)S(1)}, bf16[128,1536]{1,0:T(8,128)(2,1)S(1)}, u32[]{:S(2)}, u32[]{:S(2)}) collective-permute-start(bf16[128,1536]{1,0:T(8,128)(2,1)S(1)} %collective-permute-done.13.refs_17_), channel_id=1, source_target_pairs={{0,1},{1,0},{2,3},{3,2},{4,5},{5,4},{6,7},{7,6},{8,9},{9,8},{10,11... | collective-permute-start | bytes 1179656 | tf_op jit(solution)/shard_map/ppermute | solution.py:327
  49.9 8.8 %collective-permute-start.6 = (bf16[128,1536]{1,0:T(8,128)(2,1)S(1)}, bf16[128,1536]{1,0:T(8,128)(2,1)S(1)}, u32[]{:S(2)}, u32[]{:S(2)}) collective-permute-start(bf16[128,1536]{1,0:T(8,128)(2,1)S(1)} %collective-permute-done.5.refs_9_), channel_id=1, source_target_pairs={{0,1},{1,0},{2,3},{3,2},{4,5},{5,4},{6,7},{7,6},{8,9},{9,8},{10,11... | collective-permute-start | bytes 1179656 | tf_op jit(solution)/shard_map/ppermute | solution.py:327
  53.3 5.4 %collective-permute-start.11 = (bf16[128,1536]{1,0:T(8,128)(2,1)S(1)}, bf16[128,1536]{1,0:T(8,128)(2,1)S(1)}, u32[]{:S(2)}, u32[]{:S(2)}) collective-permute-start(bf16[128,1536]{1,0:T(8,128)(2,1)S(1)} %collective-permute-done.10.refs_13_), channel_id=1, source_target_pairs={{0,1},{1,0},{2,3},{3,2},{4,5},{5,4},{6,7},{7,6},{8,9},{9,8},{10,11... | collective-permute-start | bytes 1179656 | tf_op jit(solution)/shard_map/ppermute | solution.py:327
  64.4 7.0 %collective-permute-start.25 = (f32[2,768]{1,0:T(2,128)S(1)}, f32[2,768]{1,0:T(2,128)S(1)}, u32[]{:S(2)}, u32[]{:S(2)}) collective-permute-start(f32[2,768]{1,0:T(2,128)S(1)} %slice.11), channel_id=1, source_target_pairs={{1,0},{2,1},{3,2},{4,3},{5,4},{6,5},{7,6},{8,7},{9,8},{10,9},{11,1... | collective-permute-start | bytes 18440 | tf_op jit(solution)/shard_map/ppermute | solution.py:379
  71.4 3.8 %collective-permute-start.26 = (f32[4,1024]{1,0:T(4,128)S(1)}, f32[4,1024]{1,0:T(4,128)S(1)}, u32[]{:S(2)}, u32[]{:S(2)}) collective-permute-start(f32[4,1024]{1,0:T(4,128)S(1)} %shard_map.56), channel_id=1, source_target_pairs={{0,16},{16,0},{32,48},{48,32},{64,80},{80,64},{96,112},{112,96},{1... | collective-permute-start | bytes 49160 | tf_op jit(solution)/shard_map/ppermute | solution.py:327
  75.2 4.9 %collective-permute-start.27 = (f32[4,1024]{1,0:T(4,128)S(1)}, f32[4,1024]{1,0:T(4,128)S(1)}, u32[]{:S(2)}, u32[]{:S(2)}) collective-permute-start(f32[4,1024]{1,0:T(4,128)S(1)} %add.24), channel_id=1, source_target_pairs={{0,48},{16,32},{32,16},{48,0},{64,112},{80,96},{96,80},{112,64},{1... | collective-permute-start | bytes 49160 | tf_op jit(solution)/shard_map/ppermute | solution.py:327
  80.1 3.7 %collective-permute-start.28 = (f32[4,1024]{1,0:T(4,128)S(1)}, f32[4,1024]{1,0:T(4,128)S(1)}, u32[]{:S(2)}, u32[]{:S(2)}) collective-permute-start(f32[4,1024]{1,0:T(4,128)S(1)} %add.25.stats_ref), channel_id=1, source_target_pairs={{0,64},{16,80},{32,96},{48,112},{64,0},{80,16},{96,32},{112,48},{1... | collective-permute-start | bytes 49160 | tf_op jit(solution)/shard_map/ppermute | solution.py:327
  85.8 6.6 %collective-permute-start.30 = (f32[8,128]{1,0:T(8,128)S(1)}, f32[8,128]{1,0:T(8,128)S(1)}, u32[]{:S(2)}, u32[]{:S(2)}) collective-permute-start(f32[8,128]{1,0:T(8,128)S(1)} %add.26), channel_id=1, source_target_pairs={{0,2},{1,3},{2,0},{3,1},{4,6},{5,7},{6,4},{7,5},{8,10},{9,11},{10,... | collective-permute-start | bytes 12296 | tf_op jit(solution)/shard_map/ppermute | solution.py:327
  92.3 5.5 %collective-permute-start.31 = (f32[8,128]{1,0:T(8,128)S(1)}, f32[8,128]{1,0:T(8,128)S(1)}, u32[]{:S(2)}, u32[]{:S(2)}) collective-permute-start(f32[8,128]{1,0:T(8,128)S(1)} %add.28), channel_id=1, source_target_pairs={{0,4},{1,5},{2,6},{3,7},{4,0},{5,1},{6,2},{7,3},{8,12},{9,13},{10,... | collective-permute-start | bytes 12296 | tf_op jit(solution)/shard_map/ppermute | solution.py:327
  97.9 4.8 %collective-permute-start.32 = (f32[8,128]{1,0:T(8,128)S(1)}, f32[8,128]{1,0:T(8,128)S(1)}, u32[]{:S(2)}, u32[]{:S(2)}) collective-permute-start(f32[8,128]{1,0:T(8,128)S(1)} %add.30), channel_id=1, source_target_pairs={{0,12},{1,13},{2,14},{3,15},{4,8},{5,9},{6,10},{7,11},{8,4},{9,5},... | collective-permute-start | bytes 12296 | tf_op jit(solution)/shard_map/ppermute | solution.py:327
  (7 other events, 229.9 us)
